TPU v7x, 128 devices: a whole 4x4x4 slice. The times are simulated.
128 devices in a mesh: store: 16 (over y, x), req: 4 (over z), tp: 2 (over core).
Axes of the slice: x: 4, y: 4, z: 4, core: 2. Of those that a mesh axis runs over, the one named last changes fastest.
Arguments:
- span_keys: bfloat16 [512, 256, 1024], P('req', 'store', 'tp'), may hold values from -5 to 5
- span_values: bfloat16 [512, 256, 1024], P('req', 'store', 'tp'), may hold values from -5 to 5
- span_row: int32 [512], replicated, may hold values from 0 to 511, as said below
- span_lists: int32 [64, 8], P(('store', 'req')), may hold values from 0 to 511, as said below
- recompute_pos: int32 [64, 128], P(('store', 'req')), may hold values from 0 to 2047, as said below
- fresh_q: bfloat16 [64, 128, 8192], P(('store', 'req'), None, 'tp'), may hold values from -5 to 5
- fresh_k: bfloat16 [64, 128, 1024], P(('store', 'req'), None, 'tp'), may hold values from -5 to 5
- fresh_v: bfloat16 [64, 128, 1024], P(('store', 'req'), None, 'tp'), may hold values from -5 to 5
Outputs:
- attended: bfloat16 [64, 128, 8192], P(('store', 'req'), None, 'tp')
- span_drift: float32 [512], P(('store', 'req', 'tp'))
Inputs may be any that keep to these rules, and one draw needn't show every extreme that they name: `span_row`: each span sits in exactly one table row; rows k*128 .. (k+1)*128 - 1 form block k. `span_lists`: A request's 8 spans are distinct; at most 4 of them lie in one block of table rows, and in every draw some request has exactly 4 in one block. `recompute_pos`: entries k*16 .. (k+1)*16 - 1 of a row are distinct ascending positions within k*256 .. (k+1)*256 - 1.
All inputs are finite; a program needn't handle non-finite values.
Results may differ from a plain program's by a relative error of at most 0.0064.
Values may be sent and summed in bfloat16 or wider, within the bound.
No kernel may reach another device: no remote copies, remote signals or barrier semaphores. Data moves between devices by JAX's collectives and lax.ppermute only.
A program may use at most 128 MiB of HBM per device.

v0:
```python
import jax
import jax.numpy as jnp
from jax import lax
from jax.sharding import PartitionSpec as P

KVH = 8
HD = 128
CPR = 8
CAP = 4


def rotate(values, places):
    half = HD // 2
    freq = jnp.exp(-jnp.log(500000.0) * jnp.arange(half, dtype=jnp.float32) / half)
    angles = places.astype(jnp.float32)[:, None] * freq[None, :]
    cosine = jnp.cos(angles)[:, None, :]
    sine = jnp.sin(angles)[:, None, :]
    first = values[..., :half]
    second = values[..., half:]
    return jnp.concatenate(
        [first * cosine - second * sine, second * cosine + first * sine], axis=-1
    )


def locate(listed, span_row, shard_rows):
    table_rows = span_row[listed]
    shard_home = table_rows // shard_rows
    slot_local = table_rows % shard_rows
    count = listed.shape[-1]
    earlier = jnp.arange(count)[:, None] < jnp.arange(count)[None, :]
    same = shard_home[:, :, None] == shard_home[:, None, :]
    order_rank = jnp.sum(same & earlier[None], axis=1)
    return (shard_home, slot_local, order_rank)


def local(span_keys, span_values, span_row, span_lists, recompute_pos, fresh_q, fresh_k, fresh_v):
    n_store = lax.axis_size("store")
    n_req = lax.axis_size("req")
    shard_rows, tok_dev, width = span_keys.shape
    heads_kv = width // HD
    every_list = lax.all_gather(span_lists, ("store", "req"), axis=0, tiled=True)
    shard_home, slot_local, order_rank = locate(every_list, span_row, shard_rows)
    slot_ids = jnp.arange(CAP, dtype=jnp.int32)
    selected = (shard_home == lax.axis_index("req"))[:, None, :] & (
        order_rank[:, None, :] == slot_ids[None, :, None]
    )
    chosen = jnp.sum(jnp.where(selected, slot_local[:, None, :], 0), axis=2).T
    filled = jnp.any(selected, axis=2).T[:, :, None, None]
    send_keys = jnp.where(filled, jnp.take(span_keys, chosen, axis=0), jnp.zeros((), jnp.bfloat16))
    send_values = jnp.where(
        filled, jnp.take(span_values, chosen, axis=0), jnp.zeros((), jnp.bfloat16)
    )
    grid_shape = (CAP, n_store, n_req, tok_dev, width)
    got_keys, got_values = (
        lax.all_to_all(send_keys, ("store", "req"), split_axis=1, concat_axis=1, tiled=True),
        lax.all_to_all(send_values, ("store", "req"), split_axis=1, concat_axis=1, tiled=True),
    )
    got_keys = got_keys.reshape(grid_shape)
    got_values = got_values.reshape(grid_shape)
    own_home, own_local, own_rank = locate(span_lists, span_row, shard_rows)
    own_home = own_home[0]
    own_rank = own_rank[0]
    context = CPR * n_store * tok_dev
    keys_raw = got_keys[own_rank, :, own_home].reshape(context, width)
    values_raw = got_values[own_rank, :, own_home].reshape(context, width)
    places = recompute_pos[0]
    row_count = places.shape[0]
    positions = jnp.arange(context, dtype=jnp.int32)
    keys_rot = (
        rotate(keys_raw.astype(jnp.float32).reshape(context, heads_kv, HD), positions)
        .astype(jnp.bfloat16)
        .reshape(context, width)
    )
    new_keys = (
        rotate(fresh_k[0].astype(jnp.float32).reshape(row_count, heads_kv, HD), places)
        .astype(jnp.bfloat16)
        .reshape(row_count, width)
    )
    keys_all = keys_rot.at[places].set(new_keys)
    values_all = values_raw.at[places].set(fresh_v[0])
    heads_q = fresh_q.shape[2] // HD
    group_size = heads_q // heads_kv
    queries = rotate(fresh_q[0].astype(jnp.float32).reshape(row_count, heads_q, HD), places).astype(
        jnp.bfloat16
    )
    queries = queries.reshape(row_count, heads_kv, 2, group_size // 2, HD).transpose(1, 2, 3, 0, 4)
    key_heads = keys_all.reshape(context, heads_kv, HD).transpose(1, 0, 2)
    value_heads = values_all.reshape(context, heads_kv, HD).transpose(1, 0, 2)
    visible = positions[None, :] <= places[:, None]
    scale = HD ** (-0.5)

    def attend(members):
        query_pair, key_block, value_block = members
        results = []
        for half_index in range(2):
            scores = (
                jnp.einsum(
                    "hqd,kd->hqk",
                    query_pair[half_index],
                    key_block,
                    preferred_element_type=jnp.float32,
                )
                * scale
            )
            scores = jnp.where(visible[None], scores, -1e30)
            row_max = jnp.max(scores, axis=-1, keepdims=True)
            weights = jnp.exp(scores - row_max)
            probabilities = (weights / jnp.sum(weights, axis=-1, keepdims=True)).astype(
                jnp.bfloat16
            )
            results.append(
                jnp.einsum(
                    "hqk,kd->hqd", probabilities, value_block, preferred_element_type=jnp.float32
                ).astype(jnp.bfloat16)
            )
        return jnp.stack(results)

    combined = lax.map(attend, (queries, key_heads, value_heads))
    attended = combined.transpose(3, 0, 1, 2, 4).reshape(1, row_count, heads_q * HD)
    cached_k = keys_raw[places].astype(jnp.float32)
    cached_v = values_raw[places].astype(jnp.float32)
    deviation = jnp.sum(
        (fresh_k[0].astype(jnp.float32) - cached_k) ** 2
        + (fresh_v[0].astype(jnp.float32) - cached_v) ** 2,
        axis=1,
    ) / (2.0 * KVH * HD)
    span_share = jnp.mean(deviation.reshape(CPR, row_count // CPR), axis=1)
    total_spans = span_row.shape[0]
    onehot = (span_lists[0][:, None] == jnp.arange(total_spans, dtype=jnp.int32)[None, :]).astype(
        jnp.float32
    )
    contribution = jnp.sum(onehot * span_share[:, None], axis=0)
    drift_part = lax.psum_scatter(
        contribution, ("store", "req", "tp"), scatter_dimension=0, tiled=True
    )
    return (attended, drift_part)


def solution(mesh):
    in_specs = (
        P("req", "store", "tp"),
        P("req", "store", "tp"),
        P(),
        P(("store", "req"), None),
        P(("store", "req"), None),
        P(("store", "req"), None, "tp"),
        P(("store", "req"), None, "tp"),
        P(("store", "req"), None, "tp"),
    )
    out_specs = (P(("store", "req"), None, "tp"), P(("store", "req", "tp")))
    return jax.shard_map(local, mesh=mesh, in_specs=in_specs, out_specs=out_specs, check_vma=False)
```

profile of v0, /device:TPU:1, one launch (start us, length us, event | category | flops | bytes accessed | tf_op | source)
XLA Modules:
  0.0 431.3 jit_solution(8575588712627836426)
XLA Ops:
  0.7 150.1 %all-gather = s32[64,1,8]{2,1,0:T(1,128)S(1)} all-gather(s32[1,1,8]{2,1,0:T(1,128)} %bitcast.188), channel_id=1, replica_groups=mesh['store'=16,'req'=4,'tp'=2] {'store','req'}, dimensions={0}, use_global_device_ids=true | all-gather | bytes 2080 | tf_op jit(solution)/shard_map/all_gather | solution.py:41
  151.1 3.5 gather_fusion
  157.8 4.4 %gather_fusion.6 = bf16[256,16,512]{2,1,0:T(8,128)(2,1)} fusion(bf16[128,16,512]{2,1,0:T(8,128)(2,1)} %param.12, s32[1024]{0:T(1024)S(1)} %pad_clamp_fusion.2), kind=kCustom, calls=%fused_computation.clone | custom fusion | bytes 8389632 | tf_op jit(solution)/shard_map/jit(_take)/gather | solution.py:49
  162.1 5.4 %select_select_fusion = (bf16[4,64,16,512]{3,2,1,0:T(8,128)(2,1)}, bf16[4,64,16,512]{3,2,1,0:T(8,128)(2,1)S(1)}) fusion(bf16[4,64,16,512]{3,2,1,0:T(8,128)(2,1)} %bitcast.175, pred[4,64]{1,0:T(4,128)(4,1)S(1)} %compare_and_fusion, pred[4,64]{1,0:T(4,128)(4,1)S(1)} %bitcast.190, bf16[4,64,16,512]{3,2,1,0:T(8,128)(2,1)} %bitcast.176), kind=kLoop, calls=%fused_computation.70 | loop fusion | flops 8388608 | bytes 16777728 | tf_op jit(solution)/shard_map/jit(_where)/select_n | solution.py:50
  170.0 5.8 %all-to-all-start = ((bf16[4,64,16,512]{3,2,0,1:T(8,128)(2,1)}), bf16[4,64,16,512]{3,2,0,1:T(8,128)(2,1)}, u32[]{:S(2)}, u32[]{:S(2)}) async-start(bf16[4,64,16,512]{3,2,0,1:T(8,128)(2,1)} %copy.62), calls=%async_computation | async-start | bytes 8388608 | tf_op jit(solution)/shard_map/all_to_all | solution.py:55
  176.6 4.8 %copy.64 = bf16[4,64,16,512]{3,2,0,1:T(8,128)(2,1)} copy(bf16[4,64,16,512]{3,2,1,0:T(8,128)(2,1)} %get-tuple-element.111) | data formatting | bytes 8388608 | tf_op jit(solution)/shard_map/jit(_where)/select_n | solution.py:50
  182.1 23.0 %all-to-all-done = bf16[4,64,16,512]{3,2,0,1:T(8,128)(2,1)} async-done(((bf16[4,64,16,512]{3,2,0,1:T(8,128)(2,1)}), bf16[4,64,16,512]{3,2,0,1:T(8,128)(2,1)}, u32[]{:S(2)}, u32[]{:S(2)}) %all-to-all-start) | async-done | bytes 4194336 | tf_op jit(solution)/shard_map/all_to_all | solution.py:55
  205.0 7.1 %all-to-all-start.1 = ((bf16[4,64,16,512]{3,2,0,1:T(8,128)(2,1)}), bf16[4,64,16,512]{3,2,0,1:T(8,128)(2,1)}, u32[]{:S(2)}, u32[]{:S(2)}) async-start(bf16[4,64,16,512]{3,2,0,1:T(8,128)(2,1)} %copy.64), calls=%async_computation.1 | async-start | bytes 8388608 | tf_op jit(solution)/shard_map/all_to_all | solution.py:56
  217.8 5.3 %multiply_cosine_fusion = (f32[2048,64]{1,0:T(8,128)S(1)}, f32[2048,64]{1,0:T(8,128)}) fusion(f32[64]{0:T(128)S(1)} %multiply_exponential_fusion, f32[2048]{0:T(1024)S(1)} %iota_convert_fusion), kind=kLoop, calls=%fused_computation.81 | loop fusion | flops 131072 | bytes 1057024 | tf_op jit(solution)/shard_map/cos | solution.py:16
  223.1 2.9 gather_fusion.2
  226.0 3.3 reshape.526
  229.4 6.4 %subtract_convert_fusion = (bf16[2048,4,64]{2,1,0:T(4,128)(2,1)S(1)}, bf16[2048,4,64]{2,1,0:T(4,128)(2,1)S(1)}) fusion(f32[2048,4,128]{2,1,0:T(4,128)} %reshape.526, f32[2048,64]{1,0:T(8,128)} %get-tuple-element.110, f32[2048,64]{1,0:T(8,128)S(1)} %get-tuple-element.109), kind=kLoop, calls=%fused_computation.73 | loop fusion | flops 4194304 | bytes 7340032 | tf_op jit(solution)/shard_map/convert.6
  235.8 2.9 pad_maximum_fusion
  243.9 13.9 %all-to-all-done.1 = bf16[4,64,16,512]{3,2,0,1:T(8,128)(2,1)} async-done(((bf16[4,64,16,512]{3,2,0,1:T(8,128)(2,1)}), bf16[4,64,16,512]{3,2,0,1:T(8,128)(2,1)}, u32[]{:S(2)}, u32[]{:S(2)}) %all-to-all-start.1) | async-done | bytes 4194336 | tf_op jit(solution)/shard_map/all_to_all | solution.py:56
  257.7 2.9 gather_fusion.3
  265.7 56.1 %while.11 = (s32[]{:T(128)}, bf16[4,2,4,128,128]{4,3,2,1,0:T(8,128)(2,1)}, bf16[4,2,4,128,128]{4,3,2,1,0:T(8,128)(2,1)S(1)}, bf16[4,2048,128]{1,2,0:T(8,128)(2,1...) while((s32[]{:T(128)}, ...), condition=%wide.region_11.13_spmd.clone, body=%wide.region_6.12_spmd.clone.sunk | while | flops 1630413824 | bytes 5781617 | solution.py:118
  265.9 2.8 fusion.127
  268.7 3.8 fusion.128
  272.4 2.8 fusion.125
  275.2 3.8 fusion.126
  279.9 2.8 fusion.127
  282.7 3.8 fusion.128
  286.5 2.8 fusion.125
  289.2 3.8 fusion.126
  294.0 2.8 fusion.127
  296.7 3.8 fusion.128
  300.5 2.8 fusion.125
  303.3 3.8 fusion.126
  308.0 2.8 fusion.127
  310.8 3.8 fusion.128
  317.3 3.8 fusion.126
  328.8 101.9 %all-reduce = f32[512]{0:T(512)S(1)} all-reduce(f32[512]{0:T(512)S(1)} %select_reduce_fusion), channel_id=2, replica_groups=mesh['store'=16,'req'=4,'tp'=2] {'store','req','tp'}, use_global_device_ids=true, to_apply=%region_15.17.clone | all-reduce | flops 512 | bytes 4096
  (85 shorter events, 37.1 us)
Async XLA Ops:
  0.6 154.4 %copy-start = (bf16[128,16,512]{2,1,0:T(8,128)(2,1)S(1)}, bf16[128,16,512]{2,1,0:T(8,128)(2,1)}, u32[]{:S(2)}) copy-start(bf16[128,16,512]{2,1,0:T(8,128)(2,1)} %param.13) | copy-start | bytes 6291460
  0.6 150.4 %copy-start.2 = (s32[512]{0:T(512)S(1)}, s32[512]{0:T(512)}, u32[]{:S(2)}) copy-start(s32[512]{0:T(512)} %param.14) | copy-start | bytes 6148
  170.0 5.8 %copy-start.9 = (s32[1,8]{1,0:T(1,128)S(1)}, s32[1,8]{1,0:T(1,128)}, u32[]{:S(2)}) copy-start(s32[1,8]{1,0:T(1,128)} %param.15) | copy-start | bytes 100
  170.0 6.5 %copy-start.6 = (bf16[1,128,512]{2,1,0:T(8,128)(2,1)S(1)}, bf16[1,128,512]{2,1,0:T(8,128)(2,1)}, u32[]{:S(2)}) copy-start(bf16[1,128,512]{2,1,0:T(8,128)(2,1)} %param.18) | copy-start | bytes 393220
  170.0 35.1 %all-to-all-start = ((bf16[4,64,16,512]{3,2,0,1:T(8,128)(2,1)}), bf16[4,64,16,512]{3,2,0,1:T(8,128)(2,1)}, u32[]{:S(2)}, u32[]{:S(2)}) async-start(bf16[4,64,16,512]{3,2,0,1:T(8,128)(2,1)} %copy.62), calls=%async_computation | async-start | bytes 8388608 | tf_op jit(solution)/shard_map/all_to_all | solution.py:55
  176.6 4.9 %copy-start.4 = (bf16[1,128,4096]{2,1,0:T(8,128)(2,1)S(1)}, bf16[1,128,4096]{2,1,0:T(8,128)(2,1)}, u32[]{:S(2)}) copy-start(bf16[1,128,4096]{2,1,0:T(8,128)(2,1)} %param.17) | copy-start | bytes 3145732
  182.0 30.1 %copy-start.8 = (s32[1,128]{1,0:T(1,128)S(1)}, s32[1,128]{1,0:T(1,128)}, u32[]{:S(2)}) copy-start(s32[1,128]{1,0:T(1,128)} %param.16) | copy-start | bytes 1540
  205.0 52.7 %all-to-all-start.1 = ((bf16[4,64,16,512]{3,2,0,1:T(8,128)(2,1)}), bf16[4,64,16,512]{3,2,0,1:T(8,128)(2,1)}, u32[]{:S(2)}, u32[]{:S(2)}) async-start(bf16[4,64,16,512]{3,2,0,1:T(8,128)(2,1)} %copy.64), calls=%async_computation.1 | async-start | bytes 8388608 | tf_op jit(solution)/shard_map/all_to_all | solution.py:56
  226.0 3.3 copy-start.3
  257.7 3.8 copy-start.7
  264.0 1.7 copy-start.5
  321.8 109.5 %copy-start.1 = (bf16[128,16,512]{2,1,0:T(8,128)(2,1)S(1)}, bf16[128,16,512]{2,1,0:T(8,128)(2,1)}, u32[]{:S(2)}) copy-start(bf16[128,16,512]{2,1,0:T(8,128)(2,1)} %param.13) | copy-start | bytes 6291460
where the time goes:
time: 432 us; the launch traced here: 431 us
  blocking collectives  252 us (58%)
  matrix products  52.3 us (12%)
  local copies, waits for them, and re-layouts  46.7 us (11%)
  waiting for transfers between devices  36.8 us (9%)
  other arithmetic  29.5 us (7%)
  starting transfers between devices  12.9 us (3%)
    all_gather x1, blocking collectives, local(): lax.all_gather(span_lists, ('store', 'req'), axis=0, tiled=True)  150 us
    unnamed x1, blocking collectives  102 us
    dot_general x8, matrix products, attend(): jnp.einsum('hqk,kd->hqd', probabilities, value_block, preferred_element_t...  30.2 us
    all_to_all x1, waiting for transfers between devices, local(): lax.all_to_all(send_keys, ('store', 'req'), split_axis=1, concat_axis=1,...  23 us
    sub x8, matrix products, attend(): weights = jnp.exp(scores - row_max)  22.1 us
    all_to_all x1, waiting for transfers between devices, local(): lax.all_to_all(send_values, ('store', 'req'), split_axis=1, concat_axis=1...  13.9 us
    another operation x3, other arithmetic  9.17 us
  transfers between devices with their start and end apart: 2, of which 2 were waited for; matrix products, arithmetic and copies ran while one was open for 9% of the time, Pallas kernels for 0%

commit v1 on v0

v1 whole, which is shorter than its diff:
```python
import functools

import jax
import jax.numpy as jnp
import numpy as np
from jax import lax
from jax.experimental import pallas as pl
from jax.experimental.pallas import tpu as pltpu
from jax.sharding import PartitionSpec as P

HD = 128
HALF = HD // 2
CPR = 8
RPC = 16
CL = 256
CTX = CPR * CL
RC = CPR * RPC
KVH = 8
CAP = 4
LANES = 128
SCALE_LOG2E = float(HD ** -0.5 * np.log2(np.e))

FREQ = np.exp(-np.log(500000.0) * np.arange(HALF) / HALF).astype(np.float32)


def context_tables():
    angles = (np.arange(CTX, dtype=np.float32)[:, None] * FREQ[None, :]).astype(np.float64)
    cosine = np.cos(angles).astype(np.float32)
    sine = np.sin(angles).astype(np.float32)
    return (
        np.concatenate([cosine, cosine], axis=1),
        np.concatenate([-sine, sine], axis=1),
    )


COS_CTX, SIN_CTX = context_tables()


def turn(x, cosine, sine):
    return x * cosine + pltpu.roll(x, HALF, 1) * sine


def span_homes(span_row, span_lists, shard_rows):
    rows = [span_row[span_lists[0, j]] for j in range(CPR)]
    homes = [row // shard_rows for row in rows]
    slots = [row % shard_rows for row in rows]
    ranks = []
    for j in range(CPR):
        rank = jnp.int32(0)
        for i in range(j):
            rank = rank + jnp.where(homes[i] == homes[j], 1, 0)
        ranks.append(rank)
    return homes, slots, ranks


def ask_kernel(shard_rows, blocks, span_row, span_lists, out):
    homes, slots, ranks = span_homes(span_row, span_lists, shard_rows)
    block = lax.broadcasted_iota(jnp.int32, out.shape, 0) % blocks
    lane = lax.broadcasted_iota(jnp.int32, out.shape, 1)
    total = jnp.zeros(out.shape, jnp.int32)
    for j in range(CPR):
        total = jnp.where((block == homes[j]) & (lane == ranks[j]), slots[j], total)
    out[...] = total


def pick_kernel(wanted, keys, values, send, sem):
    def body(r, carry):
        for t in range(CAP):
            row = wanted[r, t]
            pltpu.make_async_copy(keys.at[row], send.at[r, t, 0], sem).start()
            pltpu.make_async_copy(values.at[row], send.at[r, t, 1], sem).start()
        return carry

    lax.fori_loop(0, send.shape[0], body, 0)
    pltpu.make_async_copy(send, send, sem).wait()


def fresh_kernel(heads_kv, group, q, k, cosine, sine, q_out, k_out):
    cos = cosine[...]
    sin = sine[...]
    for h in range(heads_kv):
        cols = slice(h * HD, (h + 1) * HD)
        k_out[:, cols] = turn(k[:, cols].astype(jnp.float32), cos, sin).astype(jnp.bfloat16)
        for g in range(group):
            n = h * group + g
            turned = turn(q[:, n * HD : (n + 1) * HD].astype(jnp.float32), cos, sin)
            turned = turned.astype(jnp.bfloat16)
            for j in range(CPR):
                q_out[h * CPR + j, g * RPC : (g + 1) * RPC, :] = turned[j * RPC : (j + 1) * RPC]


def fetch(got, homes, ranks, which, buf, sems):
    copies = []
    for j in range(CPR):
        copies.append(
            pltpu.make_async_copy(got.at[:, homes[j], ranks[j], which], buf.at[j], sems.at[which, j])
        )
    return copies


def drift_kernel(
    shard_rows, span_row, span_lists, places, fresh_k, fresh_v, got, out, kbuf, vbuf, sems
):
    homes, _, ranks = span_homes(span_row, span_lists, shard_rows)
    width = fresh_k.shape[1]
    key_copies = fetch(got, homes, ranks, 0, kbuf, sems)
    value_copies = fetch(got, homes, ranks, 1, vbuf, sems)
    for j in range(CPR):
        key_copies[j].start()
        value_copies[j].start()
    dest = lax.broadcasted_iota(jnp.int32, out.shape, 0)
    lane = lax.broadcasted_iota(jnp.int32, out.shape, 1)
    per_dest = (span_row.shape[0]) // out.shape[0]
    total = jnp.zeros(out.shape, jnp.float32)
    token = lax.broadcasted_iota(jnp.int32, (RPC, CL), 1)
    for j in range(CPR):
        rows = slice(j * RPC, (j + 1) * RPC)
        pick = (token + j * CL == places[rows, :]).astype(jnp.float32).astype(jnp.bfloat16)
        gap = jnp.zeros((RPC, width), jnp.float32)
        for copy, buf, fresh in (
            (key_copies[j], kbuf, fresh_k),
            (value_copies[j], vbuf, fresh_v),
        ):
            copy.wait()
            cached = jnp.dot(
                pick, buf[j].reshape(CL, width), preferred_element_type=jnp.float32
            )
            delta = fresh[rows, :].astype(jnp.float32) - cached
            gap = gap + delta * delta
        share = jnp.sum(gap) * (1.0 / (2.0 * KVH * HD * RPC))
        span = span_lists[0, j]
        total = total + jnp.where(
            (dest == span // per_dest) & (lane == span % per_dest), share, 0.0
        )
    out[...] = total


def attend_kernel(
    shard_rows,
    heads_kv,
    group,
    span_row,
    span_lists,
    places_row,
    places_col,
    q,
    new_k,
    new_v,
    cosine,
    sine,
    got,
    out,
    kbuf,
    vbuf,
    keys,
    vals,
    seen,
    sems,
):
    homes, _, ranks = span_homes(span_row, span_lists, shard_rows)
    key_copies = fetch(got, homes, ranks, 0, kbuf, sems)
    value_copies = fetch(got, homes, ranks, 1, vbuf, sems)
    for j in range(CPR):
        key_copies[j].start()
        value_copies[j].start()
    token_row = lax.broadcasted_iota(jnp.int32, (CL, RPC), 0)
    token_lane = lax.broadcasted_iota(jnp.int32, (RPC, CL), 1)
    ones = jnp.ones((RPC, HD), jnp.bfloat16)
    for j in range(CPR):
        rows = slice(j * RPC, (j + 1) * RPC)
        span = slice(j * CL, (j + 1) * CL)
        seen[j] = jnp.where(token_lane + j * CL <= places_col[rows, :], 0.0, -1e30)
        put = (token_row + j * CL == places_row[j : j + 1, :]).astype(jnp.float32)
        put = put.astype(jnp.bfloat16)
        replaced = jnp.dot(put, ones, preferred_element_type=jnp.float32) > 0.5
        cos = cosine[span, :]
        sin = sine[span, :]
        key_copies[j].wait()
        value_copies[j].wait()
        for h in range(heads_kv):
            cols = slice(h * HD, (h + 1) * HD)
            raw = kbuf[j, :, :, cols].reshape(CL, HD).astype(jnp.float32)
            fresh = jnp.dot(put, new_k[rows, cols], preferred_element_type=jnp.float32)
            keys[h, span, :] = jnp.where(replaced, fresh, turn(raw, cos, sin)).astype(jnp.bfloat16)
            raw = vbuf[j, :, :, cols].reshape(CL, HD).astype(jnp.float32)
            fresh = jnp.dot(put, new_v[rows, cols], preferred_element_type=jnp.float32)
            vals[h, span, :] = jnp.where(replaced, fresh, raw).astype(jnp.bfloat16)

    def head(h, carry):
        for j in range(CPR):
            extent = (j + 1) * CL
            scores = lax.dot_general(
                q[h * CPR + j],
                keys[h, :extent, :],
                (((1,), (1,)), ((), ())),
                preferred_element_type=jnp.float32,
            )
            bias = jnp.concatenate([seen[j]] * group, axis=0)
            last = scores[:, j * CL :] + bias
            scores = last if j == 0 else jnp.concatenate([scores[:, : j * CL], last], axis=1)
            row_max = jnp.max(scores, axis=1, keepdims=True)
            weights = jnp.exp2((scores - row_max) * SCALE_LOG2E)
            row_sum = jnp.sum(weights, axis=1, keepdims=True)
            mixed = jnp.dot(
                weights.astype(jnp.bfloat16),
                vals[h, :extent, :],
                preferred_element_type=jnp.float32,
            )
            mixed = (mixed / row_sum).astype(jnp.bfloat16)
            for g in range(group):
                start = pl.multiple_of((h * group + g) * HD, HD)
                out[j * RPC : (j + 1) * RPC, pl.ds(start, HD)] = mixed[g * RPC : (g + 1) * RPC]
        return carry

    lax.fori_loop(0, heads_kv, head, 0)


SMEM = pl.BlockSpec(memory_space=pltpu.SMEM)
VMEM = pl.BlockSpec(memory_space=pltpu.VMEM)
ANY = pl.BlockSpec(memory_space=pl.ANY)


def local(span_keys, span_values, span_row, span_lists, recompute_pos, fresh_q, fresh_k, fresh_v):
    n_store = lax.axis_size("store")
    n_req = lax.axis_size("req")
    n_tp = lax.axis_size("tp")
    n_all = n_store * n_req * n_tp
    peers = n_store * n_req
    shard_rows, tok_dev, width = span_keys.shape
    heads_kv = width // HD
    heads_q = fresh_q.shape[2] // HD
    group = heads_q // heads_kv
    bf16 = jnp.bfloat16
    params = functools.partial(pltpu.CompilerParams, vmem_limit_bytes=48 << 20)

    ask = pl.pallas_call(
        functools.partial(ask_kernel, shard_rows, n_req),
        out_shape=jax.ShapeDtypeStruct((peers, LANES), jnp.int32),
        in_specs=[SMEM, SMEM],
        out_specs=VMEM,
        name="ask",
    )(span_row, span_lists)
    wanted = lax.all_to_all(ask, ("store", "req"), split_axis=0, concat_axis=0, tiled=True)

    send = pl.pallas_call(
        pick_kernel,
        out_shape=jax.ShapeDtypeStruct((peers, CAP, 2, tok_dev, width), bf16),
        in_specs=[SMEM, ANY, ANY],
        out_specs=ANY,
        scratch_shapes=[pltpu.SemaphoreType.DMA],
        name="pick",
    )(wanted, span_keys, span_values)
    got = lax.all_to_all(send, ("store", "req"), split_axis=0, concat_axis=0, tiled=True)
    got = got.reshape(n_store, n_req, CAP, 2, tok_dev, width)

    places, raw_q, raw_k, _ = lax.optimization_barrier((recompute_pos, fresh_q, fresh_k, send))
    places = places[0]
    raw_k = raw_k[0]
    new_v = fresh_v[0]
    angles = places.astype(jnp.float32)[:, None] * jnp.asarray(FREQ)[None, :]
    cosine = jnp.cos(angles)
    sine = jnp.sin(angles)
    queries, new_k = pl.pallas_call(
        functools.partial(fresh_kernel, heads_kv, group),
        out_shape=(
            jax.ShapeDtypeStruct((heads_kv * CPR, group * RPC, HD), bf16),
            jax.ShapeDtypeStruct((RC, width), bf16),
        ),
        in_specs=[VMEM] * 4,
        out_specs=(VMEM, VMEM),
        compiler_params=params(),
        name="fresh",
    )(
        raw_q[0],
        raw_k,
        jnp.concatenate([cosine, cosine], axis=1),
        jnp.concatenate([-sine, sine], axis=1),
    )
    places_col = places[:, None]
    places_row = places.reshape(CPR, RPC)

    part = pl.pallas_call(
        functools.partial(drift_kernel, shard_rows),
        out_shape=jax.ShapeDtypeStruct((n_all, LANES), jnp.float32),
        in_specs=[SMEM, SMEM, VMEM, VMEM, VMEM, ANY],
        out_specs=VMEM,
        scratch_shapes=[
            pltpu.VMEM((CPR, n_store, tok_dev, width), bf16),
            pltpu.VMEM((CPR, n_store, tok_dev, width), bf16),
            pltpu.SemaphoreType.DMA((2, CPR)),
        ],
        compiler_params=params(),
        cost_estimate=pl.CostEstimate(
            flops=4 * RC * CTX * width // CPR, bytes_accessed=4 * CTX * width, transcendentals=0
        ),
        name="drift",
    )(span_row, span_lists, places_col, raw_k, new_v, got)
    parts = lax.all_to_all(part, ("store", "req", "tp"), split_axis=0, concat_axis=0, tiled=True)

    attended = pl.pallas_call(
        functools.partial(attend_kernel, shard_rows, heads_kv, group),
        out_shape=jax.ShapeDtypeStruct((RC, heads_q * HD), bf16),
        in_specs=[SMEM, SMEM] + [VMEM] * 7 + [ANY],
        out_specs=VMEM,
        scratch_shapes=[
            pltpu.VMEM((CPR, n_store, tok_dev, width), bf16),
            pltpu.VMEM((CPR, n_store, tok_dev, width), bf16),
            pltpu.VMEM((heads_kv, CTX, HD), bf16),
            pltpu.VMEM((heads_kv, CTX, HD), bf16),
            pltpu.VMEM((CPR, RPC, CL), jnp.float32),
            pltpu.SemaphoreType.DMA((2, CPR)),
        ],
        compiler_params=params(),
        cost_estimate=pl.CostEstimate(
            flops=2 * heads_q * RC * CTX * HD * 2,
            bytes_accessed=4 * CTX * width + 4 * RC * heads_q * HD,
            transcendentals=heads_q * RC * CTX // 2,
        ),
        name="attend",
    )(
        span_row,
        span_lists,
        places_row,
        places_col,
        queries,
        new_k,
        new_v,
        jnp.asarray(COS_CTX),
        jnp.asarray(SIN_CTX),
        got,
    )
    per_dest = span_row.shape[0] // n_all
    drift_part = jnp.sum(parts, axis=0)[:per_dest]
    return (attended[None], drift_part)


def solution(mesh):
    in_specs = (
        P("req", "store", "tp"),
        P("req", "store", "tp"),
        P(),
        P(("store", "req"), None),
        P(("store", "req"), None),
        P(("store", "req"), None, "tp"),
        P(("store", "req"), None, "tp"),
        P(("store", "req"), None, "tp"),
    )
    out_specs = (P(("store", "req"), None, "tp"), P(("store", "req", "tp")))
    return jax.shard_map(local, mesh=mesh, in_specs=in_specs, out_specs=out_specs, check_vma=False)
```

time: 432 us -> 438 us (1.014)
  Pallas kernels: 0 us -> 282 us
  blocking collectives: 252 us -> 20.6 us
  waiting for transfers between devices: 36.8 us -> 113 us
  matrix products: 52.3 us -> 0 us
  local copies, waits for them, and re-layouts: 46.7 us -> 3.19 us
  other arithmetic: 29.5 us -> 1.73 us
    pallas_call x0 -> x5, Pallas kernels: none -> 282 us  [the longest x1 256 us: local(): pl.pallas_call(pick_kernel, out_shape=jax.ShapeDtypeStruct((peers, CAP, 2...]
    all_gather x1 -> x0, blocking collectives: 150 us -> none  [local(): lax.all_gather(span_lists, ('store', 'req'), axis=0, tiled=True)]
    unnamed x1 -> x0, blocking collectives: 102 us -> none
    all_to_all x2, waiting for transfers between devices: 36.8 us -> 113 us  [the longest x1 113 us: local(): lax.all_to_all(send, ('store', 'req'), split_axis=0, concat_axis=0, tiled...]
    dot_general x8 -> x0, matrix products: 30.2 us -> none  [attend(): jnp.einsum('hqk,kd->hqd', probabilities, value_block, preferred_element_t...]
    sub x8 -> x0, matrix products: 22.1 us -> none  [attend(): weights = jnp.exp(scores - row_max)]
    gather x10 -> x0, local copies, waits for them, and re-layouts: 20.8 us -> none  [the longest x1 4.39 us: local(): jnp.take(span_keys, chosen, axis=0)]
    all_to_all x0 -> x1, blocking collectives: none -> 20.6 us  [local(): lax.all_to_all(ask, ('store', 'req'), split_axis=0, concat_axis=0, tiled=...]
  transfers between devices with their start and end apart: 2 -> 2, of which waited for: 2 -> 1; matrix products, arithmetic and copies ran while one was open for 9% -> 0% of each run, Pallas kernels for 0% -> 4%
where the time goes in v1:
time: 438 us
  Pallas kernels  282 us (64%)
  waiting for transfers between devices  113 us (26%)
  blocking collectives  20.6 us (5%)
  starting transfers between devices  16.4 us (4%)
    pallas_call x1, Pallas kernels, local(): pl.pallas_call(pick_kernel, out_shape=jax.ShapeDtypeStruct((peers, CAP, 2...  256 us
    all_to_all x1, waiting for transfers between devices, local(): lax.all_to_all(send, ('store', 'req'), split_axis=0, concat_axis=0, tiled...  113 us
    all_to_all x1, blocking collectives, local(): lax.all_to_all(ask, ('store', 'req'), split_axis=0, concat_axis=0, tiled=...  20.6 us
    pallas_call x1, Pallas kernels, local(): pl.pallas_call(functools.partial(attend_kernel, shard_rows, heads_kv, gro...  18.1 us
    all_to_all x1, starting transfers between devices, local(): lax.all_to_all(part, ('store', 'req', 'tp'), split_axis=0, concat_axis=0,...  10.5 us
  transfers between devices with their start and end apart: 2, of which 1 were waited for; matrix products, arithmetic and copies ran while one was open for 0% of the time, Pallas kernels for 4%

profile of v1, /device:TPU:1, one launch (start us, length us, event | category | flops | bytes accessed | tf_op | source)
XLA Modules:
  0.0 437.8 jit_solution(969268899507430771)
XLA Ops:
  0.6 1.4 ask.1
  2.0 20.6 %all_to_all.25 = s32[64,1,128]{2,1,0:T(1,128)} all-to-all(s32[64,1,128]{2,1,0:T(1,128)} %bitcast.22), channel_id=1, replica_groups=mesh['store'=16,'req'=4,'tp'=2] {'store','req'}, dimensions={0} | all-to-all | bytes 65536 | tf_op jit(solution)/shard_map/all_to_all | solution.py:243
  22.6 256.4 %pick.1 = bf16[64,4,2,16,512]{4,3,2,1,0:T(8,128)(2,1)} custom-call(s32[64,128]{1,0:T(8,128)} %bitcast.21, bf16[128,16,512]{2,1,0:T(8,128)(2,1)} %keys.1, bf16[128,16,512]{2,1,0:T(8,128)(2,1)} %values.1), custom_call_target="tpu_custom_call" | custom-call | tf_op jit(solution)/shard_map/pick/pallas_call | solution.py:245
  279.0 0.0 copy-start.7
  279.0 0.0 copy-start.8
  279.0 0.0 copy-start
  279.1 0.0 copy-start.1
  279.1 0.0 copy-start.2
  279.1 0.0 copy-start.3
  279.1 0.0 copy-start.4
  279.1 5.9 %all-to-all-start.1 = ((bf16[64,4,2,16,512]{4,3,2,1,0:T(8,128)(2,1)}), bf16[64,4,2,16,512]{4,3,2,1,0:T(8,128)(2,1)}, u32[]{:S(2)}, u32[]{:S(2)}) async-start(bf16[64,4,2,16,512]{4,3,2,1,0:T(8,128)(2,1)} %pick.1), calls=%async_computation.1 | async-start | bytes 16777216 | tf_op jit(solution)/shard_map/all_to_all | solution.py:253
  285.0 0.5 broadcast.4
  285.5 0.0 copy-done.7
  285.5 0.7 convert_bitcast_fusion
  286.2 0.1 reshape_squeeze.3.places_row
  286.3 0.1 copy.16.places_col.places
  286.4 0.3 fusion
  286.7 0.1 pad_maximum_fusion
  286.8 0.0 copy-done
  286.8 0.0 copy-done.1
  286.8 0.6 fresh.1
  287.4 112.9 %all-to-all-done.1 = bf16[64,4,2,16,512]{4,3,2,1,0:T(8,128)(2,1)} async-done(((bf16[64,4,2,16,512]{4,3,2,1,0:T(8,128)(2,1)}), bf16[64,4,2,16,512]{4,3,2,1,0:T(8,128)(2,1)}, u32[]{:S(2)}, u32[]{:S(2)}) %all-to-all-start.1) | async-done | bytes 8388640 | tf_op jit(solution)/shard_map/all_to_all | solution.py:253
  400.2 0.0 copy-done.2
  400.2 0.0 copy-done.4
  400.2 5.8 %drift.1 = f32[128,128]{1,0:T(8,128)} custom-call(s32[512]{0:T(512)S(1)} %copy-done.3, s32[1,8]{1,0:T(1,128)S(1)} %copy-done.4, s32[128,1]{1,0:T(8,128)S(1)} %copy.16.places_col.places, bf16[128,512]{1,0:T(8,128)(2,1)S(1)} %bitcast.18, bf16[128,512]{1,0:T(8,128)(2,1)S(1)} %bitcast.19, bf16[16,4,4,2,16,512]{5,4,3,2,1,0:T(8,128)(2,1)} %bitcast.8.got), custom_call_target="tpu_custom_call" | custom-call | flops 67108864 | bytes 4194304 | tf_op jit(solution)/shard_map/drift/pallas_call | solution.py:282
  406.0 10.5 %all-to-all-start.2 = ((f32[128,1,128]{2,1,0:T(1,128)}), f32[128,1,128]{2,1,0:T(1,128)S(1)}, u32[]{:S(2)}, u32[]{:S(2)}) async-start(f32[128,1,128]{2,1,0:T(1,128)} %bitcast.11), calls=%async_computation.2 | async-start | bytes 131072 | tf_op jit(solution)/shard_map/all_to_all | solution.py:298
  416.5 0.0 copy-start.5
  416.5 1.2 copy-done.5
  417.7 1.2 copy-done.6
  419.0 18.1 %attend.1 = bf16[128,4096]{1,0:T(8,128)(2,1)} custom-call(s32[512]{0:T(512)S(1)} %copy-done.3, s32[1,8]{1,0:T(1,128)S(1)} %copy-done.4, s32[8,16]{1,0:T(8,128)S(1)} %reshape_squeeze.3.places_row, s32[128,1]{1,0:T(8,128)S(1)} %copy.16.places_col.places, bf16[32,128,128]{2,1,0:T(8,128)(2,1)S(1)} %get-tuple-element.10.q, ...), custom_call_target="tpu_custom_call" | custom-call | flops 4294967296 | bytes 6291456 | tf_op jit(solution)/shard_map/attend/pallas_call | solution.py:300
  437.1 0.0 all-to-all-done.2
  437.1 0.7 reduce_sum.9
  (3 shorter events, 0.0 us)
Async XLA Ops:
  279.0 6.5 %copy-start.7 = (s32[1,128]{1,0:T(1,128)S(1)}, s32[1,128]{1,0:T(1,128)}, u32[]{:S(2)}) copy-start(s32[1,128]{1,0:T(1,128)} %param.15) | copy-start | bytes 1540
  279.0 7.3 %copy-start.8 = (f32[64]{0:T(128)S(1)}, f32[64]{0:T(128)}, u32[]{:S(2)}) copy-start(f32[64]{0:T(128)} %constant.8.clone) | copy-start | bytes 772
  279.0 7.8 %copy-start = (bf16[1,128,4096]{2,1,0:T(8,128)(2,1)S(1)}, bf16[1,128,4096]{2,1,0:T(8,128)(2,1)}, u32[]{:S(2)}) copy-start(bf16[1,128,4096]{2,1,0:T(8,128)(2,1)} %param.16) | copy-start | bytes 3145732
  279.1 7.8 %copy-start.1 = (bf16[1,128,512]{2,1,0:T(8,128)(2,1)S(1)}, bf16[1,128,512]{2,1,0:T(8,128)(2,1)}, u32[]{:S(2)}) copy-start(bf16[1,128,512]{2,1,0:T(8,128)(2,1)} %param.17) | copy-start | bytes 393220
  279.1 121.2 %copy-start.2 = (bf16[1,128,512]{2,1,0:T(8,128)(2,1)S(1)}, bf16[1,128,512]{2,1,0:T(8,128)(2,1)}, u32[]{:S(2)}) copy-start(bf16[1,128,512]{2,1,0:T(8,128)(2,1)} %param.18) | copy-start | bytes 393220
  279.1 121.2 %copy-start.3 = (s32[512]{0:T(512)S(1)}, s32[512]{0:T(512)}, u32[]{:S(2)}) copy-start(s32[512]{0:T(512)} %span_row.5) | copy-start | bytes 6148
  279.1 121.2 %copy-start.4 = (s32[1,8]{1,0:T(1,128)S(1)}, s32[1,8]{1,0:T(1,128)}, u32[]{:S(2)}) copy-start(s32[1,8]{1,0:T(1,128)} %span_lists.5) | copy-start | bytes 100
  279.1 121.1 %all-to-all-start.1 = ((bf16[64,4,2,16,512]{4,3,2,1,0:T(8,128)(2,1)}), bf16[64,4,2,16,512]{4,3,2,1,0:T(8,128)(2,1)}, u32[]{:S(2)}, u32[]{:S(2)}) async-start(bf16[64,4,2,16,512]{4,3,2,1,0:T(8,128)(2,1)} %pick.1), calls=%async_computation.1 | async-start | bytes 16777216 | tf_op jit(solution)/shard_map/all_to_all | solution.py:253
  406.0 31.1 %all-to-all-start.2 = ((f32[128,1,128]{2,1,0:T(1,128)}), f32[128,1,128]{2,1,0:T(1,128)S(1)}, u32[]{:S(2)}, u32[]{:S(2)}) async-start(f32[128,1,128]{2,1,0:T(1,128)} %bitcast.11), calls=%async_computation.2 | async-start | bytes 131072 | tf_op jit(solution)/shard_map/all_to_all | solution.py:298
  416.5 1.2 copy-start.5
  417.7 1.2 copy-start.6

commit v2 on v1

v2 whole, which is shorter than its diff:
```python
import functools

import jax
import jax.numpy as jnp
import numpy as np
from jax import lax
from jax.experimental import pallas as pl
from jax.experimental.pallas import tpu as pltpu
from jax.sharding import PartitionSpec as P

HD = 128
HALF = HD // 2
CPR = 8
RPC = 16
CL = 256
CTX = CPR * CL
RC = CPR * RPC
KVH = 8
CAP = 4
LANES = 128
SCALE_LOG2E = float(HD ** -0.5 * np.log2(np.e))

FREQ = np.exp(-np.log(500000.0) * np.arange(HALF) / HALF).astype(np.float32)


def angle_tables(positions):
    angles = positions[:, None].astype(np.float64) * FREQ[None, :].astype(np.float64)
    cosine = np.cos(angles).astype(np.float32)
    sine = np.sin(angles).astype(np.float32)
    return (
        np.concatenate([cosine, cosine], axis=1),
        np.concatenate([-sine, sine], axis=1),
    )


COS_SPAN, SIN_SPAN = angle_tables(CL * np.arange(CPR))
COS_TOKEN, SIN_TOKEN = angle_tables(np.arange(CL))


def turn(x, cosine, sine):
    return x * cosine + pltpu.roll(x, HALF, 1) * sine


def span_homes(span_row, span_lists, shard_rows):
    rows = [span_row[span_lists[0, j]] for j in range(CPR)]
    homes = [row // shard_rows for row in rows]
    slots = [row % shard_rows for row in rows]
    ranks = []
    for j in range(CPR):
        rank = jnp.int32(0)
        for i in range(j):
            rank = rank + jnp.where(homes[i] == homes[j], 1, 0)
        ranks.append(rank)
    return homes, slots, ranks


def ask_kernel(shard_rows, blocks, span_row, span_lists, out):
    homes, slots, ranks = span_homes(span_row, span_lists, shard_rows)
    block = lax.broadcasted_iota(jnp.int32, out.shape, 0) % blocks
    lane = lax.broadcasted_iota(jnp.int32, out.shape, 1)
    total = jnp.zeros(out.shape, jnp.int32)
    for j in range(CPR):
        total = jnp.where((block == homes[j]) & (lane == ranks[j]), slots[j], total)
    out[...] = total


def pick_kernel(wanted, keys, values, send, key_rows, value_rows, stage, in_sems, out_sem):
    loads = [
        pltpu.make_async_copy(table, rows, in_sems.at[i])
        for i, (table, rows) in enumerate(((keys, key_rows), (values, value_rows)))
    ]
    for load in loads:
        load.start()
    for load in loads:
        load.wait()

    def fill(r, carry):
        for t in range(CAP):
            row = wanted[r, t]
            stage[r, t, 0] = key_rows[row]
            stage[r, t, 1] = value_rows[row]
        pltpu.make_async_copy(stage.at[r], send.at[r], out_sem).start()
        return carry

    lax.fori_loop(0, send.shape[0], fill, 0, unroll=4)
    pltpu.make_async_copy(stage, send, out_sem).wait()


def fresh_kernel(heads_kv, group, q, k, cosine, sine, q_out, k_out):
    cos = cosine[...]
    sin = sine[...]
    for h in range(heads_kv):
        cols = slice(h * HD, (h + 1) * HD)
        k_out[:, cols] = turn(k[:, cols].astype(jnp.float32), cos, sin).astype(jnp.bfloat16)
        for g in range(group):
            n = h * group + g
            turned = turn(q[:, n * HD : (n + 1) * HD].astype(jnp.float32), cos, sin)
            turned = turned.astype(jnp.bfloat16)
            for j in range(CPR):
                q_out[h * CPR + j, g * RPC : (g + 1) * RPC, :] = turned[j * RPC : (j + 1) * RPC]


def prepare_kernel(
    shard_rows,
    heads_kv,
    span_row,
    span_lists,
    places_row,
    places_col,
    fresh_k,
    fresh_v,
    new_k,
    cos_span,
    sin_span,
    cos_token,
    sin_token,
    got,
    keys,
    vals,
    drift,
    kbuf,
    vbuf,
    key_stage,
    value_stage,
    sems,
    out_sem,
):
    homes, _, ranks = span_homes(span_row, span_lists, shard_rows)
    copies = []
    for j in range(CPR):
        pair = [
            pltpu.make_async_copy(got.at[:, homes[j], ranks[j], which], buf.at[j], sems.at[which, j])
            for which, buf in enumerate((kbuf, vbuf))
        ]
        for copy in pair:
            copy.start()
        copies.append(pair)
    width = fresh_k.shape[1]
    dest = lax.broadcasted_iota(jnp.int32, drift.shape, 0)
    lane = lax.broadcasted_iota(jnp.int32, drift.shape, 1)
    per_dest = span_row.shape[0] // drift.shape[0]
    total = jnp.zeros(drift.shape, jnp.float32)
    token_row = lax.broadcasted_iota(jnp.int32, (CL, RPC), 0)
    token_lane = lax.broadcasted_iota(jnp.int32, (RPC, CL), 1)
    ones = jnp.ones((RPC, HD), jnp.bfloat16)
    stores = []
    for j in range(CPR):
        rows = slice(j * RPC, (j + 1) * RPC)
        span = slice(j * CL, (j + 1) * CL)
        take = (token_lane + j * CL == places_col[rows, :]).astype(jnp.float32)
        take = take.astype(jnp.bfloat16)
        put = (token_row + j * CL == places_row[j : j + 1, :]).astype(jnp.float32)
        put = put.astype(jnp.bfloat16)
        replaced = jnp.dot(put, ones, preferred_element_type=jnp.float32) > 0.5
        ca, sa = cos_span[j : j + 1, :], sin_span[j : j + 1, :]
        cb, sb = cos_token[...], sin_token[...]
        cos = ca * cb - sa * sb
        sin = sa * cb + ca * sb
        gap = jnp.zeros((RPC, width), jnp.float32)
        for copy, buf, fresh in zip(copies[j], (kbuf, vbuf), (fresh_k, fresh_v)):
            copy.wait()
            cached = jnp.dot(take, buf[j].reshape(CL, width), preferred_element_type=jnp.float32)
            delta = fresh[rows, :].astype(jnp.float32) - cached
            gap = gap + delta * delta
        share = jnp.sum(gap) * (1.0 / (2.0 * KVH * HD * RPC))
        chosen = span_lists[0, j]
        total = total + jnp.where(
            (dest == chosen // per_dest) & (lane == chosen % per_dest), share, 0.0
        )
        for h in range(heads_kv):
            cols = slice(h * HD, (h + 1) * HD)
            raw = kbuf[j, :, :, cols].reshape(CL, HD).astype(jnp.float32)
            new = jnp.dot(put, new_k[rows, cols], preferred_element_type=jnp.float32)
            ready = jnp.where(replaced, new, turn(raw, cos, sin))
            key_stage[j, h] = ready.astype(jnp.bfloat16)
            raw = vbuf[j, :, :, cols].reshape(CL, HD).astype(jnp.float32)
            new = jnp.dot(put, fresh_v[rows, cols], preferred_element_type=jnp.float32)
            value_stage[j, h] = jnp.where(replaced, new, raw).astype(jnp.bfloat16)
        for stage, whole in ((key_stage, keys), (value_stage, vals)):
            copy = pltpu.make_async_copy(stage.at[j], whole.at[:, span], out_sem)
            copy.start()
            stores.append(copy)
    drift[...] = total
    for copy in stores:
        copy.wait()


def attend_kernel(
    heads_kv, group, places_col, q, all_keys, all_vals, out, keys, vals, seen, scores, sems
):
    pairs = ((all_keys, keys), (all_vals, vals))
    for h in range(heads_kv):
        for which, (whole, buf) in enumerate(pairs):
            pltpu.make_async_copy(whole.at[h], buf.at[h], sems.at[which, h]).start()
    block = group * RPC
    token = lax.broadcasted_iota(jnp.int32, (RPC, CL), 1)
    for j in range(CPR):
        rows = slice(j * RPC, (j + 1) * RPC)
        seen[j] = jnp.where(token + j * CL <= places_col[rows, :], 0.0, -1e30)

    def head(h, carry):
        for which, (whole, buf) in enumerate(pairs):
            pltpu.make_async_copy(whole.at[h], buf.at[h], sems.at[which, h]).wait()
        for t in range(CPR):
            later = q[pl.ds(h * CPR + t, CPR - t)].reshape((CPR - t) * block, HD)
            scores[t * block :, t * CL : (t + 1) * CL] = lax.dot_general(
                later,
                keys[h, t * CL : (t + 1) * CL, :],
                (((1,), (1,)), ((), ())),
                preferred_element_type=jnp.float32,
            )
        for j in range(CPR):
            extent = (j + 1) * CL
            part = scores[j * block : (j + 1) * block, :extent]
            bias = jnp.concatenate([seen[j]] * group, axis=0)
            last = part[:, j * CL :] + bias
            part = last if j == 0 else jnp.concatenate([part[:, : j * CL], last], axis=1)
            row_max = jnp.max(part, axis=1, keepdims=True)
            weights = jnp.exp2((part - row_max) * SCALE_LOG2E)
            row_sum = jnp.sum(weights, axis=1, keepdims=True)
            mixed = jnp.dot(
                weights.astype(jnp.bfloat16),
                vals[h, :extent, :],
                preferred_element_type=jnp.float32,
            )
            mixed = (mixed / row_sum).astype(jnp.bfloat16)
            for g in range(group):
                start = pl.multiple_of((h * group + g) * HD, HD)
                out[j * RPC : (j + 1) * RPC, pl.ds(start, HD)] = mixed[g * RPC : (g + 1) * RPC]
        return carry

    lax.fori_loop(0, heads_kv, head, 0)


SMEM = pl.BlockSpec(memory_space=pltpu.SMEM)
VMEM = pl.BlockSpec(memory_space=pltpu.VMEM)
ANY = pl.BlockSpec(memory_space=pl.ANY)


def local(span_keys, span_values, span_row, span_lists, recompute_pos, fresh_q, fresh_k, fresh_v):
    n_store = lax.axis_size("store")
    n_req = lax.axis_size("req")
    n_tp = lax.axis_size("tp")
    n_all = n_store * n_req * n_tp
    peers = n_store * n_req
    shard_rows, tok_dev, width = span_keys.shape
    heads_kv = width // HD
    heads_q = fresh_q.shape[2] // HD
    group = heads_q // heads_kv
    bf16 = jnp.bfloat16

    def params(mebibytes):
        return pltpu.CompilerParams(vmem_limit_bytes=mebibytes << 20)


    ask = pl.pallas_call(
        functools.partial(ask_kernel, shard_rows, n_req),
        out_shape=jax.ShapeDtypeStruct((peers, LANES), jnp.int32),
        in_specs=[SMEM, SMEM],
        out_specs=VMEM,
        name="ask",
    )(span_row, span_lists)
    wanted = lax.all_to_all(ask, ("store", "req"), split_axis=0, concat_axis=0, tiled=True)

    send = pl.pallas_call(
        pick_kernel,
        out_shape=jax.ShapeDtypeStruct((peers, CAP, 2, tok_dev, width), bf16),
        in_specs=[SMEM, ANY, ANY],
        out_specs=ANY,
        scratch_shapes=[
            pltpu.VMEM((shard_rows, tok_dev, width), bf16),
            pltpu.VMEM((shard_rows, tok_dev, width), bf16),
            pltpu.VMEM((peers, CAP, 2, tok_dev, width), bf16),
            pltpu.SemaphoreType.DMA((2,)),
            pltpu.SemaphoreType.DMA,
        ],
        compiler_params=params(58),
        name="pick",
    )(wanted, span_keys, span_values)
    got = lax.all_to_all(send, ("store", "req"), split_axis=0, concat_axis=0, tiled=True)
    got = got.reshape(n_store, n_req, CAP, 2, tok_dev, width)

    places, raw_q, raw_k, _ = lax.optimization_barrier((recompute_pos, fresh_q, fresh_k, send))
    places = places[0]
    raw_k = raw_k[0]
    new_v = fresh_v[0]
    angles = places.astype(jnp.float32)[:, None] * jnp.asarray(FREQ)[None, :]
    cosine = jnp.cos(angles)
    sine = jnp.sin(angles)
    queries, new_k = pl.pallas_call(
        functools.partial(fresh_kernel, heads_kv, group),
        out_shape=(
            jax.ShapeDtypeStruct((heads_kv * CPR, group * RPC, HD), bf16),
            jax.ShapeDtypeStruct((RC, width), bf16),
        ),
        in_specs=[VMEM] * 4,
        out_specs=(VMEM, VMEM),
        compiler_params=params(16),
        name="fresh",
    )(
        raw_q[0],
        raw_k,
        jnp.concatenate([cosine, cosine], axis=1),
        jnp.concatenate([-sine, sine], axis=1),
    )
    places_col = places[:, None]
    places_row = places.reshape(CPR, RPC)

    keys, vals, part = pl.pallas_call(
        functools.partial(prepare_kernel, shard_rows, heads_kv),
        out_shape=(
            jax.ShapeDtypeStruct((heads_kv, CTX, HD), bf16),
            jax.ShapeDtypeStruct((heads_kv, CTX, HD), bf16),
            jax.ShapeDtypeStruct((n_all, LANES), jnp.float32),
        ),
        in_specs=[SMEM, SMEM] + [VMEM] * 9 + [ANY],
        out_specs=(ANY, ANY, VMEM),
        scratch_shapes=[
            pltpu.VMEM((CPR, n_store, tok_dev, width), bf16),
            pltpu.VMEM((CPR, n_store, tok_dev, width), bf16),
            pltpu.VMEM((CPR, heads_kv, CL, HD), bf16),
            pltpu.VMEM((CPR, heads_kv, CL, HD), bf16),
            pltpu.SemaphoreType.DMA((2, CPR)),
            pltpu.SemaphoreType.DMA,
        ],
        compiler_params=params(52),
        cost_estimate=pl.CostEstimate(
            flops=8 * RC * CTX * width // CPR, bytes_accessed=8 * CTX * width, transcendentals=0
        ),
        name="prepare",
    )(
        span_row,
        span_lists,
        places_row,
        places_col,
        raw_k,
        new_v,
        new_k,
        jnp.asarray(COS_SPAN),
        jnp.asarray(SIN_SPAN),
        jnp.asarray(COS_TOKEN),
        jnp.asarray(SIN_TOKEN),
        got,
    )
    parts = lax.all_to_all(part, ("store", "req", "tp"), split_axis=0, concat_axis=0, tiled=True)

    attended = pl.pallas_call(
        functools.partial(attend_kernel, heads_kv, group),
        out_shape=jax.ShapeDtypeStruct((RC, heads_q * HD), bf16),
        in_specs=[VMEM, VMEM, ANY, ANY],
        out_specs=VMEM,
        scratch_shapes=[
            pltpu.VMEM((heads_kv, CTX, HD), bf16),
            pltpu.VMEM((heads_kv, CTX, HD), bf16),
            pltpu.VMEM((CPR, RPC, CL), jnp.float32),
            pltpu.VMEM((CPR * group * RPC, CTX), jnp.float32),
            pltpu.SemaphoreType.DMA((2, heads_kv)),
        ],
        compiler_params=params(59),
        cost_estimate=pl.CostEstimate(
            flops=2 * heads_q * RC * CTX * HD * 2,
            bytes_accessed=4 * CTX * width + 4 * RC * heads_q * HD,
            transcendentals=heads_q * RC * CTX // 2,
        ),
        name="attend",
    )(places_col, queries, keys, vals)
    per_dest = span_row.shape[0] // n_all
    drift_part = jnp.sum(parts, axis=0)[:per_dest]
    return (attended[None], drift_part)


def solution(mesh):
    in_specs = (
        P("req", "store", "tp"),
        P("req", "store", "tp"),
        P(),
        P(("store", "req"), None),
        P(("store", "req"), None),
        P(("store", "req"), None, "tp"),
        P(("store", "req"), None, "tp"),
        P(("store", "req"), None, "tp"),
    )
    out_specs = (P(("store", "req"), None, "tp"), P(("store", "req", "tp")))
    return jax.shard_map(local, mesh=mesh, in_specs=in_specs, out_specs=out_specs, check_vma=False)
```

time: 438 us -> 181 us (0.41)
  Pallas kernels: 282 us -> 27.4 us
    pallas_call x1, Pallas kernels: 256 us -> 6.69 us  [local(): pl.pallas_call(pick_kernel, out_shape=jax.ShapeDtypeStruct((peers, CAP, 2...]
    pallas_call x2, Pallas kernels: 23.9 us -> 18.8 us  [the longest x1 11.4 us: local(): pl.pallas_call(functools.partial(attend_kernel, heads_kv, group), out_sha...]
  transfers between devices with their start and end apart: 2 -> 2, of which waited for: 1 -> 1; matrix products, arithmetic and copies ran while one was open for 0% -> 1% of each run, Pallas kernels for 4% -> 7%
where the time goes in v2:
time: 181 us
  waiting for transfers between devices  112 us (62%)
  Pallas kernels  27.4 us (15%)
  blocking collectives  20.6 us (11%)
  starting transfers between devices  16.4 us (9%)
    all_to_all x1, waiting for transfers between devices, local(): lax.all_to_all(send, ('store', 'req'), split_axis=0, concat_axis=0, tiled...  112 us
    all_to_all x1, blocking collectives, local(): lax.all_to_all(ask, ('store', 'req'), split_axis=0, concat_axis=0, tiled=...  20.6 us
    pallas_call x1, Pallas kernels, local(): pl.pallas_call(functools.partial(attend_kernel, heads_kv, group), out_sha...  11.4 us
    all_to_all x1, starting transfers between devices, local(): lax.all_to_all(part, ('store', 'req', 'tp'), split_axis=0, concat_axis=0,...  10.5 us
    pallas_call x1, Pallas kernels, local(): pl.pallas_call(functools.partial(prepare_kernel, shard_rows, heads_kv), o...  7.37 us
    pallas_call x1, Pallas kernels, local(): pl.pallas_call(pick_kernel, out_shape=jax.ShapeDtypeStruct((peers, CAP, 2...  6.69 us
    all_to_all x1, starting transfers between devices, local(): lax.all_to_all(send, ('store', 'req'), split_axis=0, concat_axis=0, tiled...  5.91 us
  transfers between devices with their start and end apart: 2, of which 1 were waited for; matrix products, arithmetic and copies ran while one was open for 1% of the time, Pallas kernels for 7%

profile of v2, /device:TPU:1, one launch (start us, length us, event | category | flops | bytes accessed | tf_op | source)
XLA Modules:
  0.0 180.6 jit_solution(5488215856174522768)
XLA Ops:
  0.6 1.4 ask.1
  2.0 20.6 %all_to_all.25 = s32[64,1,128]{2,1,0:T(1,128)} all-to-all(s32[64,1,128]{2,1,0:T(1,128)} %bitcast.21), channel_id=1, replica_groups=mesh['store'=16,'req'=4,'tp'=2] {'store','req'}, dimensions={0} | all-to-all | bytes 65536 | tf_op jit(solution)/shard_map/all_to_all | solution.py:263
  22.6 6.7 %pick.1 = bf16[64,4,2,16,512]{4,3,2,1,0:T(8,128)(2,1)} custom-call(s32[64,128]{1,0:T(8,128)} %bitcast.20, bf16[128,16,512]{2,1,0:T(8,128)(2,1)} %keys.1, bf16[128,16,512]{2,1,0:T(8,128)(2,1)} %values.1), custom_call_target="tpu_custom_call" | custom-call | tf_op jit(solution)/shard_map/pick/pallas_call | solution.py:265
  29.3 0.0 copy-start.11
  29.3 0.0 copy-start.12
  29.3 0.0 copy-start
  29.3 0.0 copy-start.1
  29.3 0.0 copy-start.3
  29.3 0.0 copy-start.4
  29.4 0.0 copy-start.5
  29.4 0.0 copy-start.6
  29.4 0.0 copy-start.7
  29.4 0.0 copy-start.8
  29.4 0.0 copy-start.9
  29.4 5.9 %all-to-all-start.1 = ((bf16[64,4,2,16,512]{4,3,2,1,0:T(8,128)(2,1)}), bf16[64,4,2,16,512]{4,3,2,1,0:T(8,128)(2,1)}, u32[]{:S(2)}, u32[]{:S(2)}) async-start(bf16[64,4,2,16,512]{4,3,2,1,0:T(8,128)(2,1)} %pick.1), calls=%async_computation.1 | async-start | bytes 16777216 | tf_op jit(solution)/shard_map/all_to_all | solution.py:280
  35.3 0.5 broadcast.4
  35.9 0.7 fusion.1
  36.5 0.1 reshape_squeeze.3.places_row
  36.6 0.1 copy.19.places_col
  36.7 0.3 fusion
  37.0 0.1 pad_maximum_fusion
  37.2 0.6 fresh.1
  37.7 1.0 copy-done.10
  38.7 111.9 %all-to-all-done.1 = bf16[64,4,2,16,512]{4,3,2,1,0:T(8,128)(2,1)} async-done(((bf16[64,4,2,16,512]{4,3,2,1,0:T(8,128)(2,1)}), bf16[64,4,2,16,512]{4,3,2,1,0:T(8,128)(2,1)}, u32[]{:S(2)}, u32[]{:S(2)}) %all-to-all-start.1) | async-done | bytes 8388640 | tf_op jit(solution)/shard_map/all_to_all | solution.py:280
  150.6 0.0 copy-done.4
  150.6 0.0 copy-done.6
  150.6 7.4 %prepare.1 = (bf16[4,2048,128]{2,1,0:T(8,128)(2,1)}, bf16[4,2048,128]{2,1,0:T(8,128)(2,1)}, f32[128,128]{1,0:T(8,128)}) custom-call(s32[512]{0:T(512)S(1)} %copy-done.6, s32[1,8]{1,0:T(1,128)S(1)} %copy-done.9, s32[8,16]{1,0:T(8,128)S(1)} %reshape_squeeze.3.places_row, s32[128,1]{1,0:T(8,128)S(1)} %copy.19.places_col, bf16[128,512]{1,0:T(8,128)(2,1)S(1)} %bitcast.18, ...), custom_call_target="tpu_custom_call" | custom-call | flops 134217728 | bytes 8388608 | tf_op jit(solution)/shard_map/prepare/pallas_call | solution.py:309
  158.0 0.0 copy-done.2
  158.0 10.5 %all-to-all-start.2 = ((f32[128,1,128]{2,1,0:T(1,128)}), f32[128,1,128]{2,1,0:T(1,128)S(1)}, u32[]{:S(2)}, u32[]{:S(2)}) async-start(f32[128,1,128]{2,1,0:T(1,128)} %bitcast.11), calls=%async_computation.2 | async-start | bytes 131072 | tf_op jit(solution)/shard_map/all_to_all | solution.py:345
  168.5 11.4 %attend.1 = bf16[128,4096]{1,0:T(8,128)(2,1)} custom-call(s32[128,1]{1,0:T(8,128)} %copy-done.2, bf16[32,128,128]{2,1,0:T(8,128)(2,1)} %copy-done.10, bf16[4,2048,128]{2,1,0:T(8,128)(2,1)} %get-tuple-element.15.all_keys, bf16[4,2048,128]{2,1,0:T(8,128)(2,1)} %get-tuple-element.16.all_vals), custom_call_target="tpu_custom_call" | custom-call | flops 4294967296 | bytes 6291456 | tf_op jit(solution)/shard_map/attend/pallas_call | solution.py:347
  179.9 0.0 all-to-all-done.2
  180.0 0.7 reduce_sum.9
  (11 shorter events, 0.0 us)
Async XLA Ops:
  29.3 6.6 %copy-start.11 = (s32[1,128]{1,0:T(1,128)S(1)}, s32[1,128]{1,0:T(1,128)}, u32[]{:S(2)}) copy-start(s32[1,128]{1,0:T(1,128)} %param.17) | copy-start | bytes 1540
  29.3 7.4 %copy-start.12 = (f32[64]{0:T(128)S(1)}, f32[64]{0:T(128)}, u32[]{:S(2)}) copy-start(f32[64]{0:T(128)} %constant.12.clone) | copy-start | bytes 772
  29.3 7.8 %copy-start = (bf16[1,128,4096]{2,1,0:T(8,128)(2,1)S(1)}, bf16[1,128,4096]{2,1,0:T(8,128)(2,1)}, u32[]{:S(2)}) copy-start(bf16[1,128,4096]{2,1,0:T(8,128)(2,1)} %param.18) | copy-start | bytes 3145732
  29.3 7.8 %copy-start.1 = (bf16[1,128,512]{2,1,0:T(8,128)(2,1)S(1)}, bf16[1,128,512]{2,1,0:T(8,128)(2,1)}, u32[]{:S(2)}) copy-start(bf16[1,128,512]{2,1,0:T(8,128)(2,1)} %param.19) | copy-start | bytes 393220
  29.3 121.2 %copy-start.3 = (bf16[1,128,512]{2,1,0:T(8,128)(2,1)S(1)}, bf16[1,128,512]{2,1,0:T(8,128)(2,1)}, u32[]{:S(2)}) copy-start(bf16[1,128,512]{2,1,0:T(8,128)(2,1)} %param.20) | copy-start | bytes 393220
  29.3 121.2 %copy-start.4 = (f32[256,128]{1,0:T(8,128)S(1)}, f32[256,128]{1,0:T(8,128)}, u32[]{:S(2)}) copy-start(f32[256,128]{1,0:T(8,128)} %constant.16.clone.sin_token) | copy-start | bytes 393220
  29.4 121.2 %copy-start.5 = (f32[256,128]{1,0:T(8,128)S(1)}, f32[256,128]{1,0:T(8,128)}, u32[]{:S(2)}) copy-start(f32[256,128]{1,0:T(8,128)} %constant.15.clone.cos_token) | copy-start | bytes 393220
  29.4 121.2 %copy-start.6 = (s32[512]{0:T(512)S(1)}, s32[512]{0:T(512)}, u32[]{:S(2)}) copy-start(s32[512]{0:T(512)} %span_row.3) | copy-start | bytes 6148
  29.4 121.2 %copy-start.7 = (f32[8,128]{1,0:T(8,128)S(1)}, f32[8,128]{1,0:T(8,128)}, u32[]{:S(2)}) copy-start(f32[8,128]{1,0:T(8,128)} %constant.14.clone.sin_span) | copy-start | bytes 12292
  29.4 121.2 %copy-start.8 = (f32[8,128]{1,0:T(8,128)S(1)}, f32[8,128]{1,0:T(8,128)}, u32[]{:S(2)}) copy-start(f32[8,128]{1,0:T(8,128)} %constant.13.clone.cos_span) | copy-start | bytes 12292
  29.4 121.2 %copy-start.9 = (s32[1,8]{1,0:T(1,128)S(1)}, s32[1,8]{1,0:T(1,128)}, u32[]{:S(2)}) copy-start(s32[1,8]{1,0:T(1,128)} %span_lists.3) | copy-start | bytes 100
  29.4 121.2 %all-to-all-start.1 = ((bf16[64,4,2,16,512]{4,3,2,1,0:T(8,128)(2,1)}), bf16[64,4,2,16,512]{4,3,2,1,0:T(8,128)(2,1)}, u32[]{:S(2)}, u32[]{:S(2)}) async-start(bf16[64,4,2,16,512]{4,3,2,1,0:T(8,128)(2,1)} %pick.1), calls=%async_computation.1 | async-start | bytes 16777216 | tf_op jit(solution)/shard_map/all_to_all | solution.py:280
  36.7 121.3 %copy-start.2 = (s32[128,1]{1,0:T(8,128)}, s32[128,1]{1,0:T(8,128)S(1)}, u32[]{:S(2)}) copy-start(s32[128,1]{1,0:T(8,128)S(1)} %copy.19.places_col) | copy-start | bytes 1540
  37.7 1.0 copy-start.10
  158.0 21.9 %all-to-all-start.2 = ((f32[128,1,128]{2,1,0:T(1,128)}), f32[128,1,128]{2,1,0:T(1,128)S(1)}, u32[]{:S(2)}, u32[]{:S(2)}) async-start(f32[128,1,128]{2,1,0:T(1,128)} %bitcast.11), calls=%async_computation.2 | async-start | bytes 131072 | tf_op jit(solution)/shard_map/all_to_all | solution.py:345

commit v3 on v2

--- a/solution.py
+++ b/solution.py
@@ -16,7 +16,10 @@
 CTX = CPR * CL
 RC = CPR * RPC
 KVH = 8
-CAP = 4
+BLOCKS = 4
+SLOTS = CPR // BLOCKS
+SIZES = (24, 32, 40)
+KEPT, UP, DOWN, FROM_BELOW, FROM_ABOVE, LOADS = 0, 4, 8, 12, 13, 16
 LANES = 128
 SCALE_LOG2E = float(HD ** -0.5 * np.log2(np.e))
 
@@ -41,48 +44,142 @@
     return x * cosine + pltpu.roll(x, HALF, 1) * sine
 
 
-def span_homes(span_row, span_lists, shard_rows):
-    rows = [span_row[span_lists[0, j]] for j in range(CPR)]
-    homes = [row // shard_rows for row in rows]
-    slots = [row % shard_rows for row in rows]
-    ranks = []
+def ask_kernel(shard_rows, span_row, span_lists, plan, place):
+    spans = [span_row[span_lists[0, j]] for j in range(CPR)]
+    homes = [row // shard_rows for row in spans]
+    rows = [row % shard_rows for row in spans]
+    one = [[jnp.where(home == k, 1, 0) for home in homes] for k in range(BLOCKS)]
+    counts = [sum(one[k]) for k in range(BLOCKS)]
+    sums = []
+    total = jnp.int32(0)
+    for k in range(BLOCKS):
+        total = total + counts[k] - SLOTS
+        sums.append(total)
+    low, high = jnp.minimum(sums[0], sums[1]), jnp.maximum(sums[0], sums[1])
+    low2, high2 = jnp.minimum(sums[2], sums[3]), jnp.maximum(sums[2], sums[3])
+    middle, middle2 = jnp.maximum(low, low2), jnp.minimum(high, high2)
+    odd = lax.rem(span_lists[0, 0], 2) == 1
+    shift = jnp.where(odd, jnp.maximum(middle, middle2), jnp.minimum(middle, middle2))
+    flow = [x - shift for x in sums]
+    up = [jnp.maximum(x, 0) for x in flow]
+    down = [jnp.maximum(-flow[k - 1], 0) for k in range(BLOCKS)]
+    keep = [counts[k] - up[k] - down[k] for k in range(BLOCKS)]
+
+    block = lax.broadcasted_iota(jnp.int32, plan.shape, 0) % BLOCKS
+    lane = lax.broadcasted_iota(jnp.int32, plan.shape, 1)
+    out = jnp.zeros(plan.shape, jnp.int32)
+    for k in range(BLOCKS):
+        own = block == k
+        heads = (
+            (KEPT, keep[k]),
+            (UP, up[k]),
+            (DOWN, down[k]),
+            (FROM_BELOW, up[k - 1]),
+            (FROM_ABOVE, down[(k + 1) % BLOCKS]),
+        )
+        for at, value in heads:
+            out = jnp.where(own & (lane == at), value, out)
+        out = jnp.where(lane == LOADS + k, up[k], out)
+        out = jnp.where(lane == LOADS + BLOCKS + k, down[k], out)
+
+    def of(table, k):
+        value = table[0]
+        for i in range(1, BLOCKS):
+            value = jnp.where(k == i, table[i], value)
+        return value
+
+    base_below = [keep[k] for k in range(BLOCKS)]
+    base_above = [keep[k] + up[k - 1] for k in range(BLOCKS)]
     for j in range(CPR):
+        home = homes[j]
         rank = jnp.int32(0)
         for i in range(j):
-            rank = rank + jnp.where(homes[i] == homes[j], 1, 0)
-        ranks.append(rank)
-    return homes, slots, ranks
-
-
-def ask_kernel(shard_rows, blocks, span_row, span_lists, out):
-    homes, slots, ranks = span_homes(span_row, span_lists, shard_rows)
-    block = lax.broadcasted_iota(jnp.int32, out.shape, 0) % blocks
-    lane = lax.broadcasted_iota(jnp.int32, out.shape, 1)
-    total = jnp.zeros(out.shape, jnp.int32)
-    for j in range(CPR):
-        total = jnp.where((block == homes[j]) & (lane == ranks[j]), slots[j], total)
-    out[...] = total
-
-
-def pick_kernel(wanted, keys, values, send, key_rows, value_rows, stage, in_sems, out_sem):
+            rank = rank + jnp.where(homes[i] == home, 1, 0)
+        kept = of(keep, home)
+        after = rank - kept
+        ups = of(up, home)
+        stays = after < 0
+        climbs = after < ups
+        at = jnp.where(
+            stays, KEPT + 1 + rank, jnp.where(climbs, UP + 1 + after, DOWN + 1 + after - ups)
+        )
+        out = jnp.where((block == home) & (lane == at), rows[j], out)
+        above = lax.rem(home + 1, BLOCKS)
+        below = lax.rem(home + BLOCKS - 1, BLOCKS)
+        place[0, j] = jnp.where(stays, home, jnp.where(climbs, above, below))
+        place[1, j] = jnp.where(
+            stays,
+            rank,
+            jnp.where(climbs, of(base_below, above) + after, of(base_above, below) + after - ups),
+        )
+    plan[...] = out
+
+
+def move_kernel(size, plan, keys, values, up_out, down_out, pool, up_stage, down_stage, sems):
     loads = [
-        pltpu.make_async_copy(table, rows, in_sems.at[i])
-        for i, (table, rows) in enumerate(((keys, key_rows), (values, value_rows)))
+        pltpu.make_async_copy(table, pool.at[i], sems.at[i])
+        for i, table in enumerate((keys, values))
     ]
     for load in loads:
         load.start()
     for load in loads:
         load.wait()
 
-    def fill(r, carry):
-        for t in range(CAP):
-            row = wanted[r, t]
-            stage[r, t, 0] = key_rows[row]
-            stage[r, t, 1] = value_rows[row]
+    def fill(r, marks):
+        ends = []
+        for at, stage, mark in ((UP, up_stage, marks[0]), (DOWN, down_stage, marks[1])):
+            for i in range(SLOTS):
+                row = plan[r, at + 1 + i]
+                stage[mark + i, 0] = pool[0, row]
+                stage[mark + i, 1] = pool[1, row]
+            ends.append(mark + plan[r, at])
+        return tuple(ends)
+
+    lax.fori_loop(0, plan.shape[0], fill, (jnp.int32(0), jnp.int32(0)))
+    stores = [
+        pltpu.make_async_copy(stage.at[pl.ds(0, size)], out, sems.at[i])
+        for i, (stage, out) in enumerate(((up_stage, up_out), (down_stage, down_out)))
+    ]
+    for store in stores:
+        store.start()
+    for store in stores:
+        store.wait()
+
+
+def pick_kernel(shard_rows, size, plan, keys, values, below, above, send, pool, stage, sems, out_sem):
+    loads = []
+    for i, table in enumerate((keys, values)):
+        loads.append(
+            pltpu.make_async_copy(table, pool.at[i, pl.ds(0, shard_rows)], sems.at[i, 0])
+        )
+        for n, part in enumerate((below, above)):
+            start = shard_rows + n * size
+            loads.append(
+                pltpu.make_async_copy(
+                    part.at[:, i], pool.at[i, pl.ds(start, size)], sems.at[i, n + 1]
+                )
+            )
+    for load in loads:
+        load.start()
+    for load in loads:
+        load.wait()
+
+    def fill(r, marks):
+        kept = plan[r, KEPT]
+        came = kept + plan[r, FROM_BELOW]
+        for t in range(SLOTS):
+            row = jnp.where(
+                t < kept,
+                plan[r, KEPT + 1 + t],
+                jnp.where(t < came, marks[0] + t - kept, marks[1] + t - came),
+            )
+            stage[r, t, 0] = pool[0, row]
+            stage[r, t, 1] = pool[1, row]
         pltpu.make_async_copy(stage.at[r], send.at[r], out_sem).start()
-        return carry
-
-    lax.fori_loop(0, send.shape[0], fill, 0, unroll=4)
+        return marks[0] + plan[r, FROM_BELOW], marks[1] + plan[r, FROM_ABOVE]
+
+    first = (jnp.int32(shard_rows), jnp.int32(shard_rows + size))
+    lax.fori_loop(0, send.shape[0], fill, first)
     pltpu.make_async_copy(stage, send, out_sem).wait()
 
 
@@ -101,9 +198,9 @@
 
 
 def prepare_kernel(
-    shard_rows,
     heads_kv,
-    span_row,
+    total_spans,
+    place,
     span_lists,
     places_row,
     places_col,
@@ -125,11 +222,10 @@
     sems,
     out_sem,
 ):
-    homes, _, ranks = span_homes(span_row, span_lists, shard_rows)
     copies = []
     for j in range(CPR):
         pair = [
-            pltpu.make_async_copy(got.at[:, homes[j], ranks[j], which], buf.at[j], sems.at[which, j])
+            pltpu.make_async_copy(got.at[:, place[0, j], place[1, j], which], buf.at[j], sems.at[which, j])
             for which, buf in enumerate((kbuf, vbuf))
         ]
         for copy in pair:
@@ -138,7 +234,7 @@
     width = fresh_k.shape[1]
     dest = lax.broadcasted_iota(jnp.int32, drift.shape, 0)
     lane = lax.broadcasted_iota(jnp.int32, drift.shape, 1)
-    per_dest = span_row.shape[0] // drift.shape[0]
+    per_dest = total_spans // drift.shape[0]
     total = jnp.zeros(drift.shape, jnp.float32)
     token_row = lax.broadcasted_iota(jnp.int32, (CL, RPC), 0)
     token_lane = lax.broadcasted_iota(jnp.int32, (RPC, CL), 1)
@@ -253,32 +349,67 @@
         return pltpu.CompilerParams(vmem_limit_bytes=mebibytes << 20)
 
 
-    ask = pl.pallas_call(
-        functools.partial(ask_kernel, shard_rows, n_req),
-        out_shape=jax.ShapeDtypeStruct((peers, LANES), jnp.int32),
+    assert n_req == BLOCKS and shard_rows * n_req == span_row.shape[0]
+    plan, place = pl.pallas_call(
+        functools.partial(ask_kernel, shard_rows),
+        out_shape=(
+            jax.ShapeDtypeStruct((peers, LANES), jnp.int32),
+            jax.ShapeDtypeStruct((2, CPR), jnp.int32),
+        ),
         in_specs=[SMEM, SMEM],
-        out_specs=VMEM,
+        out_specs=(VMEM, SMEM),
         name="ask",
     )(span_row, span_lists)
-    wanted = lax.all_to_all(ask, ("store", "req"), split_axis=0, concat_axis=0, tiled=True)
-
-    send = pl.pallas_call(
-        pick_kernel,
-        out_shape=jax.ShapeDtypeStruct((peers, CAP, 2, tok_dev, width), bf16),
-        in_specs=[SMEM, ANY, ANY],
-        out_specs=ANY,
-        scratch_shapes=[
-            pltpu.VMEM((shard_rows, tok_dev, width), bf16),
-            pltpu.VMEM((shard_rows, tok_dev, width), bf16),
-            pltpu.VMEM((peers, CAP, 2, tok_dev, width), bf16),
-            pltpu.SemaphoreType.DMA((2,)),
-            pltpu.SemaphoreType.DMA,
-        ],
-        compiler_params=params(58),
-        name="pick",
-    )(wanted, span_keys, span_values)
+    plans = lax.all_to_all(plan, ("store", "req"), split_axis=0, concat_axis=0, tiled=True)
+    piece = (2, tok_dev, width)
+    climb = [(k, (k + 1) % n_req) for k in range(n_req)]
+    sink = [(k, (k - 1) % n_req) for k in range(n_req)]
+
+    def gather(size, plans, span_keys, span_values):
+        moves = jax.ShapeDtypeStruct((size,) + piece, bf16)
+        ups, downs = pl.pallas_call(
+            functools.partial(move_kernel, size),
+            out_shape=(moves, moves),
+            in_specs=[SMEM, ANY, ANY],
+            out_specs=(ANY, ANY),
+            scratch_shapes=[
+                pltpu.VMEM((2, shard_rows, tok_dev, width), bf16),
+                pltpu.VMEM((size + SLOTS,) + piece, bf16),
+                pltpu.VMEM((size + SLOTS,) + piece, bf16),
+                pltpu.SemaphoreType.DMA((2,)),
+            ],
+            compiler_params=params(58),
+            name="move",
+        )(plans, span_keys, span_values)
+        below = lax.ppermute(ups, "req", climb)
+        above = lax.ppermute(downs, "req", sink)
+        return pl.pallas_call(
+            functools.partial(pick_kernel, shard_rows, size),
+            out_shape=jax.ShapeDtypeStruct((peers, SLOTS) + piece, bf16),
+            in_specs=[SMEM] + [ANY] * 4,
+            out_specs=ANY,
+            scratch_shapes=[
+                pltpu.VMEM((2, shard_rows + 2 * size, tok_dev, width), bf16),
+                pltpu.VMEM((peers, SLOTS) + piece, bf16),
+                pltpu.SemaphoreType.DMA((2, 3)),
+                pltpu.SemaphoreType.DMA,
+            ],
+            compiler_params=params(58),
+            name="pick",
+        )(plans, span_keys, span_values, below, above)
+
+    load = jnp.max(jnp.sum(plans[:, LOADS : LOADS + 2 * BLOCKS], axis=0))
+    level = sum((load > size).astype(jnp.int32) for size in SIZES)
+    most = SLOTS * peers
+    send = lax.switch(
+        level,
+        [functools.partial(gather, size) for size in SIZES + (most,)],
+        plans,
+        span_keys,
+        span_values,
+    )
     got = lax.all_to_all(send, ("store", "req"), split_axis=0, concat_axis=0, tiled=True)
-    got = got.reshape(n_store, n_req, CAP, 2, tok_dev, width)
+    got = got.reshape((n_store, n_req, SLOTS) + piece)
 
     places, raw_q, raw_k, _ = lax.optimization_barrier((recompute_pos, fresh_q, fresh_k, send))
     places = places[0]
@@ -307,7 +438,7 @@
     places_row = places.reshape(CPR, RPC)
 
     keys, vals, part = pl.pallas_call(
-        functools.partial(prepare_kernel, shard_rows, heads_kv),
+        functools.partial(prepare_kernel, heads_kv, span_row.shape[0]),
         out_shape=(
             jax.ShapeDtypeStruct((heads_kv, CTX, HD), bf16),
             jax.ShapeDtypeStruct((heads_kv, CTX, HD), bf16),
@@ -329,7 +460,7 @@
         ),
         name="prepare",
     )(
-        span_row,
+        place,
         span_lists,
         places_row,
         places_col,

time: 181 us -> 146 us (0.81)
  waiting for transfers between devices: 112 us -> 65.6 us
  starting transfers between devices: 16.4 us -> 20.4 us
  Pallas kernels: 27.4 us -> 31.1 us
  between operations: 0.86 us -> 2.83 us
    all_to_all x1, waiting for transfers between devices: 112 us -> 44.3 us  [local(): lax.all_to_all(send, ('store', 'req'), split_axis=0, concat_axis=0, tiled...]
    ppermute x0 -> x2, waiting for transfers between devices: none -> 21.3 us  [the longest x1 21.3 us: gather(): below = lax.ppermute(ups, 'req', climb)]
    pallas_call x3 -> x4, Pallas kernels: 15.5 us -> 19.5 us  [the longest x1 7.38 us: local(): pl.pallas_call(functools.partial(prepare_kernel, heads_kv, span_row.shape...]
    ppermute x0 -> x2, starting transfers between devices: none -> 2.75 us  [the longest x1 2.39 us: gather(): above = lax.ppermute(downs, 'req', sink)]
  transfers between devices with their start and end apart: 2 -> 4, of which waited for: 1 -> 2; matrix products, arithmetic and copies ran while one was open for 1% -> 1% of each run, Pallas kernels for 7% -> 8%
where the time goes in v3:
time: 146 us
  waiting for transfers between devices  65.6 us (45%)
  Pallas kernels  31.1 us (21%)
  starting transfers between devices  20.4 us (14%)
  blocking collectives  20.3 us (14%)
  between operations  2.83 us (2%)
  local copies, waits for them, and re-layouts  2.73 us (2%)
  other arithmetic  2.47 us (2%)
    all_to_all x1, waiting for transfers between devices, local(): lax.all_to_all(send, ('store', 'req'), split_axis=0, concat_axis=0, tiled...  44.3 us
    ppermute x1, waiting for transfers between devices, gather(): below = lax.ppermute(ups, 'req', climb)  21.3 us
    all_to_all x1, blocking collectives, local(): lax.all_to_all(plan, ('store', 'req'), split_axis=0, concat_axis=0, tiled...  20.3 us
    all_to_all x1, starting transfers between devices, local(): lax.all_to_all(part, ('store', 'req', 'tp'), split_axis=0, concat_axis=0,...  11.9 us
    pallas_call x1, Pallas kernels, local(): pl.pallas_call(functools.partial(attend_kernel, heads_kv, group), out_sha...  11.1 us
    pallas_call x1, Pallas kernels, local(): pl.pallas_call(functools.partial(prepare_kernel, heads_kv, span_row.shape...  7.38 us
    all_to_all x1, starting transfers between devices, local(): lax.all_to_all(send, ('store', 'req'), split_axis=0, concat_axis=0, tiled...  5.8 us
    pallas_call x1, Pallas kernels, gather(): pl.pallas_call(functools.partial(move_kernel, size), out_shape=(moves, mo...  5.68 us
  transfers between devices with their start and end apart: 4, of which 2 were waited for; matrix products, arithmetic and copies ran while one was open for 1% of the time, Pallas kernels for 8%

profile of v3, /device:TPU:1, one launch (start us, length us, event | category | flops | bytes accessed | tf_op | source)
XLA Modules:
  0.0 145.6 jit_solution(10735656020244829314)
XLA Ops:
  0.6 1.6 %ask.1 = (s32[64,128]{1,0:T(8,128)}, s32[2,8]{1,0:T(2,128)}) custom-call(s32[512]{0:T(512)} %span_row.1, s32[1,8]{1,0:T(1,128)} %span_lists.3), custom_call_target="tpu_custom_call" | custom-call | tf_op jit(solution)/shard_map/ask/pallas_call | solution.py:353
  2.2 20.3 %all_to_all.26 = s32[64,1,128]{2,1,0:T(1,128)S(1)} all-to-all(s32[64,1,128]{2,1,0:T(1,128)} %bitcast.25), channel_id=1, replica_groups=mesh['store'=16,'req'=4,'tp'=2] {'store','req'}, dimensions={0} | all-to-all | bytes 65536 | tf_op jit(solution)/shard_map/all_to_all | solution.py:363
  22.5 0.1 slice_reduce_fusion
  22.6 0.6 reduce_max.9
  25.2 35.6 %conditional.1 = (bf16[64,2,2,16,512]{4,3,2,1,0:T(8,128)(2,1)}) conditional(s32[]{:T(128)} %clamp.3, (s32[64,128]{1,0:T(8,128)S(1)}, bf16[128,16,512]{2,1,0:T(8,128)(2,1)}, bf16[128,16,512]{2,1,0:T(8,128)(2,1)}) %tuple.32, (s32[64,128]{1,0:T(8,128)S(1)}, bf16[128,16,512]{2,1,0:T(8,128)(2,1)}, ...), branch_computations={%region_2.0_spmd, %region_3.0_spmd, %region_4.0_spmd, %region_5.0_... | conditional | bytes 50331792 | solution.py:404
  25.3 0.0 copy-start.16
  25.3 5.7 %move.5 = (bf16[32,2,16,512]{3,2,1,0:T(8,128)(2,1)}, bf16[32,2,16,512]{3,2,1,0:T(8,128)(2,1)}) custom-call(s32[64,128]{1,0:T(8,128)S(1)} %get-tuple-element.34.plan, bf16[128,16,512]{2,1,0:T(8,128)(2,1)} %get-tuple-element.35.keys, bf16[128,16,512]{2,1,0:T(8,128)(2,1)} %get-tuple-element.36.values), custom_call_target="tpu_custom_call" | custom-call | tf_op jit(solution)/shard_map/cond/branch_1_fun/move/pallas_call | solution.py:370
  31.0 0.4 collective-permute-start.2
  31.3 2.4 %collective-permute-start.3 = (bf16[32,2,16,512]{3,2,1,0:T(8,128)(2,1)}, bf16[32,2,16,512]{3,2,1,0:T(8,128)(2,1)}, u32[]{:S(2)}, u32[]{:S(2)}) collective-permute-start(bf16[32,2,16,512]{3,2,1,0:T(8,128)(2,1)} %get-tuple-element.38), channel_id=1, source_target_pairs={{0,6},{2,0},{4,2},{6,4},{1,7},{3,1},{5,3},{7,5},{8,14},{10,8},{12,... | collective-permute-start | bytes 3145736 | tf_op jit(solution)/shard_map/cond/branch_1_fun/ppermute | solution.py:385
  33.7 21.3 %collective-permute-done.2.below = bf16[32,2,16,512]{3,2,1,0:T(8,128)(2,1)S(1)} collective-permute-done((bf16[32,2,16,512]{3,2,1,0:T(8,128)(2,1)}, bf16[32,2,16,512]{3,2,1,0:T(8,128)(2,1)S(1)}, u32[]{:S(2)}, u32[]{:S(2)}) %collective-permute-start.2) | collective-permute-done | bytes 1048608 | tf_op jit(solution)/shard_map/cond/branch_1_fun/ppermute | solution.py:384
  55.0 1.0 copy-done.20
  56.0 4.8 %pick.5 = bf16[64,2,2,16,512]{4,3,2,1,0:T(8,128)(2,1)} custom-call(s32[64,128]{1,0:T(8,128)S(1)} %get-tuple-element.34.plan, bf16[128,16,512]{2,1,0:T(8,128)(2,1)S(1)} %copy-done.12, bf16[128,16,512]{2,1,0:T(8,128)(2,1)S(1)} %copy-done.16, bf16[32,2,16,512]{3,2,1,0:T(8,128)(2,1)} %copy-done.20, bf16[32,2,16,512]{3,2,1,0:T(8,128)(2,1)} %collective-permute-done.3.above), custom_call_target="tpu_custom_call" | custom-call | tf_op jit(solution)/shard_map/cond/branch_1_fun/pick/pallas_call | solution.py:386
  60.8 0.0 copy-start.23
  60.9 0.0 copy-start.24
  60.9 0.0 copy-start.4
  60.9 0.0 copy-start.5
  60.9 0.0 copy-start.6
  60.9 0.0 copy-start.7
  61.0 5.8 %all-to-all-start.1 = ((bf16[64,2,2,16,512]{4,3,2,1,0:T(8,128)(2,1)}), bf16[64,2,2,16,512]{4,3,2,1,0:T(8,128)(2,1)}, u32[]{:S(2)}, u32[]{:S(2)}) async-start(bf16[64,2,2,16,512]{4,3,2,1,0:T(8,128)(2,1)} %get-tuple-element.78), calls=%async_computation.1 | async-start | bytes 8388608 | tf_op jit(solution)/shard_map/all_to_all | solution.py:411
  66.8 0.1 copy.19.places_col
  66.9 0.5 broadcast.4
  67.4 0.7 fusion.1
  68.1 0.1 reshape_squeeze.3.places_row
  68.2 0.3 fusion
  68.5 0.1 pad_maximum_fusion
  68.6 0.5 fresh.1
  69.2 1.0 copy-done.10
  70.1 44.3 %all-to-all-done.1 = bf16[64,2,2,16,512]{4,3,2,1,0:T(8,128)(2,1)} async-done(((bf16[64,2,2,16,512]{4,3,2,1,0:T(8,128)(2,1)}), bf16[64,2,2,16,512]{4,3,2,1,0:T(8,128)(2,1)}, u32[]{:S(2)}, u32[]{:S(2)}) %all-to-all-start.1) | async-done | bytes 4194336 | tf_op jit(solution)/shard_map/all_to_all | solution.py:411
  114.5 7.4 %prepare.1 = (bf16[4,2048,128]{2,1,0:T(8,128)(2,1)}, bf16[4,2048,128]{2,1,0:T(8,128)(2,1)}, f32[128,128]{1,0:T(8,128)}) custom-call(s32[2,8]{1,0:T(2,128)S(1)} %copy-done.9, s32[1,8]{1,0:T(1,128)S(1)} %copy-done.8, s32[8,16]{1,0:T(8,128)S(1)} %reshape_squeeze.3.places_row, s32[128,1]{1,0:T(8,128)S(1)} %copy.19.places_col, bf16[128,512]{1,0:T(8,128)(2,1)S(1)} %bitcast.18, ...), custom_call_target="tpu_custom_call" | custom-call | flops 134217728 | bytes 8388608 | tf_op jit(solution)/shard_map/prepare/pallas_call | solution.py:440
  121.9 11.9 %all-to-all-start.2 = ((f32[128,1,128]{2,1,0:T(1,128)}), f32[128,1,128]{2,1,0:T(1,128)S(1)}, u32[]{:S(2)}, u32[]{:S(2)}) async-start(f32[128,1,128]{2,1,0:T(1,128)} %bitcast.11), calls=%async_computation.2 | async-start | bytes 131072 | tf_op jit(solution)/shard_map/all_to_all | solution.py:476
  133.8 11.1 %attend.1 = bf16[128,4096]{1,0:T(8,128)(2,1)} custom-call(s32[128,1]{1,0:T(8,128)} %copy-done.2, bf16[32,128,128]{2,1,0:T(8,128)(2,1)} %copy-done.10, bf16[4,2048,128]{2,1,0:T(8,128)(2,1)} %get-tuple-element.68.all_keys, bf16[4,2048,128]{2,1,0:T(8,128)(2,1)} %get-tuple-element.69.all_vals), custom_call_target="tpu_custom_call" | custom-call | flops 4294967296 | bytes 6291456 | tf_op jit(solution)/shard_map/attend/pallas_call | solution.py:478
  144.9 0.7 reduce_sum.19
  (25 shorter events, 0.1 us)
Async XLA Ops:
  25.2 30.7 %copy-start.12 = (bf16[128,16,512]{2,1,0:T(8,128)(2,1)S(1)}, bf16[128,16,512]{2,1,0:T(8,128)(2,1)}, u32[]{:S(2)}) copy-start(bf16[128,16,512]{2,1,0:T(8,128)(2,1)} %get-tuple-element.35.keys) | copy-start | bytes 6291460 | tf_op jit(solution)/shard_map/cond
  25.3 30.7 %copy-start.16 = (bf16[128,16,512]{2,1,0:T(8,128)(2,1)S(1)}, bf16[128,16,512]{2,1,0:T(8,128)(2,1)}, u32[]{:S(2)}) copy-start(bf16[128,16,512]{2,1,0:T(8,128)(2,1)} %get-tuple-element.36.values) | copy-start | bytes 6291460 | tf_op jit(solution)/shard_map/cond
  31.0 24.0 %collective-permute-start.2 = (bf16[32,2,16,512]{3,2,1,0:T(8,128)(2,1)}, bf16[32,2,16,512]{3,2,1,0:T(8,128)(2,1)S(1)}, u32[]{:S(2)}, u32[]{:S(2)}) collective-permute-start(bf16[32,2,16,512]{3,2,1,0:T(8,128)(2,1)} %get-tuple-element.37), channel_id=1, source_target_pairs={{0,2},{2,4},{4,6},{6,0},{1,3},{3,5},{5,7},{7,1},{8,10},{10,12},{12... | collective-permute-start | bytes 3145736 | tf_op jit(solution)/shard_map/cond/branch_1_fun/ppermute | solution.py:384
  31.3 23.7 %collective-permute-start.3 = (bf16[32,2,16,512]{3,2,1,0:T(8,128)(2,1)}, bf16[32,2,16,512]{3,2,1,0:T(8,128)(2,1)}, u32[]{:S(2)}, u32[]{:S(2)}) collective-permute-start(bf16[32,2,16,512]{3,2,1,0:T(8,128)(2,1)} %get-tuple-element.38), channel_id=1, source_target_pairs={{0,6},{2,0},{4,2},{6,4},{1,7},{3,1},{5,3},{7,5},{8,14},{10,8},{12,... | collective-permute-start | bytes 3145736 | tf_op jit(solution)/shard_map/cond/branch_1_fun/ppermute | solution.py:385
  55.0 1.0 copy-start.20
  60.8 5.9 %copy-start.23 = (s32[1,128]{1,0:T(1,128)S(1)}, s32[1,128]{1,0:T(1,128)}, u32[]{:S(2)}) copy-start(s32[1,128]{1,0:T(1,128)} %param.21) | copy-start | bytes 1540
  60.9 7.3 %copy-start.24 = (f32[64]{0:T(128)S(1)}, f32[64]{0:T(128)}, u32[]{:S(2)}) copy-start(f32[64]{0:T(128)} %constant.24.clone) | copy-start | bytes 772
  60.9 7.7 %copy-start = (bf16[1,128,4096]{2,1,0:T(8,128)(2,1)S(1)}, bf16[1,128,4096]{2,1,0:T(8,128)(2,1)}, u32[]{:S(2)}) copy-start(bf16[1,128,4096]{2,1,0:T(8,128)(2,1)} %param.22) | copy-start | bytes 3145732
  60.9 7.7 %copy-start.1 = (bf16[1,128,512]{2,1,0:T(8,128)(2,1)S(1)}, bf16[1,128,512]{2,1,0:T(8,128)(2,1)}, u32[]{:S(2)}) copy-start(bf16[1,128,512]{2,1,0:T(8,128)(2,1)} %param.23) | copy-start | bytes 393220
  60.9 53.6 %copy-start.3 = (bf16[1,128,512]{2,1,0:T(8,128)(2,1)S(1)}, bf16[1,128,512]{2,1,0:T(8,128)(2,1)}, u32[]{:S(2)}) copy-start(bf16[1,128,512]{2,1,0:T(8,128)(2,1)} %param.24) | copy-start | bytes 393220
  60.9 53.6 %copy-start.4 = (f32[256,128]{1,0:T(8,128)S(1)}, f32[256,128]{1,0:T(8,128)}, u32[]{:S(2)}) copy-start(f32[256,128]{1,0:T(8,128)} %constant.27.clone.cos_token) | copy-start | bytes 393220
  60.9 53.5 %copy-start.5 = (f32[256,128]{1,0:T(8,128)S(1)}, f32[256,128]{1,0:T(8,128)}, u32[]{:S(2)}) copy-start(f32[256,128]{1,0:T(8,128)} %constant.28.clone.sin_token) | copy-start | bytes 393220
  60.9 53.5 %copy-start.6 = (f32[8,128]{1,0:T(8,128)S(1)}, f32[8,128]{1,0:T(8,128)}, u32[]{:S(2)}) copy-start(f32[8,128]{1,0:T(8,128)} %constant.25.clone.cos_span) | copy-start | bytes 12292
  60.9 53.5 %copy-start.7 = (f32[8,128]{1,0:T(8,128)S(1)}, f32[8,128]{1,0:T(8,128)}, u32[]{:S(2)}) copy-start(f32[8,128]{1,0:T(8,128)} %constant.26.clone.sin_span) | copy-start | bytes 12292
  61.0 53.5 %copy-start.8 = (s32[1,8]{1,0:T(1,128)S(1)}, s32[1,8]{1,0:T(1,128)}, u32[]{:S(2)}) copy-start(s32[1,8]{1,0:T(1,128)} %span_lists.3) | copy-start | bytes 100
  61.0 53.5 %copy-start.9 = (s32[2,8]{1,0:T(2,128)S(1)}, s32[2,8]{1,0:T(2,128)}, u32[]{:S(2)}) copy-start(s32[2,8]{1,0:T(2,128)} %get-tuple-element.66.place) | copy-start | bytes 196
  61.0 53.5 %all-to-all-start.1 = ((bf16[64,2,2,16,512]{4,3,2,1,0:T(8,128)(2,1)}), bf16[64,2,2,16,512]{4,3,2,1,0:T(8,128)(2,1)}, u32[]{:S(2)}, u32[]{:S(2)}) async-start(bf16[64,2,2,16,512]{4,3,2,1,0:T(8,128)(2,1)} %get-tuple-element.78), calls=%async_computation.1 | async-start | bytes 8388608 | tf_op jit(solution)/shard_map/all_to_all | solution.py:411
  66.9 66.9 %copy-start.2 = (s32[128,1]{1,0:T(8,128)}, s32[128,1]{1,0:T(8,128)S(1)}, u32[]{:S(2)}) copy-start(s32[128,1]{1,0:T(8,128)S(1)} %copy.19.places_col) | copy-start | bytes 1540
  69.2 1.0 copy-start.10
  121.9 23.0 %all-to-all-start.2 = ((f32[128,1,128]{2,1,0:T(1,128)}), f32[128,1,128]{2,1,0:T(1,128)S(1)}, u32[]{:S(2)}, u32[]{:S(2)}) async-start(f32[128,1,128]{2,1,0:T(1,128)} %bitcast.11), calls=%async_computation.2 | async-start | bytes 131072 | tf_op jit(solution)/shard_map/all_to_all | solution.py:476

commit v4 on v3

v4 whole, which is shorter than its diff:
```python
import functools

import jax
import jax.numpy as jnp
import numpy as np
from jax import lax
from jax.experimental import pallas as pl
from jax.experimental.pallas import tpu as pltpu
from jax.sharding import PartitionSpec as P

HD = 128
HALF = HD // 2
CPR = 8
RPC = 16
CL = 256
CTX = CPR * CL
RC = CPR * RPC
KVH = 8
BLOCKS = 4
SLOTS = CPR // BLOCKS
SIZES = (25, 29, 36)
KEPT, UP, DOWN, FROM_BELOW, FROM_ABOVE, LOADS = 0, 4, 8, 12, 13, 16
LANES = 128
SCALE_LOG2E = float(HD ** -0.5 * np.log2(np.e))

FREQ = np.exp(-np.log(500000.0) * np.arange(HALF) / HALF).astype(np.float32)


def angle_tables(positions):
    angles = positions[:, None].astype(np.float64) * FREQ[None, :].astype(np.float64)
    cosine = np.cos(angles).astype(np.float32)
    sine = np.sin(angles).astype(np.float32)
    return (
        np.concatenate([cosine, cosine], axis=1),
        np.concatenate([-sine, sine], axis=1),
    )


COS_SPAN, SIN_SPAN = angle_tables(CL * np.arange(CPR))
COS_TOKEN, SIN_TOKEN = angle_tables(np.arange(CL))


def turn(x, cosine, sine):
    return x * cosine + pltpu.roll(x, HALF, 1) * sine


def ask_kernel(shard_rows, span_row, span_lists, plan, place):
    spans = [span_row[span_lists[0, j]] for j in range(CPR)]
    homes = [row // shard_rows for row in spans]
    rows = [row % shard_rows for row in spans]
    one = [[jnp.where(home == k, 1, 0) for home in homes] for k in range(BLOCKS)]
    counts = [sum(one[k]) for k in range(BLOCKS)]
    sums = []
    total = jnp.int32(0)
    for k in range(BLOCKS):
        total = total + counts[k] - SLOTS
        sums.append(total)
    low, high = jnp.minimum(sums[0], sums[1]), jnp.maximum(sums[0], sums[1])
    low2, high2 = jnp.minimum(sums[2], sums[3]), jnp.maximum(sums[2], sums[3])
    middle, middle2 = jnp.maximum(low, low2), jnp.minimum(high, high2)
    first, second = jnp.minimum(middle, middle2), jnp.maximum(middle, middle2)
    whole = sums[0] + sums[1] + sums[2] + sums[3]
    mixed = lax.rem(sum(span_lists[0, j] for j in range(CPR)), 4) == 0
    level = jnp.abs(whole - BLOCKS * first) <= jnp.abs(whole - BLOCKS * second)
    shift = jnp.where(level != mixed, first, second)
    flow = [x - shift for x in sums]
    up = [jnp.maximum(x, 0) for x in flow]
    down = [jnp.maximum(-flow[k - 1], 0) for k in range(BLOCKS)]
    keep = [counts[k] - up[k] - down[k] for k in range(BLOCKS)]

    block = lax.broadcasted_iota(jnp.int32, plan.shape, 0) % BLOCKS
    lane = lax.broadcasted_iota(jnp.int32, plan.shape, 1)
    out = jnp.zeros(plan.shape, jnp.int32)
    for k in range(BLOCKS):
        own = block == k
        heads = (
            (KEPT, keep[k]),
            (UP, up[k]),
            (DOWN, down[k]),
            (FROM_BELOW, up[k - 1]),
            (FROM_ABOVE, down[(k + 1) % BLOCKS]),
        )
        for at, value in heads:
            out = jnp.where(own & (lane == at), value, out)
        out = jnp.where(lane == LOADS + k, up[k], out)
        out = jnp.where(lane == LOADS + BLOCKS + k, down[k], out)

    def of(table, k):
        value = table[0]
        for i in range(1, BLOCKS):
            value = jnp.where(k == i, table[i], value)
        return value

    base_below = [keep[k] for k in range(BLOCKS)]
    base_above = [keep[k] + up[k - 1] for k in range(BLOCKS)]
    for j in range(CPR):
        home = homes[j]
        rank = jnp.int32(0)
        for i in range(j):
            rank = rank + jnp.where(homes[i] == home, 1, 0)
        kept = of(keep, home)
        after = rank - kept
        ups = of(up, home)
        stays = after < 0
        climbs = after < ups
        at = jnp.where(
            stays, KEPT + 1 + rank, jnp.where(climbs, UP + 1 + after, DOWN + 1 + after - ups)
        )
        out = jnp.where((block == home) & (lane == at), rows[j], out)
        above = lax.rem(home + 1, BLOCKS)
        below = lax.rem(home + BLOCKS - 1, BLOCKS)
        place[0, j] = jnp.where(stays, home, jnp.where(climbs, above, below))
        place[1, j] = jnp.where(
            stays,
            rank,
            jnp.where(climbs, of(base_below, above) + after, of(base_above, below) + after - ups),
        )
    plan[...] = out


def move_kernel(size, plan, table, up_out, down_out, rows, up_stage, down_stage, sems):
    load = pltpu.make_async_copy(table, rows, sems.at[0])
    load.start()
    load.wait()

    def fill(r, marks):
        ends = []
        for at, stage, mark in ((UP, up_stage, marks[0]), (DOWN, down_stage, marks[1])):
            for i in range(SLOTS):
                stage[mark + i] = rows[plan[r, at + 1 + i]]
            ends.append(mark + plan[r, at])
        return tuple(ends)

    lax.fori_loop(0, plan.shape[0], fill, (jnp.int32(0), jnp.int32(0)), unroll=4)
    stores = [
        pltpu.make_async_copy(stage.at[pl.ds(0, size)], out, sems.at[i])
        for i, (stage, out) in enumerate(((up_stage, up_out), (down_stage, down_out)))
    ]
    for store in stores:
        store.start()
    for store in stores:
        store.wait()


def own_kernel(plan, keys, values, send, pool, stage, sems, out_sem):
    loads = [
        pltpu.make_async_copy(table, pool.at[i], sems.at[i])
        for i, table in enumerate((keys, values))
    ]
    for load in loads:
        load.start()
    for load in loads:
        load.wait()

    def fill(r, carry):
        for t in range(SLOTS):
            row = plan[r, KEPT + 1 + t]
            stage[r, t, 0] = pool[0, row]
            stage[r, t, 1] = pool[1, row]
        pltpu.make_async_copy(stage.at[r], send.at[r], out_sem).start()
        return carry

    lax.fori_loop(0, send.shape[0], fill, 0, unroll=4)
    pltpu.make_async_copy(stage, send, out_sem).wait()


def patch_kernel(plan, below_k, above_k, below_v, above_v, own, send, sem):
    def fill(r, marks):
        kept = plan[r, KEPT]
        second = kept + plan[r, FROM_BELOW]
        for t in range(SLOTS):

            @pl.when((t >= kept) & (t < second))
            def _():
                row = marks[0] + t - kept
                pltpu.make_async_copy(below_k.at[row], send.at[r, t, 0], sem).start()
                pltpu.make_async_copy(below_v.at[row], send.at[r, t, 1], sem).start()

            @pl.when(t >= second)
            def _():
                row = marks[1] + t - second
                pltpu.make_async_copy(above_k.at[row], send.at[r, t, 0], sem).start()
                pltpu.make_async_copy(above_v.at[row], send.at[r, t, 1], sem).start()

        return marks[0] + plan[r, FROM_BELOW], marks[1] + plan[r, FROM_ABOVE]

    ends = lax.fori_loop(0, send.shape[0], fill, (jnp.int32(0), jnp.int32(0)), unroll=4)

    def drain(i, carry):
        pltpu.make_async_copy(send.at[0, 0], send.at[0, 0], sem).wait()
        return carry

    lax.fori_loop(0, ends[0] + ends[1], drain, 0)


def fresh_kernel(heads_kv, group, q, k, cosine, sine, q_out, k_out):
    cos = cosine[...]
    sin = sine[...]
    for h in range(heads_kv):
        cols = slice(h * HD, (h + 1) * HD)
        k_out[:, cols] = turn(k[:, cols].astype(jnp.float32), cos, sin).astype(jnp.bfloat16)
        for g in range(group):
            n = h * group + g
            turned = turn(q[:, n * HD : (n + 1) * HD].astype(jnp.float32), cos, sin)
            turned = turned.astype(jnp.bfloat16)
            for j in range(CPR):
                q_out[h * CPR + j, g * RPC : (g + 1) * RPC, :] = turned[j * RPC : (j + 1) * RPC]


def drift_kernel(
    total_spans, place, span_lists, places_col, fresh_k, fresh_v, got, drift, kbuf, vbuf, sems
):
    copies = []
    for j in range(CPR):
        for which, buf in enumerate((kbuf, vbuf)):
            copy = pltpu.make_async_copy(
                got.at[:, place[0, j], place[1, j], which], buf.at[j], sems.at[which, j]
            )
            copy.start()
            copies.append(copy)
    width = fresh_k.shape[1]
    dest = lax.broadcasted_iota(jnp.int32, drift.shape, 0)
    lane = lax.broadcasted_iota(jnp.int32, drift.shape, 1)
    per_dest = total_spans // drift.shape[0]
    token = lax.broadcasted_iota(jnp.int32, (RPC, CL), 1)
    total = jnp.zeros(drift.shape, jnp.float32)
    for j in range(CPR):
        rows = slice(j * RPC, (j + 1) * RPC)
        take = (token + j * CL == places_col[rows, :]).astype(jnp.float32)
        take = take.astype(jnp.bfloat16)
        gap = jnp.zeros((RPC, width), jnp.float32)
        copies[2 * j].wait()
        copies[2 * j + 1].wait()
        for buf, fresh in ((kbuf, fresh_k), (vbuf, fresh_v)):
            cached = jnp.dot(take, buf[j].reshape(CL, width), preferred_element_type=jnp.float32)
            delta = fresh[rows, :].astype(jnp.float32) - cached
            gap = gap + delta * delta
        share = jnp.sum(gap) * (1.0 / (2.0 * KVH * HD * RPC))
        chosen = span_lists[0, j]
        total = total + jnp.where(
            (dest == chosen // per_dest) & (lane == chosen % per_dest), share, 0.0
        )
    drift[...] = total


def attend_kernel(
    heads_kv,
    group,
    place,
    places_row,
    places_col,
    q,
    new_k,
    new_v,
    cos_span,
    sin_span,
    cos_token,
    sin_token,
    got,
    out,
    raw,
    keys,
    vals,
    seen,
    put,
    stay,
    cosine,
    sine,
    scores,
    sems,
):
    def loads(h, slot):
        cols = pl.ds(pl.multiple_of(h * HD, HD), HD)
        return [
            pltpu.make_async_copy(
                got.at[:, place[0, j], place[1, j], which, :, cols],
                raw.at[slot, which, j],
                sems.at[slot],
            )
            for which in range(2)
            for j in range(CPR)
        ]

    for load in loads(0, 0):
        load.start()
    block = group * RPC
    token_lane = lax.broadcasted_iota(jnp.int32, (RPC, CL), 1)
    token_row = lax.broadcasted_iota(jnp.int32, (CL, RPC), 0)
    ones = jnp.ones((RPC, HD), jnp.bfloat16)
    for j in range(CPR):
        rows = slice(j * RPC, (j + 1) * RPC)
        span = slice(j * CL, (j + 1) * CL)
        seen[j] = jnp.where(token_lane + j * CL <= places_col[rows, :], 0.0, -1e30)
        hits = (token_row + j * CL == places_row[j : j + 1, :]).astype(jnp.float32)
        hits = hits.astype(jnp.bfloat16)
        put[j] = hits
        stay[span, :] = 1.0 - jnp.dot(hits, ones, preferred_element_type=jnp.float32)
        ca, sa = cos_span[j : j + 1, :], sin_span[j : j + 1, :]
        cb, sb = cos_token[...], sin_token[...]
        cosine[span, :] = ca * cb - sa * sb
        sine[span, :] = sa * cb + ca * sb

    def head(h, carry):
        slot = lax.rem(h, 2)
        cols = pl.ds(pl.multiple_of(h * HD, HD), HD)
        pltpu.make_async_copy(raw.at[slot], raw.at[slot], sems.at[slot]).wait()

        @pl.when(h + 1 < heads_kv)
        def _():
            for load in loads(h + 1, 1 - slot):
                load.start()

        for j in range(CPR):
            rows = slice(j * RPC, (j + 1) * RPC)
            span = slice(j * CL, (j + 1) * CL)
            old = raw[slot, 0, j].reshape(CL, HD).astype(jnp.float32)
            new = jnp.dot(put[j], new_k[rows, cols], preferred_element_type=jnp.float32)
            old = turn(old, cosine[span, :], sine[span, :])
            keys[span, :] = (old * stay[span, :] + new).astype(jnp.bfloat16)
            old = raw[slot, 1, j].reshape(CL, HD).astype(jnp.float32)
            new = jnp.dot(put[j], new_v[rows, cols], preferred_element_type=jnp.float32)
            vals[span, :] = (old * stay[span, :] + new).astype(jnp.bfloat16)
        for t in range(CPR):
            later = q[pl.ds(h * CPR + t, CPR - t)].reshape((CPR - t) * block, HD)
            scores[t * block :, t * CL : (t + 1) * CL] = lax.dot_general(
                later,
                keys[t * CL : (t + 1) * CL, :],
                (((1,), (1,)), ((), ())),
                preferred_element_type=jnp.float32,
            )
        for j in range(CPR):
            extent = (j + 1) * CL
            part = scores[j * block : (j + 1) * block, :extent]
            bias = jnp.concatenate([seen[j]] * group, axis=0)
            last = part[:, j * CL :] + bias
            part = last if j == 0 else jnp.concatenate([part[:, : j * CL], last], axis=1)
            row_max = jnp.max(part, axis=1, keepdims=True)
            weights = jnp.exp2((part - row_max) * SCALE_LOG2E)
            row_sum = jnp.sum(weights, axis=1, keepdims=True)
            mixed = jnp.dot(
                weights.astype(jnp.bfloat16),
                vals[:extent, :],
                preferred_element_type=jnp.float32,
            )
            mixed = (mixed / row_sum).astype(jnp.bfloat16)
            for g in range(group):
                start = pl.multiple_of((h * group + g) * HD, HD)
                out[j * RPC : (j + 1) * RPC, pl.ds(start, HD)] = mixed[g * RPC : (g + 1) * RPC]
        return carry

    lax.fori_loop(0, heads_kv, head, 0)


SMEM = pl.BlockSpec(memory_space=pltpu.SMEM)
VMEM = pl.BlockSpec(memory_space=pltpu.VMEM)
ANY = pl.BlockSpec(memory_space=pl.ANY)


def local(span_keys, span_values, span_row, span_lists, recompute_pos, fresh_q, fresh_k, fresh_v):
    n_store = lax.axis_size("store")
    n_req = lax.axis_size("req")
    n_tp = lax.axis_size("tp")
    n_all = n_store * n_req * n_tp
    peers = n_store * n_req
    shard_rows, tok_dev, width = span_keys.shape
    heads_kv = width // HD
    heads_q = fresh_q.shape[2] // HD
    group = heads_q // heads_kv
    bf16 = jnp.bfloat16

    def params(mebibytes):
        return pltpu.CompilerParams(vmem_limit_bytes=mebibytes << 20)


    assert n_req == BLOCKS and shard_rows * n_req == span_row.shape[0]
    plan, place = pl.pallas_call(
        functools.partial(ask_kernel, shard_rows),
        out_shape=(
            jax.ShapeDtypeStruct((peers, LANES), jnp.int32),
            jax.ShapeDtypeStruct((2, CPR), jnp.int32),
        ),
        in_specs=[SMEM, SMEM],
        out_specs=(VMEM, SMEM),
        name="ask",
    )(span_row, span_lists)
    plans = lax.all_to_all(plan, ("store", "req"), split_axis=0, concat_axis=0, tiled=True)
    piece = (2, tok_dev, width)
    climb = [(k, (k + 1) % n_req) for k in range(n_req)]
    sink = [(k, (k - 1) % n_req) for k in range(n_req)]

    def gather(size, plans, span_keys, span_values):
        moves = jax.ShapeDtypeStruct((size, tok_dev, width), bf16)
        move = pl.pallas_call(
            functools.partial(move_kernel, size),
            out_shape=(moves, moves),
            in_specs=[SMEM, ANY],
            out_specs=(ANY, ANY),
            scratch_shapes=[
                pltpu.VMEM((shard_rows, tok_dev, width), bf16),
                pltpu.VMEM((size + SLOTS, tok_dev, width), bf16),
                pltpu.VMEM((size + SLOTS, tok_dev, width), bf16),
                pltpu.SemaphoreType.DMA((2,)),
            ],
            compiler_params=params(60),
            name="move",
        )
        came = []
        for table in (span_keys, span_values):
            ups, downs = move(plans, table)
            came.append(lax.ppermute(ups, "req", climb))
            came.append(lax.ppermute(downs, "req", sink))
            plans, span_keys, span_values, _ = lax.optimization_barrier(
                (plans, span_keys, span_values, ups)
            )
        own = pl.pallas_call(
            own_kernel,
            out_shape=jax.ShapeDtypeStruct((peers, SLOTS) + piece, bf16),
            in_specs=[SMEM, ANY, ANY],
            out_specs=ANY,
            scratch_shapes=[
                pltpu.VMEM((2, shard_rows, tok_dev, width), bf16),
                pltpu.VMEM((peers, SLOTS) + piece, bf16),
                pltpu.SemaphoreType.DMA((2,)),
                pltpu.SemaphoreType.DMA,
            ],
            compiler_params=params(58),
            name="own",
        )(plans, span_keys, span_values)
        return pl.pallas_call(
            patch_kernel,
            out_shape=jax.ShapeDtypeStruct((peers, SLOTS) + piece, bf16),
            in_specs=[SMEM] + [VMEM] * 4 + [ANY],
            out_specs=ANY,
            scratch_shapes=[pltpu.SemaphoreType.DMA],
            input_output_aliases={5: 0},
            compiler_params=params(40),
            name="patch",
        )(plans, *came, own)

    load = jnp.max(jnp.sum(plans[:, LOADS : LOADS + 2 * BLOCKS], axis=0))
    level = sum((load > size).astype(jnp.int32) for size in SIZES)
    most = SLOTS * peers
    send = lax.switch(
        level,
        [functools.partial(gather, size) for size in SIZES + (most,)],
        plans,
        span_keys,
        span_values,
    )
    got = lax.all_to_all(send, ("store", "req"), split_axis=0, concat_axis=0, tiled=True)
    got = got.reshape((n_store, n_req, SLOTS) + piece)

    places, raw_q, raw_k, _ = lax.optimization_barrier((recompute_pos, fresh_q, fresh_k, send))
    places = places[0]
    raw_k = raw_k[0]
    new_v = fresh_v[0]
    angles = places.astype(jnp.float32)[:, None] * jnp.asarray(FREQ)[None, :]
    cosine = jnp.cos(angles)
    sine = jnp.sin(angles)
    queries, new_k = pl.pallas_call(
        functools.partial(fresh_kernel, heads_kv, group),
        out_shape=(
            jax.ShapeDtypeStruct((heads_kv * CPR, group * RPC, HD), bf16),
            jax.ShapeDtypeStruct((RC, width), bf16),
        ),
        in_specs=[VMEM] * 4,
        out_specs=(VMEM, VMEM),
        compiler_params=params(16),
        name="fresh",
    )(
        raw_q[0],
        raw_k,
        jnp.concatenate([cosine, cosine], axis=1),
        jnp.concatenate([-sine, sine], axis=1),
    )
    places_col = places[:, None]
    places_row = places.reshape(CPR, RPC)

    part = pl.pallas_call(
        functools.partial(drift_kernel, span_row.shape[0]),
        out_shape=jax.ShapeDtypeStruct((n_all, LANES), jnp.float32),
        in_specs=[SMEM, SMEM, VMEM, VMEM, VMEM, ANY],
        out_specs=VMEM,
        scratch_shapes=[
            pltpu.VMEM((CPR, n_store, tok_dev, width), bf16),
            pltpu.VMEM((CPR, n_store, tok_dev, width), bf16),
            pltpu.SemaphoreType.DMA((2, CPR)),
        ],
        compiler_params=params(58),
        cost_estimate=pl.CostEstimate(
            flops=4 * RC * CL * width, bytes_accessed=4 * CTX * width, transcendentals=0
        ),
        name="drift",
    )(place, span_lists, places_col, raw_k, new_v, got)
    parts = lax.all_to_all(part, ("store", "req", "tp"), split_axis=0, concat_axis=0, tiled=True)

    attended = pl.pallas_call(
        functools.partial(attend_kernel, heads_kv, group),
        out_shape=jax.ShapeDtypeStruct((RC, heads_q * HD), bf16),
        in_specs=[SMEM] + [VMEM] * 9 + [ANY],
        out_specs=VMEM,
        scratch_shapes=[
            pltpu.VMEM((2, 2, CPR, n_store, tok_dev, HD), bf16),
            pltpu.VMEM((CTX, HD), bf16),
            pltpu.VMEM((CTX, HD), bf16),
            pltpu.VMEM((CPR, RPC, CL), jnp.float32),
            pltpu.VMEM((CPR, CL, RPC), bf16),
            pltpu.VMEM((CTX, HD), jnp.float32),
            pltpu.VMEM((CTX, HD), jnp.float32),
            pltpu.VMEM((CTX, HD), jnp.float32),
            pltpu.VMEM((CPR * group * RPC, CTX), jnp.float32),
            pltpu.SemaphoreType.DMA((2,)),
        ],
        compiler_params=params(58),
        cost_estimate=pl.CostEstimate(
            flops=2 * heads_q * RC * CTX * HD * 2,
            bytes_accessed=4 * CTX * width + 4 * RC * heads_q * HD,
            transcendentals=heads_q * RC * CTX // 2,
        ),
        name="attend",
    )(
        place,
        places_row,
        places_col,
        queries,
        new_k,
        new_v,
        jnp.asarray(COS_SPAN),
        jnp.asarray(SIN_SPAN),
        jnp.asarray(COS_TOKEN),
        jnp.asarray(SIN_TOKEN),
        got,
    )
    per_dest = span_row.shape[0] // n_all
    drift_part = jnp.sum(parts, axis=0)[:per_dest]
    return (attended[None], drift_part)


def solution(mesh):
    in_specs = (
        P("req", "store", "tp"),
        P("req", "store", "tp"),
        P(),
        P(("store", "req"), None),
        P(("store", "req"), None),
        P(("store", "req"), None, "tp"),
        P(("store", "req"), None, "tp"),
        P(("store", "req"), None, "tp"),
    )
    out_specs = (P(("store", "req"), None, "tp"), P(("store", "req", "tp")))
    return jax.shard_map(local, mesh=mesh, in_specs=in_specs, out_specs=out_specs, check_vma=False)
```

time: 146 us -> 139 us (0.952)
  waiting for transfers between devices: 65.6 us -> 49.6 us
  Pallas kernels: 31.1 us -> 36.4 us
  starting transfers between devices: 20.4 us -> 23.7 us
    ppermute x2 -> x4, waiting for transfers between devices: 21.3 us -> 5.56 us  [the longest x2 5.56 us: gather(): came.append(lax.ppermute(ups, 'req', climb))]
    pallas_call x3 -> x5, Pallas kernels: 17.9 us -> 21.3 us  [the longest x2 8.4 us: gather(): ups, downs = move(plans, table)]
    ppermute x2 -> x4, starting transfers between devices: 2.75 us -> 5.48 us  [the longest x2 5.05 us: gather(): came.append(lax.ppermute(downs, 'req', sink))]
    pallas_call x1, Pallas kernels: 11.1 us -> 13 us  [local(): pl.pallas_call(functools.partial(attend_kernel, heads_kv, group), out_sha...]
  transfers between devices with their start and end apart: 4 -> 6, of which waited for: 2 -> 2; matrix products, arithmetic and copies ran while one was open for 1% -> 2% of each run, Pallas kernels for 8% -> 16%
where the time goes in v4:
time: 139 us
  waiting for transfers between devices  49.6 us (36%)
  Pallas kernels  36.4 us (26%)
  starting transfers between devices  23.7 us (17%)
  blocking collectives  20.3 us (15%)
  local copies, waits for them, and re-layouts  3.62 us (3%)
  between operations  2.72 us (2%)
  other arithmetic  2.46 us (2%)
    all_to_all x1, waiting for transfers between devices, local(): lax.all_to_all(send, ('store', 'req'), split_axis=0, concat_axis=0, tiled...  44 us
    all_to_all x1, blocking collectives, local(): lax.all_to_all(plan, ('store', 'req'), split_axis=0, concat_axis=0, tiled...  20.3 us
    pallas_call x1, Pallas kernels, local(): pl.pallas_call(functools.partial(attend_kernel, heads_kv, group), out_sha...  13 us
    all_to_all x1, starting transfers between devices, local(): lax.all_to_all(part, ('store', 'req', 'tp'), split_axis=0, concat_axis=0,...  11.4 us
    pallas_call x2, Pallas kernels, gather(): ups, downs = move(plans, table)  8.4 us
    all_to_all x1, starting transfers between devices, local(): lax.all_to_all(send, ('store', 'req'), split_axis=0, concat_axis=0, tiled...  6.82 us
    ppermute x2, waiting for transfers between devices, gather(): came.append(lax.ppermute(ups, 'req', climb))  5.56 us
    pallas_call x1, Pallas kernels, local(): pl.pallas_call(functools.partial(drift_kernel, span_row.shape[0]), out_sh...  5.33 us
  transfers between devices with their start and end apart: 6, of which 2 were waited for; matrix products, arithmetic and copies ran while one was open for 2% of the time, Pallas kernels for 16%

profile of v4, /device:TPU:1, one launch (start us, length us, event | category | flops | bytes accessed | tf_op | source)
XLA Modules:
  0.0 138.9 jit_solution(12526704530895976238)
XLA Ops:
  0.6 1.6 %ask.1 = (s32[64,128]{1,0:T(8,128)}, s32[2,8]{1,0:T(2,128)}) custom-call(s32[512]{0:T(512)} %span_row.1, s32[1,8]{1,0:T(1,128)} %span_lists.3), custom_call_target="tpu_custom_call" | custom-call | tf_op jit(solution)/shard_map/ask/pallas_call | solution.py:376
  2.3 20.3 %all_to_all.26 = s32[64,1,128]{2,1,0:T(1,128)S(1)} all-to-all(s32[64,1,128]{2,1,0:T(1,128)} %bitcast.27), channel_id=1, replica_groups=mesh['store'=16,'req'=4,'tp'=2] {'store','req'}, dimensions={0} | all-to-all | bytes 65536 | tf_op jit(solution)/shard_map/all_to_all | solution.py:386
  22.6 0.1 slice_reduce_fusion
  22.7 0.6 reduce_max.9
  25.2 27.1 %conditional.1 = (bf16[64,2,2,16,512]{4,3,2,1,0:T(8,128)(2,1)}) conditional(s32[]{:T(128)} %clamp.3, (s32[64,128]{1,0:T(8,128)S(1)}, bf16[128,16,512]{2,1,0:T(8,128)(2,1)}, bf16[128,16,512]{2,1,0:T(8,128)(2,1)}) %tuple.40, (s32[64,128]{1,0:T(8,128)S(1)}, bf16[128,16,512]{2,1,0:T(8,128)(2,1)}, ...), branch_computations={%region_2.0_spmd, %region_3.0_spmd, %region_4.0_spmd, %region_5.0_... | conditional | bytes 33554600 | solution.py:443
  25.3 0.0 copy-start.4
  25.3 4.2 %move.8 = (bf16[25,16,512]{2,1,0:T(8,128)(2,1)}, bf16[25,16,512]{2,1,0:T(8,128)(2,1)}) custom-call(s32[64,128]{1,0:T(8,128)S(1)} %get-tuple-element.37.plan, bf16[128,16,512]{2,1,0:T(8,128)(2,1)} %get-tuple-element.40.table.keys), custom_call_target="tpu_custom_call" | custom-call | tf_op jit(solution)/shard_map/cond/branch_0_fun/move/pallas_call | solution.py:409
  29.5 0.4 collective-permute-start
  29.8 2.4 %collective-permute-start.1 = (bf16[25,16,512]{2,1,0:T(8,128)(2,1)}, bf16[25,16,512]{2,1,0:T(8,128)(2,1)S(1)}, u32[]{:S(2)}, u32[]{:S(2)}) collective-permute-start(bf16[25,16,512]{2,1,0:T(8,128)(2,1)} %get-tuple-element.38), channel_id=1, source_target_pairs={{0,6},{2,0},{4,2},{6,4},{1,7},{3,1},{5,3},{7,5},{8,14},{10,8},{12,... | collective-permute-start | bytes 1228808 | tf_op jit(solution)/shard_map/cond/branch_0_fun/ppermute | solution.py:411
  32.2 4.2 %move.9 = (bf16[25,16,512]{2,1,0:T(8,128)(2,1)}, bf16[25,16,512]{2,1,0:T(8,128)(2,1)}) custom-call(s32[64,128]{1,0:T(8,128)S(1)} %get-tuple-element.37.plan, bf16[128,16,512]{2,1,0:T(8,128)(2,1)} %get-tuple-element.41.table.values), custom_call_target="tpu_custom_call" | custom-call | tf_op jit(solution)/shard_map/cond/branch_0_fun/move/pallas_call | solution.py:409
  36.4 0.1 collective-permute-start.2
  36.5 2.7 %collective-permute-start.3 = (bf16[25,16,512]{2,1,0:T(8,128)(2,1)}, bf16[25,16,512]{2,1,0:T(8,128)(2,1)S(1)}, u32[]{:S(2)}, u32[]{:S(2)}) collective-permute-start(bf16[25,16,512]{2,1,0:T(8,128)(2,1)} %get-tuple-element.39), channel_id=1, source_target_pairs={{0,6},{2,0},{4,2},{6,4},{1,7},{3,1},{5,3},{7,5},{8,14},{10,8},{12,... | collective-permute-start | bytes 1228808 | tf_op jit(solution)/shard_map/cond/branch_0_fun/ppermute | solution.py:411
  39.2 4.7 %own.4 = bf16[64,2,2,16,512]{4,3,2,1,0:T(8,128)(2,1)} custom-call(s32[64,128]{1,0:T(8,128)S(1)} %get-tuple-element.37.plan, bf16[128,16,512]{2,1,0:T(8,128)(2,1)} %get-tuple-element.40.table.keys, bf16[128,16,512]{2,1,0:T(8,128)(2,1)S(1)} %copy-done.4), custom_call_target="tpu_custom_call" | custom-call | tf_op jit(solution)/shard_map/cond/branch_0_fun/own/pallas_call | solution.py:415
  43.9 5.6 %collective-permute-done.2.below_v = bf16[25,16,512]{2,1,0:T(8,128)(2,1)S(1)} collective-permute-done((bf16[25,16,512]{2,1,0:T(8,128)(2,1)}, bf16[25,16,512]{2,1,0:T(8,128)(2,1)S(1)}, u32[]{:S(2)}, u32[]{:S(2)}) %collective-permute-start.2) | collective-permute-done | bytes 409632 | tf_op jit(solution)/shard_map/cond/branch_0_fun/ppermute | solution.py:410
  49.5 2.8 %patch.4 = bf16[64,2,2,16,512]{4,3,2,1,0:T(8,128)(2,1)} custom-call(s32[64,128]{1,0:T(8,128)S(1)} %get-tuple-element.37.plan, bf16[25,16,512]{2,1,0:T(8,128)(2,1)S(1)} %collective-permute-done.below_k, bf16[25,16,512]{2,1,0:T(8,128)(2,1)S(1)} %collective-permute-done.1.above_k, ...), custom_call_target="tpu_custom_call", output_to_operand_aliasing={{}: (5, {})} | custom-call | tf_op jit(solution)/shard_map/cond/branch_0_fun/patch/pallas_call | solution.py:429
  52.4 0.0 copy-start.8
  52.4 0.0 copy-start.1
  52.4 6.8 %all-to-all-start.1 = ((bf16[64,2,2,16,512]{4,3,2,1,0:T(8,128)(2,1)}), bf16[64,2,2,16,512]{4,3,2,1,0:T(8,128)(2,1)}, u32[]{:S(2)}, u32[]{:S(2)}) async-start(bf16[64,2,2,16,512]{4,3,2,1,0:T(8,128)(2,1)} %get-tuple-element.104), calls=%async_computation.1 | async-start | bytes 8388608 | tf_op jit(solution)/shard_map/all_to_all | solution.py:450
  59.2 0.5 broadcast.4
  59.7 0.7 convert_bitcast_fusion
  60.4 0.7 reshape_squeeze.3.places_row
  61.1 0.7 copy.22.places_col
  61.8 0.3 fusion
  62.1 0.1 pad_maximum_fusion
  62.3 0.5 fresh.1
  62.8 1.0 copy-done.2
  63.8 0.6 copy-done.3
  64.5 44.0 %all-to-all-done.1 = bf16[64,2,2,16,512]{4,3,2,1,0:T(8,128)(2,1)} async-done(((bf16[64,2,2,16,512]{4,3,2,1,0:T(8,128)(2,1)}), bf16[64,2,2,16,512]{4,3,2,1,0:T(8,128)(2,1)}, u32[]{:S(2)}, u32[]{:S(2)}) %all-to-all-start.1) | async-done | bytes 4194336 | tf_op jit(solution)/shard_map/all_to_all | solution.py:450
  108.5 5.3 %drift.1 = f32[128,128]{1,0:T(8,128)} custom-call(s32[2,8]{1,0:T(2,128)} %get-tuple-element.90.place, s32[1,8]{1,0:T(1,128)} %span_lists.3, s32[128,1]{1,0:T(8,128)} %copy.22.places_col, bf16[128,512]{1,0:T(8,128)(2,1)} %bitcast.17, bf16[128,512]{1,0:T(8,128)(2,1)} %bitcast.25, bf16[16,4,2,2,16,512]{5,4,3,2,1,0:T(8,128)(2,1)} %bitcast.8.got), custom_call_target="tpu_custom_call" | custom-call | flops 67108864 | bytes 4194304 | tf_op jit(solution)/shard_map/drift/pallas_call | solution.py:479
  113.8 11.4 %all-to-all-start.2 = ((f32[128,1,128]{2,1,0:T(1,128)}), f32[128,1,128]{2,1,0:T(1,128)S(1)}, u32[]{:S(2)}, u32[]{:S(2)}) async-start(f32[128,1,128]{2,1,0:T(1,128)} %bitcast.24), calls=%async_computation.2 | async-start | bytes 131072 | tf_op jit(solution)/shard_map/all_to_all | solution.py:495
  125.2 13.0 %attend.1 = bf16[128,4096]{1,0:T(8,128)(2,1)} custom-call(s32[2,8]{1,0:T(2,128)} %get-tuple-element.90.place, s32[8,16]{1,0:T(8,128)} %reshape_squeeze.3.places_row, s32[128,1]{1,0:T(8,128)} %copy.22.places_col, bf16[32,128,128]{2,1,0:T(8,128)(2,1)} %copy-done.2, bf16[128,512]{1,0:T(8,128)(2,1)} %copy-done.3, bf16[128,512]{1,0:T(8,128)(2,1)} %bitcast.26, ...), custom_call_target="tpu_custom_call" | custom-call | flops 4294967296 | bytes 6291456 | tf_op jit(solution)/shard_map/attend/pallas_call | solution.py:497
  138.2 0.7 reduce_sum.19
  (13 shorter events, 0.0 us)
Async XLA Ops:
  25.3 13.9 %copy-start.4 = (bf16[128,16,512]{2,1,0:T(8,128)(2,1)S(1)}, bf16[128,16,512]{2,1,0:T(8,128)(2,1)}, u32[]{:S(2)}) copy-start(bf16[128,16,512]{2,1,0:T(8,128)(2,1)} %get-tuple-element.41.table.values) | copy-start | bytes 6291460 | tf_op jit(solution)/shard_map/cond
  29.5 14.4 %collective-permute-start = (bf16[25,16,512]{2,1,0:T(8,128)(2,1)}, bf16[25,16,512]{2,1,0:T(8,128)(2,1)S(1)}, u32[]{:S(2)}, u32[]{:S(2)}) collective-permute-start(bf16[25,16,512]{2,1,0:T(8,128)(2,1)} %get-tuple-element.32), channel_id=1, source_target_pairs={{0,2},{2,4},{4,6},{6,0},{1,3},{3,5},{5,7},{7,1},{8,10},{10,12},{12... | collective-permute-start | bytes 1228808 | tf_op jit(solution)/shard_map/cond/branch_0_fun/ppermute | solution.py:410
  29.8 14.1 %collective-permute-start.1 = (bf16[25,16,512]{2,1,0:T(8,128)(2,1)}, bf16[25,16,512]{2,1,0:T(8,128)(2,1)S(1)}, u32[]{:S(2)}, u32[]{:S(2)}) collective-permute-start(bf16[25,16,512]{2,1,0:T(8,128)(2,1)} %get-tuple-element.38), channel_id=1, source_target_pairs={{0,6},{2,0},{4,2},{6,4},{1,7},{3,1},{5,3},{7,5},{8,14},{10,8},{12,... | collective-permute-start | bytes 1228808 | tf_op jit(solution)/shard_map/cond/branch_0_fun/ppermute | solution.py:411
  36.4 13.0 %collective-permute-start.2 = (bf16[25,16,512]{2,1,0:T(8,128)(2,1)}, bf16[25,16,512]{2,1,0:T(8,128)(2,1)S(1)}, u32[]{:S(2)}, u32[]{:S(2)}) collective-permute-start(bf16[25,16,512]{2,1,0:T(8,128)(2,1)} %get-tuple-element.36), channel_id=1, source_target_pairs={{0,2},{2,4},{4,6},{6,0},{1,3},{3,5},{5,7},{7,1},{8,10},{10,12},{12... | collective-permute-start | bytes 1228808 | tf_op jit(solution)/shard_map/cond/branch_0_fun/ppermute | solution.py:410
  36.5 13.0 %collective-permute-start.3 = (bf16[25,16,512]{2,1,0:T(8,128)(2,1)}, bf16[25,16,512]{2,1,0:T(8,128)(2,1)S(1)}, u32[]{:S(2)}, u32[]{:S(2)}) collective-permute-start(bf16[25,16,512]{2,1,0:T(8,128)(2,1)} %get-tuple-element.39), channel_id=1, source_target_pairs={{0,6},{2,0},{4,2},{6,4},{1,7},{3,1},{5,3},{7,5},{8,14},{10,8},{12,... | collective-permute-start | bytes 1228808 | tf_op jit(solution)/shard_map/cond/branch_0_fun/ppermute | solution.py:411
  52.3 7.4 %copy-start.7 = (s32[1,128]{1,0:T(1,128)S(1)}, s32[1,128]{1,0:T(1,128)}, u32[]{:S(2)}) copy-start(s32[1,128]{1,0:T(1,128)} %param.21) | copy-start | bytes 1540
  52.4 9.5 %copy-start.8 = (f32[64]{0:T(128)S(1)}, f32[64]{0:T(128)}, u32[]{:S(2)}) copy-start(f32[64]{0:T(128)} %constant.24.clone) | copy-start | bytes 772
  52.4 9.9 %copy-start = (bf16[1,128,4096]{2,1,0:T(8,128)(2,1)S(1)}, bf16[1,128,4096]{2,1,0:T(8,128)(2,1)}, u32[]{:S(2)}) copy-start(bf16[1,128,4096]{2,1,0:T(8,128)(2,1)} %param.22) | copy-start | bytes 3145732
  52.4 9.9 %copy-start.1 = (bf16[1,128,512]{2,1,0:T(8,128)(2,1)S(1)}, bf16[1,128,512]{2,1,0:T(8,128)(2,1)}, u32[]{:S(2)}) copy-start(bf16[1,128,512]{2,1,0:T(8,128)(2,1)} %param.23) | copy-start | bytes 393220
  52.4 56.1 %all-to-all-start.1 = ((bf16[64,2,2,16,512]{4,3,2,1,0:T(8,128)(2,1)}), bf16[64,2,2,16,512]{4,3,2,1,0:T(8,128)(2,1)}, u32[]{:S(2)}, u32[]{:S(2)}) async-start(bf16[64,2,2,16,512]{4,3,2,1,0:T(8,128)(2,1)} %get-tuple-element.104), calls=%async_computation.1 | async-start | bytes 8388608 | tf_op jit(solution)/shard_map/all_to_all | solution.py:450
  62.8 1.0 copy-start.2
  63.8 0.7 copy-start.3
  113.8 24.4 %all-to-all-start.2 = ((f32[128,1,128]{2,1,0:T(1,128)}), f32[128,1,128]{2,1,0:T(1,128)S(1)}, u32[]{:S(2)}, u32[]{:S(2)}) async-start(f32[128,1,128]{2,1,0:T(1,128)} %bitcast.24), calls=%async_computation.2 | async-start | bytes 131072 | tf_op jit(solution)/shard_map/all_to_all | solution.py:495

commit v5 on v4

--- a/solution.py
+++ b/solution.py
@@ -193,12 +193,14 @@
     lax.fori_loop(0, ends[0] + ends[1], drain, 0)
 
 
-def fresh_kernel(heads_kv, group, q, k, cosine, sine, q_out, k_out):
+def fresh_kernel(heads_kv, group, q, k, v, cosine, sine, q_out, pair_out):
     cos = cosine[...]
     sin = sine[...]
     for h in range(heads_kv):
         cols = slice(h * HD, (h + 1) * HD)
-        k_out[:, cols] = turn(k[:, cols].astype(jnp.float32), cos, sin).astype(jnp.bfloat16)
+        turned = turn(k[:, cols].astype(jnp.float32), cos, sin)
+        pair_out[h, :, :HD] = turned.astype(jnp.bfloat16)
+        pair_out[h, :, HD:] = v[:, cols]
         for g in range(group):
             n = h * group + g
             turned = turn(q[:, n * HD : (n + 1) * HD].astype(jnp.float32), cos, sin)
@@ -250,8 +252,7 @@
     places_row,
     places_col,
     q,
-    new_k,
-    new_v,
+    new_pair,
     cos_span,
     sin_span,
     cos_token,
@@ -302,7 +303,6 @@
 
     def head(h, carry):
         slot = lax.rem(h, 2)
-        cols = pl.ds(pl.multiple_of(h * HD, HD), HD)
         pltpu.make_async_copy(raw.at[slot], raw.at[slot], sems.at[slot]).wait()
 
         @pl.when(h + 1 < heads_kv)
@@ -314,12 +314,11 @@
             rows = slice(j * RPC, (j + 1) * RPC)
             span = slice(j * CL, (j + 1) * CL)
             old = raw[slot, 0, j].reshape(CL, HD).astype(jnp.float32)
-            new = jnp.dot(put[j], new_k[rows, cols], preferred_element_type=jnp.float32)
+            new = jnp.dot(put[j], new_pair[h, rows, :], preferred_element_type=jnp.float32)
             old = turn(old, cosine[span, :], sine[span, :])
-            keys[span, :] = (old * stay[span, :] + new).astype(jnp.bfloat16)
+            keys[span, :] = (old * stay[span, :] + new[:, :HD]).astype(jnp.bfloat16)
             old = raw[slot, 1, j].reshape(CL, HD).astype(jnp.float32)
-            new = jnp.dot(put[j], new_v[rows, cols], preferred_element_type=jnp.float32)
-            vals[span, :] = (old * stay[span, :] + new).astype(jnp.bfloat16)
+            vals[span, :] = (old * stay[span, :] + new[:, HD:]).astype(jnp.bfloat16)
         for t in range(CPR):
             later = q[pl.ds(h * CPR + t, CPR - t)].reshape((CPR - t) * block, HD)
             scores[t * block :, t * CL : (t + 1) * CL] = lax.dot_general(
@@ -457,19 +456,20 @@
     angles = places.astype(jnp.float32)[:, None] * jnp.asarray(FREQ)[None, :]
     cosine = jnp.cos(angles)
     sine = jnp.sin(angles)
-    queries, new_k = pl.pallas_call(
+    queries, new_pair = pl.pallas_call(
         functools.partial(fresh_kernel, heads_kv, group),
         out_shape=(
             jax.ShapeDtypeStruct((heads_kv * CPR, group * RPC, HD), bf16),
-            jax.ShapeDtypeStruct((RC, width), bf16),
+            jax.ShapeDtypeStruct((heads_kv, RC, 2 * HD), bf16),
         ),
-        in_specs=[VMEM] * 4,
+        in_specs=[VMEM] * 5,
         out_specs=(VMEM, VMEM),
         compiler_params=params(16),
         name="fresh",
     )(
         raw_q[0],
         raw_k,
+        new_v,
         jnp.concatenate([cosine, cosine], axis=1),
         jnp.concatenate([-sine, sine], axis=1),
     )
@@ -486,7 +486,7 @@
             pltpu.VMEM((CPR, n_store, tok_dev, width), bf16),
             pltpu.SemaphoreType.DMA((2, CPR)),
         ],
-        compiler_params=params(58),
+        compiler_params=params(50),
         cost_estimate=pl.CostEstimate(
             flops=4 * RC * CL * width, bytes_accessed=4 * CTX * width, transcendentals=0
         ),
@@ -497,7 +497,7 @@
     attended = pl.pallas_call(
         functools.partial(attend_kernel, heads_kv, group),
         out_shape=jax.ShapeDtypeStruct((RC, heads_q * HD), bf16),
-        in_specs=[SMEM] + [VMEM] * 9 + [ANY],
+        in_specs=[SMEM] + [VMEM] * 8 + [ANY],
         out_specs=VMEM,
         scratch_shapes=[
             pltpu.VMEM((2, 2, CPR, n_store, tok_dev, HD), bf16),
@@ -511,7 +511,7 @@
             pltpu.VMEM((CPR * group * RPC, CTX), jnp.float32),
             pltpu.SemaphoreType.DMA((2,)),
         ],
-        compiler_params=params(58),
+        compiler_params=params(50),
         cost_estimate=pl.CostEstimate(
             flops=2 * heads_q * RC * CTX * HD * 2,
             bytes_accessed=4 * CTX * width + 4 * RC * heads_q * HD,
@@ -523,8 +523,7 @@
         places_row,
         places_col,
         queries,
-        new_k,
-        new_v,
+        new_pair,
         jnp.asarray(COS_SPAN),
         jnp.asarray(SIN_SPAN),
         jnp.asarray(COS_TOKEN),

time: 139 us -> 138 us (level)
  waiting for transfers between devices: 49.6 us -> 52.8 us
  local copies, waits for them, and re-layouts: 3.62 us -> 0.78 us
    ppermute x2, waiting for transfers between devices: 5.56 us -> 7.46 us  [gather(): came.append(lax.ppermute(ups, 'req', climb))]
    unnamed x12 -> x22, local copies, waits for them, and re-layouts: 1.7 us -> 0.07 us
  transfers between devices with their start and end apart: 6 -> 6, of which waited for: 2 -> 2; matrix products, arithmetic and copies ran while one was open for 2% -> 1% of each run, Pallas kernels for 16% -> 16%
where the time goes in v5:
time: 138 us
  waiting for transfers between devices  52.8 us (38%)
  Pallas kernels  35.1 us (25%)
  starting transfers between devices  23.2 us (17%)
  blocking collectives  20.3 us (15%)
  between operations  2.81 us (2%)
  other arithmetic  2.46 us (2%)
    all_to_all x1, waiting for transfers between devices, local(): lax.all_to_all(send, ('store', 'req'), split_axis=0, concat_axis=0, tiled...  45.4 us
    all_to_all x1, blocking collectives, local(): lax.all_to_all(plan, ('store', 'req'), split_axis=0, concat_axis=0, tiled...  20.3 us
    pallas_call x1, Pallas kernels, local(): pl.pallas_call(functools.partial(attend_kernel, heads_kv, group), out_sha...  12 us
    all_to_all x1, starting transfers between devices, local(): lax.all_to_all(part, ('store', 'req', 'tp'), split_axis=0, concat_axis=0,...  11.2 us
    pallas_call x2, Pallas kernels, gather(): ups, downs = move(plans, table)  8.52 us
    ppermute x2, waiting for transfers between devices, gather(): came.append(lax.ppermute(ups, 'req', climb))  7.46 us
    all_to_all x1, starting transfers between devices, local(): lax.all_to_all(send, ('store', 'req'), split_axis=0, concat_axis=0, tiled...  6.61 us
    ppermute x2, starting transfers between devices, gather(): came.append(lax.ppermute(downs, 'req', sink))  5.05 us
  transfers between devices with their start and end apart: 6, of which 2 were waited for; matrix products, arithmetic and copies ran while one was open for 1% of the time, Pallas kernels for 16%

profile of v5, /device:TPU:1, one launch (start us, length us, event | category | flops | bytes accessed | tf_op | source)
XLA Modules:
  0.0 137.6 jit_solution(12253094514384031529)
XLA Ops:
  0.6 1.6 %ask.1 = (s32[64,128]{1,0:T(8,128)}, s32[2,8]{1,0:T(2,128)}) custom-call(s32[512]{0:T(512)} %span_row.1, s32[1,8]{1,0:T(1,128)} %span_lists.3), custom_call_target="tpu_custom_call" | custom-call | tf_op jit(solution)/shard_map/ask/pallas_call | solution.py:375
  2.3 20.3 %all_to_all.26 = s32[64,1,128]{2,1,0:T(1,128)S(1)} all-to-all(s32[64,1,128]{2,1,0:T(1,128)} %bitcast.26), channel_id=1, replica_groups=mesh['store'=16,'req'=4,'tp'=2] {'store','req'}, dimensions={0} | all-to-all | bytes 65536 | tf_op jit(solution)/shard_map/all_to_all | solution.py:385
  22.6 0.1 slice_reduce_fusion
  22.7 0.6 reduce_max.9
  25.2 29.0 %conditional.1 = (bf16[64,2,2,16,512]{4,3,2,1,0:T(8,128)(2,1)}) conditional(s32[]{:T(128)} %clamp.3, (s32[64,128]{1,0:T(8,128)S(1)}, bf16[128,16,512]{2,1,0:T(8,128)(2,1)}, bf16[128,16,512]{2,1,0:T(8,128)(2,1)}) %tuple.40, (s32[64,128]{1,0:T(8,128)S(1)}, bf16[128,16,512]{2,1,0:T(8,128)(2,1)}, ...), branch_computations={%region_2.0_spmd, %region_3.0_spmd, %region_4.0_spmd, %region_5.0_... | conditional | bytes 33554600 | solution.py:442
  25.3 4.2 %move.10 = (bf16[29,16,512]{2,1,0:T(8,128)(2,1)}, bf16[29,16,512]{2,1,0:T(8,128)(2,1)}) custom-call(s32[64,128]{1,0:T(8,128)S(1)} %get-tuple-element.50.plan, bf16[128,16,512]{2,1,0:T(8,128)(2,1)} %get-tuple-element.53.table.keys), custom_call_target="tpu_custom_call" | custom-call | tf_op jit(solution)/shard_map/cond/branch_1_fun/move/pallas_call | solution.py:408
  29.5 0.4 collective-permute-start.4
  29.9 2.4 %collective-permute-start.5 = (bf16[29,16,512]{2,1,0:T(8,128)(2,1)}, bf16[29,16,512]{2,1,0:T(8,128)(2,1)S(1)}, u32[]{:S(2)}, u32[]{:S(2)}) collective-permute-start(bf16[29,16,512]{2,1,0:T(8,128)(2,1)} %get-tuple-element.51), channel_id=1, source_target_pairs={{0,6},{2,0},{4,2},{6,4},{1,7},{3,1},{5,3},{7,5},{8,14},{10,8},{12,... | collective-permute-start | bytes 1425416 | tf_op jit(solution)/shard_map/cond/branch_1_fun/ppermute | solution.py:410
  32.3 4.3 %move.11 = (bf16[29,16,512]{2,1,0:T(8,128)(2,1)}, bf16[29,16,512]{2,1,0:T(8,128)(2,1)}) custom-call(s32[64,128]{1,0:T(8,128)S(1)} %get-tuple-element.50.plan, bf16[128,16,512]{2,1,0:T(8,128)(2,1)} %get-tuple-element.54.table.values), custom_call_target="tpu_custom_call" | custom-call | tf_op jit(solution)/shard_map/cond/branch_1_fun/move/pallas_call | solution.py:408
  36.6 0.1 collective-permute-start.6
  36.6 2.7 %collective-permute-start.7 = (bf16[29,16,512]{2,1,0:T(8,128)(2,1)}, bf16[29,16,512]{2,1,0:T(8,128)(2,1)S(1)}, u32[]{:S(2)}, u32[]{:S(2)}) collective-permute-start(bf16[29,16,512]{2,1,0:T(8,128)(2,1)} %get-tuple-element.52), channel_id=1, source_target_pairs={{0,6},{2,0},{4,2},{6,4},{1,7},{3,1},{5,3},{7,5},{8,14},{10,8},{12,... | collective-permute-start | bytes 1425416 | tf_op jit(solution)/shard_map/cond/branch_1_fun/ppermute | solution.py:410
  39.3 4.7 %own.5 = bf16[64,2,2,16,512]{4,3,2,1,0:T(8,128)(2,1)} custom-call(s32[64,128]{1,0:T(8,128)S(1)} %get-tuple-element.50.plan, bf16[128,16,512]{2,1,0:T(8,128)(2,1)} %get-tuple-element.53.table.keys, bf16[128,16,512]{2,1,0:T(8,128)(2,1)S(1)} %copy-done.10), custom_call_target="tpu_custom_call" | custom-call | tf_op jit(solution)/shard_map/cond/branch_1_fun/own/pallas_call | solution.py:414
  44.0 7.5 %collective-permute-done.6.below_v = bf16[29,16,512]{2,1,0:T(8,128)(2,1)S(1)} collective-permute-done((bf16[29,16,512]{2,1,0:T(8,128)(2,1)}, bf16[29,16,512]{2,1,0:T(8,128)(2,1)S(1)}, u32[]{:S(2)}, u32[]{:S(2)}) %collective-permute-start.6) | collective-permute-done | bytes 475168 | tf_op jit(solution)/shard_map/cond/branch_1_fun/ppermute | solution.py:409
  51.5 2.8 %patch.5 = bf16[64,2,2,16,512]{4,3,2,1,0:T(8,128)(2,1)} custom-call(s32[64,128]{1,0:T(8,128)S(1)} %get-tuple-element.50.plan, bf16[29,16,512]{2,1,0:T(8,128)(2,1)S(1)} %collective-permute-done.4.below_k, bf16[29,16,512]{2,1,0:T(8,128)(2,1)S(1)} %collective-permute-done.5.above_k, ...), custom_call_target="tpu_custom_call", output_to_operand_aliasing={{}: (5, {})} | custom-call | tf_op jit(solution)/shard_map/cond/branch_1_fun/patch/pallas_call | solution.py:428
  54.3 0.0 copy-start.13
  54.4 6.6 %all-to-all-start.1 = ((bf16[64,2,2,16,512]{4,3,2,1,0:T(8,128)(2,1)}), bf16[64,2,2,16,512]{4,3,2,1,0:T(8,128)(2,1)}, u32[]{:S(2)}, u32[]{:S(2)}) async-start(bf16[64,2,2,16,512]{4,3,2,1,0:T(8,128)(2,1)} %get-tuple-element.104), calls=%async_computation.1 | async-start | bytes 8388608 | tf_op jit(solution)/shard_map/all_to_all | solution.py:449
  61.0 0.0 copy-start.5
  61.0 0.0 copy-start.6
  61.0 0.0 copy-start.7
  61.0 0.0 copy-start.8
  61.0 0.5 broadcast.4
  61.6 0.7 convert_bitcast_fusion
  62.2 0.1 reshape_squeeze.3.places_row
  62.3 0.1 copy.22.places_col
  62.4 0.3 fusion
  62.7 0.1 pad_maximum_fusion
  62.9 0.6 fresh.1
  63.4 45.4 %all-to-all-done.1 = bf16[64,2,2,16,512]{4,3,2,1,0:T(8,128)(2,1)} async-done(((bf16[64,2,2,16,512]{4,3,2,1,0:T(8,128)(2,1)}), bf16[64,2,2,16,512]{4,3,2,1,0:T(8,128)(2,1)}, u32[]{:S(2)}, u32[]{:S(2)}) %all-to-all-start.1) | async-done | bytes 4194336 | tf_op jit(solution)/shard_map/all_to_all | solution.py:449
  108.8 4.9 %drift.1 = f32[128,128]{1,0:T(8,128)} custom-call(s32[2,8]{1,0:T(2,128)S(1)} %copy-done.4, s32[1,8]{1,0:T(1,128)S(1)} %copy-done.3, s32[128,1]{1,0:T(8,128)S(1)} %copy.22.places_col, bf16[128,512]{1,0:T(8,128)(2,1)S(1)} %bitcast.18, bf16[128,512]{1,0:T(8,128)(2,1)S(1)} %bitcast.20, bf16[16,4,2,2,16,512]{5,4,3,2,1,0:T(8,128)(2,1)} %bitcast.8.got), custom_call_target="tpu_custom_call" | custom-call | flops 67108864 | bytes 4194304 | tf_op jit(solution)/shard_map/drift/pallas_call | solution.py:479
  113.7 11.2 %all-to-all-start.2 = ((f32[128,1,128]{2,1,0:T(1,128)}), f32[128,1,128]{2,1,0:T(1,128)S(1)}, u32[]{:S(2)}, u32[]{:S(2)}) async-start(f32[128,1,128]{2,1,0:T(1,128)} %bitcast.11), calls=%async_computation.2 | async-start | bytes 131072 | tf_op jit(solution)/shard_map/all_to_all | solution.py:495
  124.9 12.0 %attend.1 = bf16[128,4096]{1,0:T(8,128)(2,1)} custom-call(s32[2,8]{1,0:T(2,128)S(1)} %copy-done.4, s32[8,16]{1,0:T(8,128)S(1)} %reshape_squeeze.3.places_row, s32[128,1]{1,0:T(8,128)S(1)} %copy.22.places_col, bf16[32,128,128]{2,1,0:T(8,128)(2,1)S(1)} %get-tuple-element.95.q, bf16[4,128,256]{2,1,0:T(8,128)(2,1)S(1)} %get-tuple-element.96.new_pair, ...), custom_call_target="tpu_custom_call" | custom-call | flops 4294967296 | bytes 6291456 | tf_op jit(solution)/shard_map/attend/pallas_call | solution.py:497
  136.9 0.7 reduce_sum.19
  (23 shorter events, 0.1 us)
Async XLA Ops:
  25.3 14.0 %copy-start.10 = (bf16[128,16,512]{2,1,0:T(8,128)(2,1)S(1)}, bf16[128,16,512]{2,1,0:T(8,128)(2,1)}, u32[]{:S(2)}) copy-start(bf16[128,16,512]{2,1,0:T(8,128)(2,1)} %get-tuple-element.54.table.values) | copy-start | bytes 6291460 | tf_op jit(solution)/shard_map/cond
  29.5 14.5 %collective-permute-start.4 = (bf16[29,16,512]{2,1,0:T(8,128)(2,1)}, bf16[29,16,512]{2,1,0:T(8,128)(2,1)S(1)}, u32[]{:S(2)}, u32[]{:S(2)}) collective-permute-start(bf16[29,16,512]{2,1,0:T(8,128)(2,1)} %get-tuple-element.45), channel_id=1, source_target_pairs={{0,2},{2,4},{4,6},{6,0},{1,3},{3,5},{5,7},{7,1},{8,10},{10,12},{12... | collective-permute-start | bytes 1425416 | tf_op jit(solution)/shard_map/cond/branch_1_fun/ppermute | solution.py:409
  29.9 14.1 %collective-permute-start.5 = (bf16[29,16,512]{2,1,0:T(8,128)(2,1)}, bf16[29,16,512]{2,1,0:T(8,128)(2,1)S(1)}, u32[]{:S(2)}, u32[]{:S(2)}) collective-permute-start(bf16[29,16,512]{2,1,0:T(8,128)(2,1)} %get-tuple-element.51), channel_id=1, source_target_pairs={{0,6},{2,0},{4,2},{6,4},{1,7},{3,1},{5,3},{7,5},{8,14},{10,8},{12,... | collective-permute-start | bytes 1425416 | tf_op jit(solution)/shard_map/cond/branch_1_fun/ppermute | solution.py:410
  36.6 14.9 %collective-permute-start.6 = (bf16[29,16,512]{2,1,0:T(8,128)(2,1)}, bf16[29,16,512]{2,1,0:T(8,128)(2,1)S(1)}, u32[]{:S(2)}, u32[]{:S(2)}) collective-permute-start(bf16[29,16,512]{2,1,0:T(8,128)(2,1)} %get-tuple-element.49), channel_id=1, source_target_pairs={{0,2},{2,4},{4,6},{6,0},{1,3},{3,5},{5,7},{7,1},{8,10},{10,12},{12... | collective-permute-start | bytes 1425416 | tf_op jit(solution)/shard_map/cond/branch_1_fun/ppermute | solution.py:409
  36.6 14.8 %collective-permute-start.7 = (bf16[29,16,512]{2,1,0:T(8,128)(2,1)}, bf16[29,16,512]{2,1,0:T(8,128)(2,1)S(1)}, u32[]{:S(2)}, u32[]{:S(2)}) collective-permute-start(bf16[29,16,512]{2,1,0:T(8,128)(2,1)} %get-tuple-element.52), channel_id=1, source_target_pairs={{0,6},{2,0},{4,2},{6,4},{1,7},{3,1},{5,3},{7,5},{8,14},{10,8},{12,... | collective-permute-start | bytes 1425416 | tf_op jit(solution)/shard_map/cond/branch_1_fun/ppermute | solution.py:410
  54.3 7.3 %copy-start.12 = (s32[1,128]{1,0:T(1,128)S(1)}, s32[1,128]{1,0:T(1,128)}, u32[]{:S(2)}) copy-start(s32[1,128]{1,0:T(1,128)} %param.21) | copy-start | bytes 1540
  54.3 8.1 %copy-start.13 = (f32[64]{0:T(128)S(1)}, f32[64]{0:T(128)}, u32[]{:S(2)}) copy-start(f32[64]{0:T(128)} %constant.24.clone) | copy-start | bytes 772
  54.3 8.5 %copy-start = (bf16[1,128,4096]{2,1,0:T(8,128)(2,1)S(1)}, bf16[1,128,4096]{2,1,0:T(8,128)(2,1)}, u32[]{:S(2)}) copy-start(bf16[1,128,4096]{2,1,0:T(8,128)(2,1)} %param.22) | copy-start | bytes 3145732
  54.3 8.5 %copy-start.1 = (bf16[1,128,512]{2,1,0:T(8,128)(2,1)S(1)}, bf16[1,128,512]{2,1,0:T(8,128)(2,1)}, u32[]{:S(2)}) copy-start(bf16[1,128,512]{2,1,0:T(8,128)(2,1)} %param.23) | copy-start | bytes 393220
  54.3 8.5 %copy-start.2 = (bf16[1,128,512]{2,1,0:T(8,128)(2,1)S(1)}, bf16[1,128,512]{2,1,0:T(8,128)(2,1)}, u32[]{:S(2)}) copy-start(bf16[1,128,512]{2,1,0:T(8,128)(2,1)} %param.24) | copy-start | bytes 393220
  54.3 54.5 %copy-start.3 = (s32[1,8]{1,0:T(1,128)S(1)}, s32[1,8]{1,0:T(1,128)}, u32[]{:S(2)}) copy-start(s32[1,8]{1,0:T(1,128)} %span_lists.3) | copy-start | bytes 100
  54.4 54.5 %copy-start.4 = (s32[2,8]{1,0:T(2,128)S(1)}, s32[2,8]{1,0:T(2,128)}, u32[]{:S(2)}) copy-start(s32[2,8]{1,0:T(2,128)} %get-tuple-element.90.place) | copy-start | bytes 196
  54.4 54.5 %all-to-all-start.1 = ((bf16[64,2,2,16,512]{4,3,2,1,0:T(8,128)(2,1)}), bf16[64,2,2,16,512]{4,3,2,1,0:T(8,128)(2,1)}, u32[]{:S(2)}, u32[]{:S(2)}) async-start(bf16[64,2,2,16,512]{4,3,2,1,0:T(8,128)(2,1)} %get-tuple-element.104), calls=%async_computation.1 | async-start | bytes 8388608 | tf_op jit(solution)/shard_map/all_to_all | solution.py:449
  61.0 63.9 %copy-start.5 = (f32[256,128]{1,0:T(8,128)S(1)}, f32[256,128]{1,0:T(8,128)}, u32[]{:S(2)}) copy-start(f32[256,128]{1,0:T(8,128)} %constant.27.clone.cos_token) | copy-start | bytes 393220
  61.0 63.9 %copy-start.6 = (f32[256,128]{1,0:T(8,128)S(1)}, f32[256,128]{1,0:T(8,128)}, u32[]{:S(2)}) copy-start(f32[256,128]{1,0:T(8,128)} %constant.28.clone.sin_token) | copy-start | bytes 393220
  61.0 63.9 %copy-start.7 = (f32[8,128]{1,0:T(8,128)S(1)}, f32[8,128]{1,0:T(8,128)}, u32[]{:S(2)}) copy-start(f32[8,128]{1,0:T(8,128)} %constant.25.clone.cos_span) | copy-start | bytes 12292
  61.0 63.9 %copy-start.8 = (f32[8,128]{1,0:T(8,128)S(1)}, f32[8,128]{1,0:T(8,128)}, u32[]{:S(2)}) copy-start(f32[8,128]{1,0:T(8,128)} %constant.26.clone.sin_span) | copy-start | bytes 12292
  113.7 23.2 %all-to-all-start.2 = ((f32[128,1,128]{2,1,0:T(1,128)}), f32[128,1,128]{2,1,0:T(1,128)S(1)}, u32[]{:S(2)}, u32[]{:S(2)}) async-start(f32[128,1,128]{2,1,0:T(1,128)} %bitcast.11), calls=%async_computation.2 | async-start | bytes 131072 | tf_op jit(solution)/shard_map/all_to_all | solution.py:495

commit v6 on v5

--- a/solution.py
+++ b/solution.py
@@ -18,7 +18,7 @@
 KVH = 8
 BLOCKS = 4
 SLOTS = CPR // BLOCKS
-SIZES = (25, 29, 36)
+SIZES = (22, 24, 26, 28, 30, 33, 36, 40)
 KEPT, UP, DOWN, FROM_BELOW, FROM_ABOVE, LOADS = 0, 4, 8, 12, 13, 16
 LANES = 128
 SCALE_LOG2E = float(HD ** -0.5 * np.log2(np.e))
@@ -116,6 +116,17 @@
             jnp.where(climbs, of(base_below, above) + after, of(base_above, below) + after - ups),
         )
     plan[...] = out
+
+
+def level_kernel(plan, out):
+    lane = lax.broadcasted_iota(jnp.int32, (1, LANES), 1)
+    loads = jnp.sum(plan[...].astype(jnp.float32), axis=0, keepdims=True)
+    loads = jnp.where((lane >= LOADS) & (lane < LOADS + 2 * BLOCKS), loads, 0.0)
+    load = jnp.max(loads).astype(jnp.int32)
+    level = jnp.int32(0)
+    for size in SIZES:
+        level = level + jnp.where(load > size, 1, 0)
+    out[0] = level
 
 
 def move_kernel(size, plan, table, up_out, down_out, rows, up_stage, down_stage, sems):
@@ -436,8 +447,13 @@
             name="patch",
         )(plans, *came, own)
 
-    load = jnp.max(jnp.sum(plans[:, LOADS : LOADS + 2 * BLOCKS], axis=0))
-    level = sum((load > size).astype(jnp.int32) for size in SIZES)
+    level = pl.pallas_call(
+        level_kernel,
+        out_shape=jax.ShapeDtypeStruct((1,), jnp.int32),
+        in_specs=[VMEM],
+        out_specs=SMEM,
+        name="level",
+    )(plans)[0]
     most = SLOTS * peers
     send = lax.switch(
         level,

time: 138 us -> 137 us (level)
    ppermute x2, waiting for transfers between devices: 7.46 us -> 5.77 us  [gather(): came.append(lax.ppermute(ups, 'req', climb))]
    all_to_all x1, waiting for transfers between devices: 45.4 us -> 46.8 us  [local(): lax.all_to_all(send, ('store', 'req'), split_axis=0, concat_axis=0, tiled...]
where the time goes in v6:
time: 137 us; the launch traced here: 136 us
  waiting for transfers between devices  52.6 us (38%)
  Pallas kernels  35.8 us (26%)
  starting transfers between devices  23.1 us (17%)
  blocking collectives  20.3 us (15%)
  other arithmetic  1.73 us (1%)
  between operations  1.52 us (1%)
    all_to_all x1, waiting for transfers between devices, local(): lax.all_to_all(send, ('store', 'req'), split_axis=0, concat_axis=0, tiled...  46.8 us
    all_to_all x1, blocking collectives, local(): lax.all_to_all(plan, ('store', 'req'), split_axis=0, concat_axis=0, tiled...  20.3 us
    pallas_call x1, Pallas kernels, local(): pl.pallas_call(functools.partial(attend_kernel, heads_kv, group), out_sha...  11.9 us
    all_to_all x1, starting transfers between devices, local(): lax.all_to_all(part, ('store', 'req', 'tp'), split_axis=0, concat_axis=0,...  10.8 us
    pallas_call x2, Pallas kernels, gather(): ups, downs = move(plans, table)  8.42 us
    all_to_all x1, starting transfers between devices, local(): lax.all_to_all(send, ('store', 'req'), split_axis=0, concat_axis=0, tiled...  6.74 us
    ppermute x2, waiting for transfers between devices, gather(): came.append(lax.ppermute(ups, 'req', climb))  5.77 us
    ppermute x2, starting transfers between devices, gather(): came.append(lax.ppermute(downs, 'req', sink))  5.05 us
  transfers between devices with their start and end apart: 6, of which 2 were waited for; matrix products, arithmetic and copies ran while one was open for 1% of the time, Pallas kernels for 16%

profile of v6, /device:TPU:1, one launch (start us, length us, event | category | flops | bytes accessed | tf_op | source)
XLA Modules:
  0.0 136.1 jit_solution(16452621075016484878)
XLA Ops:
  0.6 1.6 %ask.1 = (s32[64,128]{1,0:T(8,128)}, s32[2,8]{1,0:T(2,128)}) custom-call(s32[512]{0:T(512)} %span_row.1, s32[1,8]{1,0:T(1,128)} %span_lists.3), custom_call_target="tpu_custom_call" | custom-call | tf_op jit(solution)/shard_map/ask/pallas_call | solution.py:386
  2.3 20.3 %all_to_all.25 = s32[64,1,128]{2,1,0:T(1,128)S(1)} all-to-all(s32[64,1,128]{2,1,0:T(1,128)} %bitcast.32), channel_id=1, replica_groups=mesh['store'=16,'req'=4,'tp'=2] {'store','req'}, dimensions={0} | all-to-all | bytes 65536 | tf_op jit(solution)/shard_map/all_to_all | solution.py:396
  22.6 0.7 level.1
  23.9 27.7 %conditional.1 = (bf16[64,2,2,16,512]{4,3,2,1,0:T(8,128)(2,1)}) conditional(s32[]{:T(128)} %bitcast.3, (s32[64,128]{1,0:T(8,128)S(1)}, bf16[128,16,512]{2,1,0:T(8,128)(2,1)}, bf16[128,16,512]{2,1,0:T(8,128)(2,1)}) %tuple.70, (s32[64,128]{1,0:T(8,128)S(1)}, bf16[128,16,512]{2,1,0:T(8,128)(2,1)}, ...), branch_computations={%region_0.0_spmd, %region_1.0_spmd, %region_2.0_spmd, %region_3.0_... | conditional | bytes 33554600 | solution.py:458
  23.9 0.0 copy-start.11
  23.9 4.2 %move.22 = (bf16[26,16,512]{2,1,0:T(8,128)(2,1)}, bf16[26,16,512]{2,1,0:T(8,128)(2,1)}) custom-call(s32[64,128]{1,0:T(8,128)S(1)} %get-tuple-element.98.plan, bf16[128,16,512]{2,1,0:T(8,128)(2,1)} %get-tuple-element.101.table.keys), custom_call_target="tpu_custom_call" | custom-call | tf_op jit(solution)/shard_map/cond/branch_2_fun/move/pallas_call | solution.py:419
  28.1 0.4 collective-permute-start.8
  28.5 2.4 %collective-permute-start.9 = (bf16[26,16,512]{2,1,0:T(8,128)(2,1)}, bf16[26,16,512]{2,1,0:T(8,128)(2,1)S(1)}, u32[]{:S(2)}, u32[]{:S(2)}) collective-permute-start(bf16[26,16,512]{2,1,0:T(8,128)(2,1)} %get-tuple-element.99), channel_id=1, source_target_pairs={{0,6},{2,0},{4,2},{6,4},{1,7},{3,1},{5,3},{7,5},{8,14},{10,8},{12,... | collective-permute-start | bytes 1277960 | tf_op jit(solution)/shard_map/cond/branch_2_fun/ppermute | solution.py:421
  30.9 4.2 %move.23 = (bf16[26,16,512]{2,1,0:T(8,128)(2,1)}, bf16[26,16,512]{2,1,0:T(8,128)(2,1)}) custom-call(s32[64,128]{1,0:T(8,128)S(1)} %get-tuple-element.98.plan, bf16[128,16,512]{2,1,0:T(8,128)(2,1)} %get-tuple-element.102.table.values), custom_call_target="tpu_custom_call" | custom-call | tf_op jit(solution)/shard_map/cond/branch_2_fun/move/pallas_call | solution.py:419
  35.1 0.1 collective-permute-start.10
  35.2 2.7 %collective-permute-start.11 = (bf16[26,16,512]{2,1,0:T(8,128)(2,1)}, bf16[26,16,512]{2,1,0:T(8,128)(2,1)S(1)}, u32[]{:S(2)}, u32[]{:S(2)}) collective-permute-start(bf16[26,16,512]{2,1,0:T(8,128)(2,1)} %get-tuple-element.100), channel_id=1, source_target_pairs={{0,6},{2,0},{4,2},{6,4},{1,7},{3,1},{5,3},{7,5},{8,14},{10,8},{12,... | collective-permute-start | bytes 1277960 | tf_op jit(solution)/shard_map/cond/branch_2_fun/ppermute | solution.py:421
  37.8 4.8 %own.11 = bf16[64,2,2,16,512]{4,3,2,1,0:T(8,128)(2,1)} custom-call(s32[64,128]{1,0:T(8,128)S(1)} %get-tuple-element.98.plan, bf16[128,16,512]{2,1,0:T(8,128)(2,1)S(1)} %copy-done.11, bf16[128,16,512]{2,1,0:T(8,128)(2,1)} %get-tuple-element.102.table.values), custom_call_target="tpu_custom_call" | custom-call | tf_op jit(solution)/shard_map/cond/branch_2_fun/own/pallas_call | solution.py:425
  42.7 5.8 %collective-permute-done.10.below_v = bf16[26,16,512]{2,1,0:T(8,128)(2,1)S(1)} collective-permute-done((bf16[26,16,512]{2,1,0:T(8,128)(2,1)}, bf16[26,16,512]{2,1,0:T(8,128)(2,1)S(1)}, u32[]{:S(2)}, u32[]{:S(2)}) %collective-permute-start.10) | collective-permute-done | bytes 426016 | tf_op jit(solution)/shard_map/cond/branch_2_fun/ppermute | solution.py:420
  48.5 2.9 %patch.11 = bf16[64,2,2,16,512]{4,3,2,1,0:T(8,128)(2,1)} custom-call(s32[64,128]{1,0:T(8,128)S(1)} %get-tuple-element.98.plan, bf16[26,16,512]{2,1,0:T(8,128)(2,1)S(1)} %collective-permute-done.8.below_k, bf16[26,16,512]{2,1,0:T(8,128)(2,1)S(1)} %collective-permute-done.9.above_k, ...), custom_call_target="tpu_custom_call", output_to_operand_aliasing={{}: (5, {})} | custom-call | tf_op jit(solution)/shard_map/cond/branch_2_fun/patch/pallas_call | solution.py:439
  51.6 0.0 copy-start.18
  51.7 6.7 %all-to-all-start.1 = ((bf16[64,2,2,16,512]{4,3,2,1,0:T(8,128)(2,1)}), bf16[64,2,2,16,512]{4,3,2,1,0:T(8,128)(2,1)}, u32[]{:S(2)}, u32[]{:S(2)}) async-start(bf16[64,2,2,16,512]{4,3,2,1,0:T(8,128)(2,1)} %get-tuple-element.204), calls=%async_computation.1 | async-start | bytes 8388608 | tf_op jit(solution)/shard_map/all_to_all | solution.py:465
  58.4 0.0 copy-start.5
  58.4 0.0 copy-start.6
  58.4 0.0 copy-start.7
  58.5 0.0 copy-start.8
  58.5 0.5 broadcast.4
  59.0 0.7 convert_bitcast_fusion
  59.7 0.1 reshape_squeeze.3.places_row
  59.7 0.1 copy.27.places_col
  59.9 0.3 fusion
  60.2 0.1 pad_maximum_fusion
  60.3 0.5 fresh.1
  60.9 46.8 %all-to-all-done.1 = bf16[64,2,2,16,512]{4,3,2,1,0:T(8,128)(2,1)} async-done(((bf16[64,2,2,16,512]{4,3,2,1,0:T(8,128)(2,1)}), bf16[64,2,2,16,512]{4,3,2,1,0:T(8,128)(2,1)}, u32[]{:S(2)}, u32[]{:S(2)}) %all-to-all-start.1) | async-done | bytes 4194336 | tf_op jit(solution)/shard_map/all_to_all | solution.py:465
  107.7 4.9 %drift.1 = f32[128,128]{1,0:T(8,128)} custom-call(s32[2,8]{1,0:T(2,128)S(1)} %copy-done.4, s32[1,8]{1,0:T(1,128)S(1)} %copy-done.3, s32[128,1]{1,0:T(8,128)S(1)} %copy.27.places_col, bf16[128,512]{1,0:T(8,128)(2,1)S(1)} %bitcast.19, bf16[128,512]{1,0:T(8,128)(2,1)S(1)} %bitcast.21, bf16[16,4,2,2,16,512]{5,4,3,2,1,0:T(8,128)(2,1)} %bitcast.9.got), custom_call_target="tpu_custom_call" | custom-call | flops 67108864 | bytes 4194304 | tf_op jit(solution)/shard_map/drift/pallas_call | solution.py:495
  112.6 10.8 %all-to-all-start.2 = ((f32[128,1,128]{2,1,0:T(1,128)}), f32[128,1,128]{2,1,0:T(1,128)S(1)}, u32[]{:S(2)}, u32[]{:S(2)}) async-start(f32[128,1,128]{2,1,0:T(1,128)} %bitcast.12), calls=%async_computation.2 | async-start | bytes 131072 | tf_op jit(solution)/shard_map/all_to_all | solution.py:511
  123.5 11.9 %attend.1 = bf16[128,4096]{1,0:T(8,128)(2,1)} custom-call(s32[2,8]{1,0:T(2,128)S(1)} %copy-done.4, s32[8,16]{1,0:T(8,128)S(1)} %reshape_squeeze.3.places_row, s32[128,1]{1,0:T(8,128)S(1)} %copy.27.places_col, bf16[32,128,128]{2,1,0:T(8,128)(2,1)S(1)} %get-tuple-element.195.q, bf16[4,128,256]{2,1,0:T(8,128)(2,1)S(1)} %get-tuple-element.196.new_pair, ...), custom_call_target="tpu_custom_call" | custom-call | flops 4294967296 | bytes 6291456 | tf_op jit(solution)/shard_map/attend/pallas_call | solution.py:513
  135.4 0.7 reduce_sum.9
  (22 shorter events, 0.1 us)
Async XLA Ops:
  23.9 13.9 %copy-start.11 = (bf16[128,16,512]{2,1,0:T(8,128)(2,1)S(1)}, bf16[128,16,512]{2,1,0:T(8,128)(2,1)}, u32[]{:S(2)}) copy-start(bf16[128,16,512]{2,1,0:T(8,128)(2,1)} %get-tuple-element.101.table.keys) | copy-start | bytes 6291460 | tf_op jit(solution)/shard_map/cond
  28.1 14.6 %collective-permute-start.8 = (bf16[26,16,512]{2,1,0:T(8,128)(2,1)}, bf16[26,16,512]{2,1,0:T(8,128)(2,1)S(1)}, u32[]{:S(2)}, u32[]{:S(2)}) collective-permute-start(bf16[26,16,512]{2,1,0:T(8,128)(2,1)} %get-tuple-element.93), channel_id=1, source_target_pairs={{0,2},{2,4},{4,6},{6,0},{1,3},{3,5},{5,7},{7,1},{8,10},{10,12},{12... | collective-permute-start | bytes 1277960 | tf_op jit(solution)/shard_map/cond/branch_2_fun/ppermute | solution.py:420
  28.5 14.2 %collective-permute-start.9 = (bf16[26,16,512]{2,1,0:T(8,128)(2,1)}, bf16[26,16,512]{2,1,0:T(8,128)(2,1)S(1)}, u32[]{:S(2)}, u32[]{:S(2)}) collective-permute-start(bf16[26,16,512]{2,1,0:T(8,128)(2,1)} %get-tuple-element.99), channel_id=1, source_target_pairs={{0,6},{2,0},{4,2},{6,4},{1,7},{3,1},{5,3},{7,5},{8,14},{10,8},{12,... | collective-permute-start | bytes 1277960 | tf_op jit(solution)/shard_map/cond/branch_2_fun/ppermute | solution.py:421
  35.1 13.4 %collective-permute-start.10 = (bf16[26,16,512]{2,1,0:T(8,128)(2,1)}, bf16[26,16,512]{2,1,0:T(8,128)(2,1)S(1)}, u32[]{:S(2)}, u32[]{:S(2)}) collective-permute-start(bf16[26,16,512]{2,1,0:T(8,128)(2,1)} %get-tuple-element.97), channel_id=1, source_target_pairs={{0,2},{2,4},{4,6},{6,0},{1,3},{3,5},{5,7},{7,1},{8,10},{10,12},{12... | collective-permute-start | bytes 1277960 | tf_op jit(solution)/shard_map/cond/branch_2_fun/ppermute | solution.py:420
  35.2 13.3 %collective-permute-start.11 = (bf16[26,16,512]{2,1,0:T(8,128)(2,1)}, bf16[26,16,512]{2,1,0:T(8,128)(2,1)S(1)}, u32[]{:S(2)}, u32[]{:S(2)}) collective-permute-start(bf16[26,16,512]{2,1,0:T(8,128)(2,1)} %get-tuple-element.100), channel_id=1, source_target_pairs={{0,6},{2,0},{4,2},{6,4},{1,7},{3,1},{5,3},{7,5},{8,14},{10,8},{12,... | collective-permute-start | bytes 1277960 | tf_op jit(solution)/shard_map/cond/branch_2_fun/ppermute | solution.py:421
  51.6 7.4 %copy-start.17 = (s32[1,128]{1,0:T(1,128)S(1)}, s32[1,128]{1,0:T(1,128)}, u32[]{:S(2)}) copy-start(s32[1,128]{1,0:T(1,128)} %param.26) | copy-start | bytes 1540
  51.6 8.2 %copy-start.18 = (f32[64]{0:T(128)S(1)}, f32[64]{0:T(128)}, u32[]{:S(2)}) copy-start(f32[64]{0:T(128)} %constant.18.clone) | copy-start | bytes 772
  51.6 8.7 %copy-start = (bf16[1,128,4096]{2,1,0:T(8,128)(2,1)S(1)}, bf16[1,128,4096]{2,1,0:T(8,128)(2,1)}, u32[]{:S(2)}) copy-start(bf16[1,128,4096]{2,1,0:T(8,128)(2,1)} %param.27) | copy-start | bytes 3145732
  51.6 8.7 %copy-start.1 = (bf16[1,128,512]{2,1,0:T(8,128)(2,1)S(1)}, bf16[1,128,512]{2,1,0:T(8,128)(2,1)}, u32[]{:S(2)}) copy-start(bf16[1,128,512]{2,1,0:T(8,128)(2,1)} %param.28) | copy-start | bytes 393220
  51.6 8.7 %copy-start.2 = (bf16[1,128,512]{2,1,0:T(8,128)(2,1)S(1)}, bf16[1,128,512]{2,1,0:T(8,128)(2,1)}, u32[]{:S(2)}) copy-start(bf16[1,128,512]{2,1,0:T(8,128)(2,1)} %param.29) | copy-start | bytes 393220
  51.7 56.0 %copy-start.3 = (s32[1,8]{1,0:T(1,128)S(1)}, s32[1,8]{1,0:T(1,128)}, u32[]{:S(2)}) copy-start(s32[1,8]{1,0:T(1,128)} %span_lists.3) | copy-start | bytes 100
  51.7 56.0 %copy-start.4 = (s32[2,8]{1,0:T(2,128)S(1)}, s32[2,8]{1,0:T(2,128)}, u32[]{:S(2)}) copy-start(s32[2,8]{1,0:T(2,128)} %get-tuple-element.190.place) | copy-start | bytes 196
  51.7 56.0 %all-to-all-start.1 = ((bf16[64,2,2,16,512]{4,3,2,1,0:T(8,128)(2,1)}), bf16[64,2,2,16,512]{4,3,2,1,0:T(8,128)(2,1)}, u32[]{:S(2)}, u32[]{:S(2)}) async-start(bf16[64,2,2,16,512]{4,3,2,1,0:T(8,128)(2,1)} %get-tuple-element.204), calls=%async_computation.1 | async-start | bytes 8388608 | tf_op jit(solution)/shard_map/all_to_all | solution.py:465
  58.4 65.1 %copy-start.5 = (f32[256,128]{1,0:T(8,128)S(1)}, f32[256,128]{1,0:T(8,128)}, u32[]{:S(2)}) copy-start(f32[256,128]{1,0:T(8,128)} %constant.21.clone.cos_token) | copy-start | bytes 393220
  58.4 65.0 %copy-start.6 = (f32[256,128]{1,0:T(8,128)S(1)}, f32[256,128]{1,0:T(8,128)}, u32[]{:S(2)}) copy-start(f32[256,128]{1,0:T(8,128)} %constant.22.clone.sin_token) | copy-start | bytes 393220
  58.4 65.0 %copy-start.7 = (f32[8,128]{1,0:T(8,128)S(1)}, f32[8,128]{1,0:T(8,128)}, u32[]{:S(2)}) copy-start(f32[8,128]{1,0:T(8,128)} %constant.19.clone.cos_span) | copy-start | bytes 12292
  58.5 65.0 %copy-start.8 = (f32[8,128]{1,0:T(8,128)S(1)}, f32[8,128]{1,0:T(8,128)}, u32[]{:S(2)}) copy-start(f32[8,128]{1,0:T(8,128)} %constant.20.clone.sin_span) | copy-start | bytes 12292
  112.6 22.8 %all-to-all-start.2 = ((f32[128,1,128]{2,1,0:T(1,128)}), f32[128,1,128]{2,1,0:T(1,128)S(1)}, u32[]{:S(2)}, u32[]{:S(2)}) async-start(f32[128,1,128]{2,1,0:T(1,128)} %bitcast.12), calls=%async_computation.2 | async-start | bytes 131072 | tf_op jit(solution)/shard_map/all_to_all | solution.py:511

commit v7 on v6

--- a/solution.py
+++ b/solution.py
@@ -129,10 +129,15 @@
     out[0] = level
 
 
-def move_kernel(size, plan, table, up_out, down_out, rows, up_stage, down_stage, sems):
-    load = pltpu.make_async_copy(table, rows, sems.at[0])
-    load.start()
-    load.wait()
+def move_kernel(size, plans, table, up_out, down_out, plan, rows, up_stage, down_stage, sems):
+    loads = [
+        pltpu.make_async_copy(plans, plan, sems.at[0]),
+        pltpu.make_async_copy(table, rows, sems.at[1]),
+    ]
+    for load in loads:
+        load.start()
+    for load in loads:
+        load.wait()
 
     def fill(r, marks):
         ends = []
@@ -403,9 +408,10 @@
         move = pl.pallas_call(
             functools.partial(move_kernel, size),
             out_shape=(moves, moves),
-            in_specs=[SMEM, ANY],
+            in_specs=[ANY, ANY],
             out_specs=(ANY, ANY),
             scratch_shapes=[
+                pltpu.SMEM((peers, LANES), jnp.int32),
                 pltpu.VMEM((shard_rows, tok_dev, width), bf16),
                 pltpu.VMEM((size + SLOTS, tok_dev, width), bf16),
                 pltpu.VMEM((size + SLOTS, tok_dev, width), bf16),

time: 137 us -> 134 us (0.978)
  Pallas kernels: 35.8 us -> 33.7 us
    pallas_call x2, Pallas kernels: 8.42 us -> 6.42 us  [gather(): ups, downs = move(plans, table)]
    all_to_all x1, waiting for transfers between devices: 46.8 us -> 45.4 us  [local(): lax.all_to_all(send, ('store', 'req'), split_axis=0, concat_axis=0, tiled...]
  transfers between devices with their start and end apart: 6 -> 6, of which waited for: 2 -> 2; matrix products, arithmetic and copies ran while one was open for 1% -> 1% of each run, Pallas kernels for 16% -> 15%
where the time goes in v7:
time: 134 us; the launch traced here: 133 us
  waiting for transfers between devices  51.7 us (39%)
  Pallas kernels  33.7 us (25%)
  starting transfers between devices  23.2 us (17%)
  blocking collectives  20.3 us (15%)
  other arithmetic  1.73 us (1%)
  between operations  1.52 us (1%)
    all_to_all x1, waiting for transfers between devices, local(): lax.all_to_all(send, ('store', 'req'), split_axis=0, concat_axis=0, tiled...  45.4 us
    all_to_all x1, blocking collectives, local(): lax.all_to_all(plan, ('store', 'req'), split_axis=0, concat_axis=0, tiled...  20.3 us
    pallas_call x1, Pallas kernels, local(): pl.pallas_call(functools.partial(attend_kernel, heads_kv, group), out_sha...  11.9 us
    all_to_all x1, starting transfers between devices, local(): lax.all_to_all(part, ('store', 'req', 'tp'), split_axis=0, concat_axis=0,...  11.2 us
    all_to_all x1, starting transfers between devices, local(): lax.all_to_all(send, ('store', 'req'), split_axis=0, concat_axis=0, tiled...  6.59 us
    pallas_call x2, Pallas kernels, gather(): ups, downs = move(plans, table)  6.42 us
    ppermute x2, waiting for transfers between devices, gather(): came.append(lax.ppermute(ups, 'req', climb))  6.3 us
    ppermute x2, starting transfers between devices, gather(): came.append(lax.ppermute(downs, 'req', sink))  5.05 us
  transfers between devices with their start and end apart: 6, of which 2 were waited for; matrix products, arithmetic and copies ran while one was open for 1% of the time, Pallas kernels for 15%

profile of v7, /device:TPU:1, one launch (start us, length us, event | category | flops | bytes accessed | tf_op | source)
XLA Modules:
  0.0 133.3 jit_solution(9499805814582734641)
XLA Ops:
  0.6 1.6 %ask.1 = (s32[64,128]{1,0:T(8,128)}, s32[2,8]{1,0:T(2,128)}) custom-call(s32[512]{0:T(512)} %span_row.1, s32[1,8]{1,0:T(1,128)} %span_lists.3), custom_call_target="tpu_custom_call" | custom-call | tf_op jit(solution)/shard_map/ask/pallas_call | solution.py:391
  2.3 20.3 %all_to_all.25 = s32[64,1,128]{2,1,0:T(1,128)S(1)} all-to-all(s32[64,1,128]{2,1,0:T(1,128)} %bitcast.32), channel_id=1, replica_groups=mesh['store'=16,'req'=4,'tp'=2] {'store','req'}, dimensions={0} | all-to-all | bytes 65536 | tf_op jit(solution)/shard_map/all_to_all | solution.py:401
  22.6 0.7 level.1
  23.9 26.2 %conditional.1 = (bf16[64,2,2,16,512]{4,3,2,1,0:T(8,128)(2,1)}) conditional(s32[]{:T(128)} %bitcast.3, (s32[64,128]{1,0:T(8,128)S(1)}, bf16[128,16,512]{2,1,0:T(8,128)(2,1)}, bf16[128,16,512]{2,1,0:T(8,128)(2,1)}) %tuple.70, (s32[64,128]{1,0:T(8,128)S(1)}, bf16[128,16,512]{2,1,0:T(8,128)(2,1)}, ...), branch_computations={%region_0.0_spmd, %region_1.0_spmd, %region_2.0_spmd, %region_3.0_... | conditional | bytes 33554600 | solution.py:464
  23.9 3.3 %move.22 = (bf16[26,16,512]{2,1,0:T(8,128)(2,1)}, bf16[26,16,512]{2,1,0:T(8,128)(2,1)}) custom-call(s32[64,128]{1,0:T(8,128)S(1)} %get-tuple-element.98.plans.plan, bf16[128,16,512]{2,1,0:T(8,128)(2,1)} %get-tuple-element.101.table.keys), custom_call_target="tpu_custom_call" | custom-call | tf_op jit(solution)/shard_map/cond/branch_2_fun/move/pallas_call | solution.py:425
  27.2 0.4 collective-permute-start.8
  27.6 2.4 %collective-permute-start.9 = (bf16[26,16,512]{2,1,0:T(8,128)(2,1)}, bf16[26,16,512]{2,1,0:T(8,128)(2,1)S(1)}, u32[]{:S(2)}, u32[]{:S(2)}) collective-permute-start(bf16[26,16,512]{2,1,0:T(8,128)(2,1)} %get-tuple-element.99), channel_id=1, source_target_pairs={{0,6},{2,0},{4,2},{6,4},{1,7},{3,1},{5,3},{7,5},{8,14},{10,8},{12,... | collective-permute-start | bytes 1277960 | tf_op jit(solution)/shard_map/cond/branch_2_fun/ppermute | solution.py:427
  29.9 3.1 %move.23 = (bf16[26,16,512]{2,1,0:T(8,128)(2,1)}, bf16[26,16,512]{2,1,0:T(8,128)(2,1)}) custom-call(s32[64,128]{1,0:T(8,128)S(1)} %get-tuple-element.98.plans.plan, bf16[128,16,512]{2,1,0:T(8,128)(2,1)} %get-tuple-element.102.table.values), custom_call_target="tpu_custom_call" | custom-call | tf_op jit(solution)/shard_map/cond/branch_2_fun/move/pallas_call | solution.py:425
  33.1 0.1 collective-permute-start.10
  33.2 2.7 %collective-permute-start.11 = (bf16[26,16,512]{2,1,0:T(8,128)(2,1)}, bf16[26,16,512]{2,1,0:T(8,128)(2,1)S(1)}, u32[]{:S(2)}, u32[]{:S(2)}) collective-permute-start(bf16[26,16,512]{2,1,0:T(8,128)(2,1)} %get-tuple-element.100), channel_id=1, source_target_pairs={{0,6},{2,0},{4,2},{6,4},{1,7},{3,1},{5,3},{7,5},{8,14},{10,8},{12,... | collective-permute-start | bytes 1277960 | tf_op jit(solution)/shard_map/cond/branch_2_fun/ppermute | solution.py:427
  35.8 4.8 %own.11 = bf16[64,2,2,16,512]{4,3,2,1,0:T(8,128)(2,1)} custom-call(s32[64,128]{1,0:T(8,128)S(1)} %get-tuple-element.98.plans.plan, bf16[128,16,512]{2,1,0:T(8,128)(2,1)S(1)} %copy-done.11, bf16[128,16,512]{2,1,0:T(8,128)(2,1)} %get-tuple-element.102.table.values), custom_call_target="tpu_custom_call" | custom-call | tf_op jit(solution)/shard_map/cond/branch_2_fun/own/pallas_call | solution.py:431
  40.7 6.3 %collective-permute-done.10.below_v = bf16[26,16,512]{2,1,0:T(8,128)(2,1)S(1)} collective-permute-done((bf16[26,16,512]{2,1,0:T(8,128)(2,1)}, bf16[26,16,512]{2,1,0:T(8,128)(2,1)S(1)}, u32[]{:S(2)}, u32[]{:S(2)}) %collective-permute-start.10) | collective-permute-done | bytes 426016 | tf_op jit(solution)/shard_map/cond/branch_2_fun/ppermute | solution.py:426
  47.0 2.8 %patch.11 = bf16[64,2,2,16,512]{4,3,2,1,0:T(8,128)(2,1)} custom-call(s32[64,128]{1,0:T(8,128)S(1)} %get-tuple-element.98.plans.plan, bf16[26,16,512]{2,1,0:T(8,128)(2,1)S(1)} %collective-permute-done.8.below_k, bf16[26,16,512]{2,1,0:T(8,128)(2,1)S(1)} %collective-permute-done.9.above_k, ...), custom_call_target="tpu_custom_call", output_to_operand_aliasing={{}: (5, {})} | custom-call | tf_op jit(solution)/shard_map/cond/branch_2_fun/patch/pallas_call | solution.py:445
  50.1 0.0 copy-start.17
  50.1 0.0 copy-start.18
  50.2 6.6 %all-to-all-start.1 = ((bf16[64,2,2,16,512]{4,3,2,1,0:T(8,128)(2,1)}), bf16[64,2,2,16,512]{4,3,2,1,0:T(8,128)(2,1)}, u32[]{:S(2)}, u32[]{:S(2)}) async-start(bf16[64,2,2,16,512]{4,3,2,1,0:T(8,128)(2,1)} %get-tuple-element.204), calls=%async_computation.1 | async-start | bytes 8388608 | tf_op jit(solution)/shard_map/all_to_all | solution.py:471
  56.8 0.0 copy-start.5
  56.8 0.0 copy-start.6
  56.8 0.0 copy-start.7
  56.8 0.0 copy-start.8
  56.8 0.5 broadcast.4
  57.4 0.7 convert_bitcast_fusion
  58.0 0.1 reshape_squeeze.3.places_row
  58.1 0.1 copy.27.places_col
  58.2 0.3 fusion
  58.5 0.1 pad_maximum_fusion
  58.7 0.5 fresh.1
  59.2 45.4 %all-to-all-done.1 = bf16[64,2,2,16,512]{4,3,2,1,0:T(8,128)(2,1)} async-done(((bf16[64,2,2,16,512]{4,3,2,1,0:T(8,128)(2,1)}), bf16[64,2,2,16,512]{4,3,2,1,0:T(8,128)(2,1)}, u32[]{:S(2)}, u32[]{:S(2)}) %all-to-all-start.1) | async-done | bytes 4194336 | tf_op jit(solution)/shard_map/all_to_all | solution.py:471
  104.6 4.9 %drift.1 = f32[128,128]{1,0:T(8,128)} custom-call(s32[2,8]{1,0:T(2,128)S(1)} %copy-done.4, s32[1,8]{1,0:T(1,128)S(1)} %copy-done.3, s32[128,1]{1,0:T(8,128)S(1)} %copy.27.places_col, bf16[128,512]{1,0:T(8,128)(2,1)S(1)} %bitcast.19, bf16[128,512]{1,0:T(8,128)(2,1)S(1)} %bitcast.21, bf16[16,4,2,2,16,512]{5,4,3,2,1,0:T(8,128)(2,1)} %bitcast.9.got), custom_call_target="tpu_custom_call" | custom-call | flops 67108864 | bytes 4194304 | tf_op jit(solution)/shard_map/drift/pallas_call | solution.py:501
  109.5 11.2 %all-to-all-start.2 = ((f32[128,1,128]{2,1,0:T(1,128)}), f32[128,1,128]{2,1,0:T(1,128)S(1)}, u32[]{:S(2)}, u32[]{:S(2)}) async-start(f32[128,1,128]{2,1,0:T(1,128)} %bitcast.12), calls=%async_computation.2 | async-start | bytes 131072 | tf_op jit(solution)/shard_map/all_to_all | solution.py:517
  120.7 11.9 %attend.1 = bf16[128,4096]{1,0:T(8,128)(2,1)} custom-call(s32[2,8]{1,0:T(2,128)S(1)} %copy-done.4, s32[8,16]{1,0:T(8,128)S(1)} %reshape_squeeze.3.places_row, s32[128,1]{1,0:T(8,128)S(1)} %copy.27.places_col, bf16[32,128,128]{2,1,0:T(8,128)(2,1)S(1)} %get-tuple-element.195.q, bf16[4,128,256]{2,1,0:T(8,128)(2,1)S(1)} %get-tuple-element.196.new_pair, ...), custom_call_target="tpu_custom_call" | custom-call | flops 4294967296 | bytes 6291456 | tf_op jit(solution)/shard_map/attend/pallas_call | solution.py:519
  132.6 0.7 reduce_sum.9
  (22 shorter events, 0.1 us)
Async XLA Ops:
  23.9 11.9 %copy-start.11 = (bf16[128,16,512]{2,1,0:T(8,128)(2,1)S(1)}, bf16[128,16,512]{2,1,0:T(8,128)(2,1)}, u32[]{:S(2)}) copy-start(bf16[128,16,512]{2,1,0:T(8,128)(2,1)} %get-tuple-element.101.table.keys) | copy-start | bytes 6291460 | tf_op jit(solution)/shard_map/cond
  27.2 13.5 %collective-permute-start.8 = (bf16[26,16,512]{2,1,0:T(8,128)(2,1)}, bf16[26,16,512]{2,1,0:T(8,128)(2,1)S(1)}, u32[]{:S(2)}, u32[]{:S(2)}) collective-permute-start(bf16[26,16,512]{2,1,0:T(8,128)(2,1)} %get-tuple-element.93), channel_id=1, source_target_pairs={{0,2},{2,4},{4,6},{6,0},{1,3},{3,5},{5,7},{7,1},{8,10},{10,12},{12... | collective-permute-start | bytes 1277960 | tf_op jit(solution)/shard_map/cond/branch_2_fun/ppermute | solution.py:426
  27.6 13.2 %collective-permute-start.9 = (bf16[26,16,512]{2,1,0:T(8,128)(2,1)}, bf16[26,16,512]{2,1,0:T(8,128)(2,1)S(1)}, u32[]{:S(2)}, u32[]{:S(2)}) collective-permute-start(bf16[26,16,512]{2,1,0:T(8,128)(2,1)} %get-tuple-element.99), channel_id=1, source_target_pairs={{0,6},{2,0},{4,2},{6,4},{1,7},{3,1},{5,3},{7,5},{8,14},{10,8},{12,... | collective-permute-start | bytes 1277960 | tf_op jit(solution)/shard_map/cond/branch_2_fun/ppermute | solution.py:427
  33.1 13.9 %collective-permute-start.10 = (bf16[26,16,512]{2,1,0:T(8,128)(2,1)}, bf16[26,16,512]{2,1,0:T(8,128)(2,1)S(1)}, u32[]{:S(2)}, u32[]{:S(2)}) collective-permute-start(bf16[26,16,512]{2,1,0:T(8,128)(2,1)} %get-tuple-element.97), channel_id=1, source_target_pairs={{0,2},{2,4},{4,6},{6,0},{1,3},{3,5},{5,7},{7,1},{8,10},{10,12},{12... | collective-permute-start | bytes 1277960 | tf_op jit(solution)/shard_map/cond/branch_2_fun/ppermute | solution.py:426
  33.2 13.8 %collective-permute-start.11 = (bf16[26,16,512]{2,1,0:T(8,128)(2,1)}, bf16[26,16,512]{2,1,0:T(8,128)(2,1)S(1)}, u32[]{:S(2)}, u32[]{:S(2)}) collective-permute-start(bf16[26,16,512]{2,1,0:T(8,128)(2,1)} %get-tuple-element.100), channel_id=1, source_target_pairs={{0,6},{2,0},{4,2},{6,4},{1,7},{3,1},{5,3},{7,5},{8,14},{10,8},{12,... | collective-permute-start | bytes 1277960 | tf_op jit(solution)/shard_map/cond/branch_2_fun/ppermute | solution.py:427
  50.1 7.3 %copy-start.17 = (s32[1,128]{1,0:T(1,128)S(1)}, s32[1,128]{1,0:T(1,128)}, u32[]{:S(2)}) copy-start(s32[1,128]{1,0:T(1,128)} %param.26) | copy-start | bytes 1540
  50.1 8.1 %copy-start.18 = (f32[64]{0:T(128)S(1)}, f32[64]{0:T(128)}, u32[]{:S(2)}) copy-start(f32[64]{0:T(128)} %constant.18.clone) | copy-start | bytes 772
  50.1 8.5 %copy-start = (bf16[1,128,4096]{2,1,0:T(8,128)(2,1)S(1)}, bf16[1,128,4096]{2,1,0:T(8,128)(2,1)}, u32[]{:S(2)}) copy-start(bf16[1,128,4096]{2,1,0:T(8,128)(2,1)} %param.27) | copy-start | bytes 3145732
  50.1 8.5 %copy-start.1 = (bf16[1,128,512]{2,1,0:T(8,128)(2,1)S(1)}, bf16[1,128,512]{2,1,0:T(8,128)(2,1)}, u32[]{:S(2)}) copy-start(bf16[1,128,512]{2,1,0:T(8,128)(2,1)} %param.28) | copy-start | bytes 393220
  50.1 8.5 %copy-start.2 = (bf16[1,128,512]{2,1,0:T(8,128)(2,1)S(1)}, bf16[1,128,512]{2,1,0:T(8,128)(2,1)}, u32[]{:S(2)}) copy-start(bf16[1,128,512]{2,1,0:T(8,128)(2,1)} %param.29) | copy-start | bytes 393220
  50.2 54.5 %copy-start.3 = (s32[1,8]{1,0:T(1,128)S(1)}, s32[1,8]{1,0:T(1,128)}, u32[]{:S(2)}) copy-start(s32[1,8]{1,0:T(1,128)} %span_lists.3) | copy-start | bytes 100
  50.2 54.5 %copy-start.4 = (s32[2,8]{1,0:T(2,128)S(1)}, s32[2,8]{1,0:T(2,128)}, u32[]{:S(2)}) copy-start(s32[2,8]{1,0:T(2,128)} %get-tuple-element.190.place) | copy-start | bytes 196
  50.2 54.4 %all-to-all-start.1 = ((bf16[64,2,2,16,512]{4,3,2,1,0:T(8,128)(2,1)}), bf16[64,2,2,16,512]{4,3,2,1,0:T(8,128)(2,1)}, u32[]{:S(2)}, u32[]{:S(2)}) async-start(bf16[64,2,2,16,512]{4,3,2,1,0:T(8,128)(2,1)} %get-tuple-element.204), calls=%async_computation.1 | async-start | bytes 8388608 | tf_op jit(solution)/shard_map/all_to_all | solution.py:471
  56.8 63.9 %copy-start.5 = (f32[256,128]{1,0:T(8,128)S(1)}, f32[256,128]{1,0:T(8,128)}, u32[]{:S(2)}) copy-start(f32[256,128]{1,0:T(8,128)} %constant.21.clone.cos_token) | copy-start | bytes 393220
  56.8 63.9 %copy-start.6 = (f32[256,128]{1,0:T(8,128)S(1)}, f32[256,128]{1,0:T(8,128)}, u32[]{:S(2)}) copy-start(f32[256,128]{1,0:T(8,128)} %constant.22.clone.sin_token) | copy-start | bytes 393220
  56.8 63.9 %copy-start.7 = (f32[8,128]{1,0:T(8,128)S(1)}, f32[8,128]{1,0:T(8,128)}, u32[]{:S(2)}) copy-start(f32[8,128]{1,0:T(8,128)} %constant.19.clone.cos_span) | copy-start | bytes 12292
  56.8 63.9 %copy-start.8 = (f32[8,128]{1,0:T(8,128)S(1)}, f32[8,128]{1,0:T(8,128)}, u32[]{:S(2)}) copy-start(f32[8,128]{1,0:T(8,128)} %constant.20.clone.sin_span) | copy-start | bytes 12292
  109.5 23.1 %all-to-all-start.2 = ((f32[128,1,128]{2,1,0:T(1,128)}), f32[128,1,128]{2,1,0:T(1,128)S(1)}, u32[]{:S(2)}, u32[]{:S(2)}) async-start(f32[128,1,128]{2,1,0:T(1,128)} %bitcast.12), calls=%async_computation.2 | async-start | bytes 131072 | tf_op jit(solution)/shard_map/all_to_all | solution.py:517

commit v8 on v7

--- a/solution.py
+++ b/solution.py
@@ -18,7 +18,7 @@
 KVH = 8
 BLOCKS = 4
 SLOTS = CPR // BLOCKS
-SIZES = (22, 24, 26, 28, 30, 33, 36, 40)
+SIZES = (22, 23, 24, 25, 26, 27, 28, 30, 33, 38)
 KEPT, UP, DOWN, FROM_BELOW, FROM_ABOVE, LOADS = 0, 4, 8, 12, 13, 16
 LANES = 128
 SCALE_LOG2E = float(HD ** -0.5 * np.log2(np.e))

time: 134 us -> 134 us (level)
    all_to_all x1, waiting for transfers between devices: 45.4 us -> 47.5 us  [local(): lax.all_to_all(send, ('store', 'req'), split_axis=0, concat_axis=0, tiled...]
    ppermute x2, waiting for transfers between devices: 6.3 us -> 4.37 us  [gather(): came.append(lax.ppermute(ups, 'req', climb))]
where the time goes in v8:
time: 134 us; the launch traced here: 133 us
  waiting for transfers between devices  51.8 us (39%)
  Pallas kernels  33.8 us (25%)
  starting transfers between devices  23 us (17%)
  blocking collectives  20.3 us (15%)
  other arithmetic  1.73 us (1%)
  between operations  1.52 us (1%)
    all_to_all x1, waiting for transfers between devices, local(): lax.all_to_all(send, ('store', 'req'), split_axis=0, concat_axis=0, tiled...  47.5 us
    all_to_all x1, blocking collectives, local(): lax.all_to_all(plan, ('store', 'req'), split_axis=0, concat_axis=0, tiled...  20.3 us
    pallas_call x1, Pallas kernels, local(): pl.pallas_call(functools.partial(attend_kernel, heads_kv, group), out_sha...  11.9 us
    all_to_all x1, starting transfers between devices, local(): lax.all_to_all(part, ('store', 'req', 'tp'), split_axis=0, concat_axis=0,...  10.7 us
    all_to_all x1, starting transfers between devices, local(): lax.all_to_all(send, ('store', 'req'), split_axis=0, concat_axis=0, tiled...  6.81 us
    pallas_call x2, Pallas kernels, gather(): ups, downs = move(plans, table)  6.32 us
    ppermute x2, starting transfers between devices, gather(): came.append(lax.ppermute(downs, 'req', sink))  5.05 us
    pallas_call x1, Pallas kernels, local(): pl.pallas_call(functools.partial(drift_kernel, span_row.shape[0]), out_sh...  5 us
  transfers between devices with their start and end apart: 6, of which 2 were waited for; matrix products, arithmetic and copies ran while one was open for 1% of the time, Pallas kernels for 15%

profile of v8, /device:TPU:1, one launch (start us, length us, event | category | flops | bytes accessed | tf_op | source)
XLA Modules:
  0.0 133.3 jit_solution(13139831924879397343)
XLA Ops:
  0.6 1.6 %ask.1 = (s32[64,128]{1,0:T(8,128)}, s32[2,8]{1,0:T(2,128)}) custom-call(s32[512]{0:T(512)} %span_row.1, s32[1,8]{1,0:T(1,128)} %span_lists.3), custom_call_target="tpu_custom_call" | custom-call | tf_op jit(solution)/shard_map/ask/pallas_call | solution.py:391
  2.3 20.3 %all_to_all.25 = s32[64,1,128]{2,1,0:T(1,128)S(1)} all-to-all(s32[64,1,128]{2,1,0:T(1,128)} %bitcast.34), channel_id=1, replica_groups=mesh['store'=16,'req'=4,'tp'=2] {'store','req'}, dimensions={0} | all-to-all | bytes 65536 | tf_op jit(solution)/shard_map/all_to_all | solution.py:401
  22.6 0.7 level.1
  23.9 24.3 %conditional.1 = (bf16[64,2,2,16,512]{4,3,2,1,0:T(8,128)(2,1)}) conditional(s32[]{:T(128)} %bitcast.3, (s32[64,128]{1,0:T(8,128)S(1)}, bf16[128,16,512]{2,1,0:T(8,128)(2,1)}, bf16[128,16,512]{2,1,0:T(8,128)(2,1)}) %tuple.82, (s32[64,128]{1,0:T(8,128)S(1)}, bf16[128,16,512]{2,1,0:T(8,128)(2,1)}, ...), branch_computations={%region_0.0_spmd, %region_1.0_spmd, %region_2.0_spmd, %region_3.0_... | conditional | bytes 33554600 | solution.py:464
  23.9 3.2 %move.22 = (bf16[22,16,512]{2,1,0:T(8,128)(2,1)}, bf16[22,16,512]{2,1,0:T(8,128)(2,1)}) custom-call(s32[64,128]{1,0:T(8,128)S(1)} %get-tuple-element.82.plans.plan, bf16[128,16,512]{2,1,0:T(8,128)(2,1)} %get-tuple-element.89.table.keys), custom_call_target="tpu_custom_call" | custom-call | tf_op jit(solution)/shard_map/cond/branch_0_fun/move/pallas_call | solution.py:425
  27.1 0.4 collective-permute-start
  27.5 2.4 %collective-permute-start.1 = (bf16[22,16,512]{2,1,0:T(8,128)(2,1)}, bf16[22,16,512]{2,1,0:T(8,128)(2,1)S(1)}, u32[]{:S(2)}, u32[]{:S(2)}) collective-permute-start(bf16[22,16,512]{2,1,0:T(8,128)(2,1)} %get-tuple-element.83), channel_id=1, source_target_pairs={{0,6},{2,0},{4,2},{6,4},{1,7},{3,1},{5,3},{7,5},{8,14},{10,8},{12,... | collective-permute-start | bytes 1081352 | tf_op jit(solution)/shard_map/cond/branch_0_fun/ppermute | solution.py:427
  29.9 3.1 %move.23 = (bf16[22,16,512]{2,1,0:T(8,128)(2,1)}, bf16[22,16,512]{2,1,0:T(8,128)(2,1)}) custom-call(s32[64,128]{1,0:T(8,128)S(1)} %get-tuple-element.82.plans.plan, bf16[128,16,512]{2,1,0:T(8,128)(2,1)} %get-tuple-element.90.table.values), custom_call_target="tpu_custom_call" | custom-call | tf_op jit(solution)/shard_map/cond/branch_0_fun/move/pallas_call | solution.py:425
  33.0 0.1 collective-permute-start.2
  33.1 2.7 %collective-permute-start.3 = (bf16[22,16,512]{2,1,0:T(8,128)(2,1)}, bf16[22,16,512]{2,1,0:T(8,128)(2,1)S(1)}, u32[]{:S(2)}, u32[]{:S(2)}) collective-permute-start(bf16[22,16,512]{2,1,0:T(8,128)(2,1)} %get-tuple-element.88), channel_id=1, source_target_pairs={{0,6},{2,0},{4,2},{6,4},{1,7},{3,1},{5,3},{7,5},{8,14},{10,8},{12,... | collective-permute-start | bytes 1081352 | tf_op jit(solution)/shard_map/cond/branch_0_fun/ppermute | solution.py:427
  35.7 4.8 %own.11 = bf16[64,2,2,16,512]{4,3,2,1,0:T(8,128)(2,1)} custom-call(s32[64,128]{1,0:T(8,128)S(1)} %get-tuple-element.82.plans.plan, bf16[128,16,512]{2,1,0:T(8,128)(2,1)S(1)} %copy-done.9, bf16[128,16,512]{2,1,0:T(8,128)(2,1)} %get-tuple-element.90.table.values), custom_call_target="tpu_custom_call" | custom-call | tf_op jit(solution)/shard_map/cond/branch_0_fun/own/pallas_call | solution.py:431
  40.6 4.4 %collective-permute-done.2.below_v = bf16[22,16,512]{2,1,0:T(8,128)(2,1)S(1)} collective-permute-done((bf16[22,16,512]{2,1,0:T(8,128)(2,1)}, bf16[22,16,512]{2,1,0:T(8,128)(2,1)S(1)}, u32[]{:S(2)}, u32[]{:S(2)}) %collective-permute-start.2) | collective-permute-done | bytes 360480 | tf_op jit(solution)/shard_map/cond/branch_0_fun/ppermute | solution.py:426
  45.0 2.9 %patch.11 = bf16[64,2,2,16,512]{4,3,2,1,0:T(8,128)(2,1)} custom-call(s32[64,128]{1,0:T(8,128)S(1)} %get-tuple-element.82.plans.plan, bf16[22,16,512]{2,1,0:T(8,128)(2,1)S(1)} %collective-permute-done.below_k, bf16[22,16,512]{2,1,0:T(8,128)(2,1)S(1)} %collective-permute-done.1.above_k, ...), custom_call_target="tpu_custom_call", output_to_operand_aliasing={{}: (5, {})} | custom-call | tf_op jit(solution)/shard_map/cond/branch_0_fun/patch/pallas_call | solution.py:445
  48.2 0.0 copy-start.19
  48.2 0.0 copy-start.20
  48.3 6.8 %all-to-all-start.1 = ((bf16[64,2,2,16,512]{4,3,2,1,0:T(8,128)(2,1)}), bf16[64,2,2,16,512]{4,3,2,1,0:T(8,128)(2,1)}, u32[]{:S(2)}, u32[]{:S(2)}) async-start(bf16[64,2,2,16,512]{4,3,2,1,0:T(8,128)(2,1)} %get-tuple-element.244), calls=%async_computation.1 | async-start | bytes 8388608 | tf_op jit(solution)/shard_map/all_to_all | solution.py:471
  55.1 0.0 copy-start.5
  55.1 0.0 copy-start.6
  55.1 0.0 copy-start.7
  55.1 0.0 copy-start.8
  55.1 0.5 broadcast.4
  55.6 0.7 convert_bitcast_fusion
  56.3 0.1 reshape_squeeze.3.places_row
  56.4 0.1 copy.29.places_col
  56.5 0.3 fusion
  56.8 0.1 pad_maximum_fusion
  57.0 0.5 fresh.1
  57.5 47.5 %all-to-all-done.1 = bf16[64,2,2,16,512]{4,3,2,1,0:T(8,128)(2,1)} async-done(((bf16[64,2,2,16,512]{4,3,2,1,0:T(8,128)(2,1)}), bf16[64,2,2,16,512]{4,3,2,1,0:T(8,128)(2,1)}, u32[]{:S(2)}, u32[]{:S(2)}) %all-to-all-start.1) | async-done | bytes 4194336 | tf_op jit(solution)/shard_map/all_to_all | solution.py:471
  105.0 5.0 %drift.1 = f32[128,128]{1,0:T(8,128)} custom-call(s32[2,8]{1,0:T(2,128)S(1)} %copy-done.4, s32[1,8]{1,0:T(1,128)S(1)} %copy-done.3, s32[128,1]{1,0:T(8,128)S(1)} %copy.29.places_col, bf16[128,512]{1,0:T(8,128)(2,1)S(1)} %bitcast.19, bf16[128,512]{1,0:T(8,128)(2,1)S(1)} %bitcast.21, bf16[16,4,2,2,16,512]{5,4,3,2,1,0:T(8,128)(2,1)} %bitcast.9.got), custom_call_target="tpu_custom_call" | custom-call | flops 67108864 | bytes 4194304 | tf_op jit(solution)/shard_map/drift/pallas_call | solution.py:501
  110.0 10.7 %all-to-all-start.2 = ((f32[128,1,128]{2,1,0:T(1,128)}), f32[128,1,128]{2,1,0:T(1,128)S(1)}, u32[]{:S(2)}, u32[]{:S(2)}) async-start(f32[128,1,128]{2,1,0:T(1,128)} %bitcast.12), calls=%async_computation.2 | async-start | bytes 131072 | tf_op jit(solution)/shard_map/all_to_all | solution.py:517
  120.7 11.9 %attend.1 = bf16[128,4096]{1,0:T(8,128)(2,1)} custom-call(s32[2,8]{1,0:T(2,128)S(1)} %copy-done.4, s32[8,16]{1,0:T(8,128)S(1)} %reshape_squeeze.3.places_row, s32[128,1]{1,0:T(8,128)S(1)} %copy.29.places_col, bf16[32,128,128]{2,1,0:T(8,128)(2,1)S(1)} %get-tuple-element.235.q, bf16[4,128,256]{2,1,0:T(8,128)(2,1)S(1)} %get-tuple-element.236.new_pair, ...), custom_call_target="tpu_custom_call" | custom-call | flops 4294967296 | bytes 6291456 | tf_op jit(solution)/shard_map/attend/pallas_call | solution.py:519
  132.6 0.7 reduce_sum.9
  (22 shorter events, 0.1 us)
Async XLA Ops:
  23.9 11.8 %copy-start.9 = (bf16[128,16,512]{2,1,0:T(8,128)(2,1)S(1)}, bf16[128,16,512]{2,1,0:T(8,128)(2,1)}, u32[]{:S(2)}) copy-start(bf16[128,16,512]{2,1,0:T(8,128)(2,1)} %get-tuple-element.89.table.keys) | copy-start | bytes 6291460 | tf_op jit(solution)/shard_map/cond
  27.1 13.4 %collective-permute-start = (bf16[22,16,512]{2,1,0:T(8,128)(2,1)}, bf16[22,16,512]{2,1,0:T(8,128)(2,1)S(1)}, u32[]{:S(2)}, u32[]{:S(2)}) collective-permute-start(bf16[22,16,512]{2,1,0:T(8,128)(2,1)} %get-tuple-element.73), channel_id=1, source_target_pairs={{0,2},{2,4},{4,6},{6,0},{1,3},{3,5},{5,7},{7,1},{8,10},{10,12},{12... | collective-permute-start | bytes 1081352 | tf_op jit(solution)/shard_map/cond/branch_0_fun/ppermute | solution.py:426
  27.5 13.1 %collective-permute-start.1 = (bf16[22,16,512]{2,1,0:T(8,128)(2,1)}, bf16[22,16,512]{2,1,0:T(8,128)(2,1)S(1)}, u32[]{:S(2)}, u32[]{:S(2)}) collective-permute-start(bf16[22,16,512]{2,1,0:T(8,128)(2,1)} %get-tuple-element.83), channel_id=1, source_target_pairs={{0,6},{2,0},{4,2},{6,4},{1,7},{3,1},{5,3},{7,5},{8,14},{10,8},{12,... | collective-permute-start | bytes 1081352 | tf_op jit(solution)/shard_map/cond/branch_0_fun/ppermute | solution.py:427
  33.0 12.0 %collective-permute-start.2 = (bf16[22,16,512]{2,1,0:T(8,128)(2,1)}, bf16[22,16,512]{2,1,0:T(8,128)(2,1)S(1)}, u32[]{:S(2)}, u32[]{:S(2)}) collective-permute-start(bf16[22,16,512]{2,1,0:T(8,128)(2,1)} %get-tuple-element.81), channel_id=1, source_target_pairs={{0,2},{2,4},{4,6},{6,0},{1,3},{3,5},{5,7},{7,1},{8,10},{10,12},{12... | collective-permute-start | bytes 1081352 | tf_op jit(solution)/shard_map/cond/branch_0_fun/ppermute | solution.py:426
  33.1 11.9 %collective-permute-start.3 = (bf16[22,16,512]{2,1,0:T(8,128)(2,1)}, bf16[22,16,512]{2,1,0:T(8,128)(2,1)S(1)}, u32[]{:S(2)}, u32[]{:S(2)}) collective-permute-start(bf16[22,16,512]{2,1,0:T(8,128)(2,1)} %get-tuple-element.88), channel_id=1, source_target_pairs={{0,6},{2,0},{4,2},{6,4},{1,7},{3,1},{5,3},{7,5},{8,14},{10,8},{12,... | collective-permute-start | bytes 1081352 | tf_op jit(solution)/shard_map/cond/branch_0_fun/ppermute | solution.py:427
  48.2 7.5 %copy-start.19 = (s32[1,128]{1,0:T(1,128)S(1)}, s32[1,128]{1,0:T(1,128)}, u32[]{:S(2)}) copy-start(s32[1,128]{1,0:T(1,128)} %param.28) | copy-start | bytes 1540
  48.2 8.3 %copy-start.20 = (f32[64]{0:T(128)S(1)}, f32[64]{0:T(128)}, u32[]{:S(2)}) copy-start(f32[64]{0:T(128)} %constant.18.clone) | copy-start | bytes 772
  48.2 8.7 %copy-start = (bf16[1,128,4096]{2,1,0:T(8,128)(2,1)S(1)}, bf16[1,128,4096]{2,1,0:T(8,128)(2,1)}, u32[]{:S(2)}) copy-start(bf16[1,128,4096]{2,1,0:T(8,128)(2,1)} %param.29) | copy-start | bytes 3145732
  48.2 8.7 %copy-start.1 = (bf16[1,128,512]{2,1,0:T(8,128)(2,1)S(1)}, bf16[1,128,512]{2,1,0:T(8,128)(2,1)}, u32[]{:S(2)}) copy-start(bf16[1,128,512]{2,1,0:T(8,128)(2,1)} %param.30) | copy-start | bytes 393220
  48.2 8.7 %copy-start.2 = (bf16[1,128,512]{2,1,0:T(8,128)(2,1)S(1)}, bf16[1,128,512]{2,1,0:T(8,128)(2,1)}, u32[]{:S(2)}) copy-start(bf16[1,128,512]{2,1,0:T(8,128)(2,1)} %param.31) | copy-start | bytes 393220
  48.2 56.7 %copy-start.3 = (s32[1,8]{1,0:T(1,128)S(1)}, s32[1,8]{1,0:T(1,128)}, u32[]{:S(2)}) copy-start(s32[1,8]{1,0:T(1,128)} %span_lists.3) | copy-start | bytes 100
  48.2 56.7 %copy-start.4 = (s32[2,8]{1,0:T(2,128)S(1)}, s32[2,8]{1,0:T(2,128)}, u32[]{:S(2)}) copy-start(s32[2,8]{1,0:T(2,128)} %get-tuple-element.230.place) | copy-start | bytes 196
  48.3 56.7 %all-to-all-start.1 = ((bf16[64,2,2,16,512]{4,3,2,1,0:T(8,128)(2,1)}), bf16[64,2,2,16,512]{4,3,2,1,0:T(8,128)(2,1)}, u32[]{:S(2)}, u32[]{:S(2)}) async-start(bf16[64,2,2,16,512]{4,3,2,1,0:T(8,128)(2,1)} %get-tuple-element.244), calls=%async_computation.1 | async-start | bytes 8388608 | tf_op jit(solution)/shard_map/all_to_all | solution.py:471
  55.1 65.6 %copy-start.5 = (f32[256,128]{1,0:T(8,128)S(1)}, f32[256,128]{1,0:T(8,128)}, u32[]{:S(2)}) copy-start(f32[256,128]{1,0:T(8,128)} %constant.21.clone.cos_token) | copy-start | bytes 393220
  55.1 65.6 %copy-start.6 = (f32[256,128]{1,0:T(8,128)S(1)}, f32[256,128]{1,0:T(8,128)}, u32[]{:S(2)}) copy-start(f32[256,128]{1,0:T(8,128)} %constant.22.clone.sin_token) | copy-start | bytes 393220
  55.1 65.6 %copy-start.7 = (f32[8,128]{1,0:T(8,128)S(1)}, f32[8,128]{1,0:T(8,128)}, u32[]{:S(2)}) copy-start(f32[8,128]{1,0:T(8,128)} %constant.19.clone.cos_span) | copy-start | bytes 12292
  55.1 65.6 %copy-start.8 = (f32[8,128]{1,0:T(8,128)S(1)}, f32[8,128]{1,0:T(8,128)}, u32[]{:S(2)}) copy-start(f32[8,128]{1,0:T(8,128)} %constant.20.clone.sin_span) | copy-start | bytes 12292
  110.0 22.7 %all-to-all-start.2 = ((f32[128,1,128]{2,1,0:T(1,128)}), f32[128,1,128]{2,1,0:T(1,128)S(1)}, u32[]{:S(2)}, u32[]{:S(2)}) async-start(f32[128,1,128]{2,1,0:T(1,128)} %bitcast.12), calls=%async_computation.2 | async-start | bytes 131072 | tf_op jit(solution)/shard_map/all_to_all | solution.py:517
